TPU v7x, 256 devices: a whole 4x4x8 slice. The times are simulated.
256 devices in a mesh: row: 16 (over y, x), col: 16 (over z, core).
Axes of the slice: x: 4, y: 4, z: 8, core: 2. Of those that a mesh axis runs over, the one named last changes fastest.
Arguments:
- matrix: float32 [16384, 4, 4096], P('row', None, 'col'), may hold values from -28 to 28
Outputs:
- coefficients: float32 [512, 4, 4096], P(None, None, 'col')
- remainder: float32 [16384, 4, 4096], P('row', None, 'col')
All inputs are finite; a program needn't handle non-finite values.
Results may differ from a plain program's by a relative error of at most 0.0003.
Values sent between devices are 32-bit elements; how exact they have to be, the bound alone decides.
No kernel may reach another device: no remote copies, remote signals or barrier semaphores. Data moves between devices by JAX's collectives and lax.ppermute only.
A program may use at most 64 MiB of HBM per device.

v0:
```python
import jax
import jax.numpy as jnp
from jax import lax
from jax.experimental import pallas as pl
from jax.experimental.pallas import tpu as pltpu
from jax.sharding import PartitionSpec as P

BLOCK = 256
TILE = 128
NB = 4
STRIP = 4
FULL = NB * TILE
PEERS = 16
DEPTH = 8
PIECE = 128
HALF = ((0, 0), (1, 0), (1, 1), (2, 0), (2, 1)), ((2, 2), (3, 0), (3, 1), (3, 2), (3, 3))
HALF_ROWS = len(HALF[0]) * TILE

highest = lax.Precision.HIGHEST
by_rows = ((0,), (0,))
plain = ((1,), (0,))
by_cols = ((1,), (1,))


def mm(a, b, dims):
    return lax.dot_general(a, b, (dims, ((), ())), precision=highest, preferred_element_type=jnp.float32)

def invert_factor(s):
    n = TILE
    rows = lax.broadcasted_iota(jnp.int32, (n, n), 0)
    cols = lax.broadcasted_iota(jnp.int32, (n, n), 1)
    t = jnp.where(rows == cols, 1.0, 0.0).astype(jnp.float32)
    s_done, t_done = [], []
    for k in range(0, n, STRIP):
        top = (k // 8) * 8
        off = k - top
        height = n - top
        sub = lax.broadcasted_iota(jnp.int32, (height, n), 0)
        col = [jnp.broadcast_to(s[:, k + m : k + m + 1], (height, n)) for m in range(STRIP)]
        pivot = [[jnp.broadcast_to(col[j][off + i : off + i + 1, :], (8, n)) for j in range(STRIP)] for i in range(STRIP)]
        srow = [jnp.broadcast_to(s[off + m : off + m + 1, :], (8, n)) for m in range(STRIP)]
        trow = [jnp.broadcast_to(t[off + m : off + m + 1, :], (8, n)) for m in range(STRIP)]
        inv = []
        for m in range(STRIP):
            inv.append(1.0 / pivot[m][m])
            for i in range(m + 1, STRIP):
                low = pivot[i][m] * inv[m]
                for j in range(m + 1, STRIP):
                    if j <= i:
                        pivot[i][j] = pivot[i][j] - low * pivot[j][m]
                srow[i] = srow[i] - low * srow[m]
                trow[i] = trow[i] - low * trow[m]
        def tall(x):
            return jnp.concatenate([x] * (height // 8), axis=0) if height > 8 else x
        factor = []
        for m in range(STRIP):
            f = col[m]
            for j in range(m):
                f = f - factor[j] * tall(pivot[m][j])
            f = f * tall(inv[m])
            factor.append(f)
        for m in range(STRIP):
            f = jnp.where(sub > off + m, factor[m], 0.0)
            s = s - f * tall(srow[m])
            t = t - f * tall(trow[m])
        if off + STRIP == 8:
            s_done.append(s[:8])
            t_done.append(t[:8])
            if height > 8:
                s, t = s[8:], t[8:]
    s = jnp.concatenate(s_done, axis=0)
    t = jnp.concatenate(t_done, axis=0)
    diag = jnp.sum(jnp.where(rows == cols, s, 0.0), axis=1, keepdims=True)
    return t * lax.rsqrt(diag)


def split(x):
    high = x.astype(jnp.bfloat16)
    return high, (x - high.astype(jnp.float32)).astype(jnp.bfloat16)


def one_pass(a, b, dims):
    return lax.dot_general(a, b, (dims, ((), ())), preferred_element_type=jnp.float32)


def three_pass(a, b, dims):
    return one_pass(a[0], b[0], dims) + (one_pass(a[0], b[1], dims) + one_pass(a[1], b[0], dims))


def gram_kernel(place, own_ref, other_ref, high_ref, low_ref, gram_ref):
    first = place[1] == 0
    own, other = own_ref[...], other_ref[...]
    panel = jnp.concatenate([jnp.where(first, own, other), jnp.where(first, other, own)], axis=1)
    parts = split(panel)
    high_ref[...], low_ref[...] = parts
    gram = three_pass(parts, parts, by_rows)
    for t in range(len(HALF[0])):
        (i, j), (p, q) = HALF[0][t], HALF[1][t]
        here = gram[i * TILE : (i + 1) * TILE, j * TILE : (j + 1) * TILE]
        there = gram[p * TILE : (p + 1) * TILE, q * TILE : (q + 1) * TILE]
        gram_ref[t * TILE : (t + 1) * TILE, :] = jnp.where(first, here, there)


def product_kernel(place, high_ref, low_ref, a0_ref, a1_ref, acc_ref):
    @pl.when(pl.program_id(0) == 0)
    def _():
        acc_ref[...] = jnp.zeros_like(acc_ref)

    panel = high_ref[...], low_ref[...]
    for l in range(a0_ref.shape[0]):
        a = split(jnp.concatenate([a0_ref[l], a1_ref[l]], axis=0))
        acc_ref[:, l * BLOCK : (l + 1) * BLOCK] += three_pass(panel, a, by_rows)


def factor_kernel(place, own_ref, other_ref, m_ref, s_ref, t_ref):
    first = place[1] == 0
    s_ref[...] = jnp.zeros_like(s_ref)
    t_ref[...] = jnp.zeros_like(t_ref)
    for t in range(len(HALF[0])):
        own, other = own_ref[t * TILE : (t + 1) * TILE, :], other_ref[t * TILE : (t + 1) * TILE, :]
        for (i, j), block in zip((HALF[0][t], HALF[1][t]), (jnp.where(first, own, other), jnp.where(first, other, own))):
            s_ref[j, i * TILE : (i + 1) * TILE, :] = block

    @pl.loop(0, NB)
    def _(j):
        d = pl.multiple_of(j * TILE, TILE)
        mj = invert_factor(s_ref[j, pl.ds(d, TILE), :])
        mrow = mm(mj, t_ref[j], plain)
        lanes = lax.broadcasted_iota(jnp.int32, (TILE, FULL), 1)
        mrow = jnp.where(lanes // TILE == j, jnp.concatenate([mj] * NB, axis=1), mrow)
        m_ref[pl.ds(d, TILE), :] = mrow
        rows = lax.broadcasted_iota(jnp.int32, (FULL, TILE), 0)
        low = jnp.where(rows >= d + TILE, mm(s_ref[j], mj, by_cols), 0.0)
        for i in range(1, NB):

            @pl.when(i > j)
            def _():
                part = low[i * TILE : (i + 1) * TILE]
                s_ref[i] -= mm(low, part, by_cols)
                t_ref[i] -= mm(part, mrow, plain)


def basis_kernel(place, high_ref, low_ref, m_ref, qh_ref, ql_ref):
    q = three_pass((high_ref[...], low_ref[...]), split(m_ref[...]), by_cols)
    qh_ref[...], ql_ref[...] = split(q)


def remainder_kernel(place, qh_ref, ql_ref, a_ref, m_ref, w_ref, coeff_ref, out_ref, ch_ref, cl_ref):
    width = a_ref.shape[2]

    @pl.when(pl.program_id(0) == 0)
    def _():
        coeffs = three_pass(split(m_ref[...]), split(w_ref[...]), plain)
        for l in range(coeff_ref.shape[0]):
            coeff_ref[l] = coeffs[:, l * width : (l + 1) * width]
        ch_ref[...], cl_ref[...] = split(coeffs)

    q = qh_ref[...], ql_ref[...]
    for l in range(a_ref.shape[0]):
        window = slice(l * width, (l + 1) * width)
        out_ref[l] = a_ref[l] - three_pass(q, (ch_ref[:, window], cl_ref[:, window]), plain)


def call(kernel, name, mib, grid, ins, outs, out_shape, scratch=()):
    return pl.pallas_call(
        kernel,
        out_shape=out_shape,
        grid_spec=pltpu.PrefetchScalarGridSpec(
            num_scalar_prefetch=1, grid=grid, in_specs=ins, out_specs=outs, scratch_shapes=scratch
        ),
        compiler_params=pltpu.CompilerParams(vmem_limit_bytes=mib << 20),
        name=name,
    )


def whole(*shape):
    return pl.BlockSpec(shape, lambda g, place: (0,) * len(shape))


def f32(*shape):
    return jax.ShapeDtypeStruct(shape, jnp.float32)


def bf16(*shape):
    return jax.ShapeDtypeStruct(shape, jnp.bfloat16)


def shift(x, axis, by):
    return lax.ppermute(x, axis, [(i, (i + by) % PEERS) for i in range(PEERS)])


def exchange(x):
    rows, width = x.shape
    return lax.all_to_all(x.reshape(PEERS, rows // PEERS, width), "row", 0, 0)


def everywhere(shares):
    total = jnp.broadcast_to(jnp.sum(shares, axis=0), shares.shape)
    return lax.all_to_all(total, "row", 0, 0).reshape(shares.shape[0] * shares.shape[1], shares.shape[2])


def swap_cores(x):
    return lax.ppermute(x, "col", [(i, i ^ 1) for i in range(PEERS)])


def share_panel(mine, z):
    own = jnp.where(z == 0, mine[:PIECE], jnp.zeros((PIECE, BLOCK), jnp.float32))
    for k in range(1, DEPTH):
        own = own + lax.ppermute(mine[k * PIECE : (k + 1) * PIECE], "col", [(0, 2 * k), (1, 2 * k + 1)])
    up, down = [own], [own]
    for _ in range(DEPTH // 2 - 1):
        up.append(shift(up[-1], "col", 2))
        down.append(shift(down[-1], "col", -2))
    half = PIECE // 2
    far = [shift(up[-1][:half], "col", 2), shift(down[-1][half:], "col", -2)]
    return jnp.concatenate(down + far + up[:0:-1], axis=0)


def on_device(matrix):
    rows, blocks, width = matrix.shape
    col = lax.axis_index("col")
    z, core, row = col // 2, col % 2, lax.axis_index("row")
    place = jnp.stack([z, core, row]).astype(jnp.int32)

    own = share_panel(matrix[:, 0, :], z)
    other = swap_cores(own)
    high, low, gram = call(
        gram_kernel, "gram", 20, (1,),
        [whole(rows, BLOCK), whole(rows, BLOCK)],
        [whole(rows, FULL), whole(rows, FULL), whole(HALF_ROWS, TILE)],
        [bf16(rows, FULL), bf16(rows, FULL), f32(HALF_ROWS, TILE)],
    )(place, own, other)

    stacked = jnp.transpose(matrix, (1, 0, 2))
    step = 2 * PIECE
    steps = rows // step
    panel_spec = pl.BlockSpec((step, FULL), lambda g, place: (g, 0))
    terms = call(
        product_kernel, "product", 20, (steps,),
        [panel_spec, panel_spec]
        + [
            pl.BlockSpec((blocks, PIECE, width), lambda g, place, e=e: (0, lax.rem(place[0] + 2 * g + e, DEPTH), 0))
            for e in range(2)
        ],
        whole(FULL, blocks * width),
        f32(FULL, blocks * width),
    )(place, high, low, stacked, stacked)

    gram = exchange(gram)
    terms = exchange(terms)
    gram = everywhere(gram)
    sums = everywhere(terms)

    m = call(
        factor_kernel, "factor", 12, (1,),
        [whole(HALF_ROWS, TILE)] * 2,
        whole(FULL, FULL),
        f32(FULL, FULL),
        [pltpu.VMEM((NB, FULL, TILE), jnp.float32), pltpu.VMEM((NB, TILE, FULL), jnp.float32)],
    )(place, gram, swap_cores(gram))

    rolled = pl.BlockSpec((PIECE, FULL), lambda g, place: (g, 0))
    natural = pl.BlockSpec((PIECE, FULL), lambda g, place: (lax.rem(place[0] + g, DEPTH), 0))
    qh, ql = call(
        basis_kernel, "basis", 14, (DEPTH,),
        [rolled, rolled, whole(FULL, FULL)],
        [natural, natural],
        [bf16(rows, FULL), bf16(rows, FULL)],
    )(place, high, low, m)

    a_spec = pl.BlockSpec((blocks, step, width), lambda g, place: (0, g, 0))
    coeffs, rest = call(
        remainder_kernel, "remainder", 22, (steps,),
        [panel_spec, panel_spec, a_spec, whole(FULL, FULL), whole(FULL, blocks * width)],
        [whole(blocks, FULL, width), a_spec],
        [f32(blocks, FULL, width), f32(blocks, rows, width)],
        [pltpu.VMEM((FULL, blocks * width), jnp.bfloat16)] * 2,
    )(place, qh, ql, stacked, m, sums)
    return jnp.transpose(coeffs, (1, 0, 2)), jnp.transpose(rest, (1, 0, 2))


def solution(mesh):
    return jax.shard_map(
        on_device,
        mesh=mesh,
        in_specs=(P("row", None, "col"),),
        out_specs=(P(None, None, "col"), P("row", None, "col")),
        check_vma=False,
    )
```

profile of v0, /device:TPU:1, one launch (start us, length us, event | category | flops | bytes accessed | tf_op | source)
XLA Modules:
  0.0 194.3 jit_solution(12095003740212962825)
XLA Ops:
  0.6 3.0 %copy.16 = f32[1024,4,256]{2,0,1:T(8,128)S(1)} copy(f32[1024,4,256]{2,1,0:T(4,128)} %param.1) | data formatting | bytes 8388608 | tf_op args[0]
  3.6 2.0 %copy-done = f32[1024,4,256]{2,0,1:T(8,128)} copy-done((f32[1024,4,256]{2,0,1:T(8,128)}, f32[1024,4,256]{2,0,1:T(8,128)S(1)}, u32[]{:S(2)}) %copy-start) | copy-done | bytes 4194328
  5.7 4.4 %collective-permute-start = (f32[128,256]{1,0:T(8,128)S(1)}, f32[128,256]{1,0:T(8,128)S(1)}, u32[]{:S(2)}, u32[]{:S(2)}) collective-permute-start(f32[128,256]{1,0:T(8,128)S(1)} %get-tuple-element.22), channel_id=1, source_target_pairs={{0,2},{1,3},{16,18},{17,19},{32,34},{33,35},{48,50},{49,51},{64,66... | collective-permute-start | bytes 393224 | tf_op jit(solution)/shard_map/ppermute | solution.py:209
  10.1 4.6 %collective-permute-start.6 = (f32[128,256]{1,0:T(8,128)S(1)}, f32[128,256]{1,0:T(8,128)S(1)}, u32[]{:S(2)}, u32[]{:S(2)}) collective-permute-start(f32[128,256]{1,0:T(8,128)S(1)} %get-tuple-element.23), channel_id=1, source_target_pairs={{0,14},{1,15},{16,30},{17,31},{32,46},{33,47},{48,62},{49,63},{64,... | collective-permute-start | bytes 393224 | tf_op jit(solution)/shard_map/ppermute | solution.py:209
  14.7 1.3 collective-permute-start.5
  16.0 1.3 collective-permute-start.4
  17.4 1.3 collective-permute-start.3
  18.7 1.3 collective-permute-start.2
  20.0 1.3 collective-permute-start.1
  21.3 1.2 collective-permute-done.4
  22.5 1.1 collective-permute-done.2
  23.6 2.8 %collective-permute-done.1 = f32[128,256]{1,0:T(8,128)S(1)} collective-permute-done((f32[128,256]{1,0:T(8,128)S(1)}, f32[128,256]{1,0:T(8,128)S(1)}, u32[]{:S(2)}, u32[]{:S(2)}) %collective-permute-start.1) | collective-permute-done | bytes 131104 | tf_op jit(solution)/shard_map/ppermute | solution.py:209
  26.4 1.0 constant_dynamic-update-slice_fusion.8
  27.5 2.7 %collective-permute-start.7 = (f32[128,256]{1,0:T(8,128)S(1)}, f32[128,256]{1,0:T(8,128)S(1)}, u32[]{:S(2)}, u32[]{:S(2)}) collective-permute-start(f32[128,256]{1,0:T(8,128)S(1)} %get-tuple-element.19), channel_id=1, source_target_pairs={{0,14},{1,15},{2,0},{3,1},{4,2},{5,3},{6,4},{7,5},{8,6},{9,7},{10,... | collective-permute-start | bytes 393224 | tf_op jit(solution)/shard_map/ppermute | solution.py:189
  30.1 2.4 %collective-permute-done.10 = f32[128,256]{1,0:T(8,128)S(1)} collective-permute-done((f32[128,256]{1,0:T(8,128)S(1)}, f32[128,256]{1,0:T(8,128)S(1)}, u32[]{:S(2)}, u32[]{:S(2)}) %collective-permute-start.10) | collective-permute-done | bytes 131104 | tf_op jit(solution)/shard_map/ppermute | solution.py:189
  33.5 1.7 collective-permute-start.8
  35.2 2.3 %collective-permute-done.11 = f32[128,256]{1,0:T(8,128)S(1)} collective-permute-done((f32[128,256]{1,0:T(8,128)S(1)}, f32[128,256]{1,0:T(8,128)S(1)}, u32[]{:S(2)}, u32[]{:S(2)}) %collective-permute-start.11) | collective-permute-done | bytes 131104 | tf_op jit(solution)/shard_map/ppermute | solution.py:189
  37.5 2.7 %collective-permute-start.9 = (f32[128,256]{1,0:T(8,128)S(1)}, f32[128,256]{1,0:T(8,128)S(1)}, u32[]{:S(2)}, u32[]{:S(2)}) collective-permute-start(f32[128,256]{1,0:T(8,128)S(1)} %collective-permute-done.8), channel_id=1, source_target_pairs={{0,14},{1,15},{2,0},{3,1},{4,2},{5,3},{6,4},{7,5},{8,6},{9,7},{10,... | collective-permute-start | bytes 393224 | tf_op jit(solution)/shard_map/ppermute | solution.py:189
  40.2 2.3 %collective-permute-done.12 = f32[128,256]{1,0:T(8,128)S(1)} collective-permute-done((f32[128,256]{1,0:T(8,128)S(1)}, f32[128,256]{1,0:T(8,128)S(1)}, u32[]{:S(2)}, u32[]{:S(2)}) %collective-permute-start.12) | collective-permute-done | bytes 131104 | tf_op jit(solution)/shard_map/ppermute | solution.py:189
  42.6 2.7 %collective-permute-start.14 = (f32[64,256]{1,0:T(8,128)S(1)}, f32[64,256]{1,0:T(8,128)S(1)}, u32[]{:S(2)}, u32[]{:S(2)}) collective-permute-start(f32[64,256]{1,0:T(8,128)S(1)} %slice.87), channel_id=1, source_target_pairs={{0,14},{1,15},{2,0},{3,1},{4,2},{5,3},{6,4},{7,5},{8,6},{9,7},{10,... | collective-permute-start | bytes 196616 | tf_op jit(solution)/shard_map/ppermute | solution.py:189
  45.3 2.5 %collective-permute-done.13 = f32[64,256]{1,0:T(8,128)S(1)} collective-permute-done((f32[64,256]{1,0:T(8,128)S(1)}, f32[64,256]{1,0:T(8,128)S(1)}, u32[]{:S(2)}, u32[]{:S(2)}) %collective-permute-start.13) | collective-permute-done | bytes 65568 | tf_op jit(solution)/shard_map/ppermute | solution.py:189
  47.9 6.0 %collective-permute-start.15 = (f32[1024,256]{1,0:T(8,128)S(1)}, f32[1024,256]{1,0:T(8,128)S(1)}, u32[]{:S(2)}, u32[]{:S(2)}) collective-permute-start(f32[1024,256]{1,0:T(8,128)S(1)} %constant_dynamic-update-slice_fusion.own_ref), channel_id=1, source_target_pairs={{0,1},{1,0},{2,3},{3,2},{4,5},{5,4},{6,7},{7,6},{8,9},{9,8},{10,11... | collective-permute-start | bytes 3145736 | tf_op jit(solution)/shard_map/ppermute | solution.py:203
  54.0 2.2 %collective-permute-done.15.other_ref = f32[1024,256]{1,0:T(8,128)S(1)} collective-permute-done((f32[1024,256]{1,0:T(8,128)S(1)}, f32[1024,256]{1,0:T(8,128)S(1)}, u32[]{:S(2)}, u32[]{:S(2)}) %collective-permute-start.15) | collective-permute-done | bytes 1048608 | tf_op jit(solution)/shard_map/ppermute | solution.py:203
  56.2 1.0 copy-done.11
  57.2 1.2 copy-done.12
  58.4 3.2 %gram.1 = (bf16[1024,512]{1,0:T(8,128)(2,1)S(1)}, bf16[1024,512]{1,0:T(8,128)(2,1)S(1)}, f32[640,128]{1,0:T(8,128)}) custom-call(s32[3]{0:T(128)S(1)} %pad_add_fusion.place, f32[1024,256]{1,0:T(8,128)S(1)} %constant_dynamic-update-slice_fusion.own_ref, f32[1024,256]{1,0:T(8,128)S(1)} %copy-done.12), custom_call_target="tpu_custom_call" | custom-call | tf_op jit(solution)/shard_map/gram/pallas_call | solution.py:227
  61.6 6.8 %all-to-all-start = ((f32[16,40,128]{2,1,0:T(8,128)}), f32[16,40,128]{2,1,0:T(8,128)S(1)}, u32[]{:S(2)}, u32[]{:S(2)}) async-start(f32[16,40,128]{2,1,0:T(8,128)} %bitcast.11), calls=%async_computation | async-start | bytes 655360 | tf_op jit(solution)/shard_map/all_to_all | solution.py:194
  68.4 2.2 %copy-done.1 = f32[1024,4,256]{2,0,1:T(8,128)S(1)} copy-done((f32[1024,4,256]{2,0,1:T(8,128)S(1)}, f32[1024,4,256]{2,0,1:T(8,128)}, u32[]{:S(2)}) %copy-start.1) | copy-done | bytes 4194328
  70.5 6.5 %product.1 = f32[512,1024]{1,0:T(8,128)} custom-call(s32[3]{0:T(128)S(1)} %pad_add_fusion.place, bf16[1024,512]{1,0:T(8,128)(2,1)S(1)} %get-tuple-element.9.high_ref, bf16[1024,512]{1,0:T(8,128)(2,1)S(1)} %get-tuple-element.10.low_ref, f32[4,1024,256]{2,1,0:T(8,128)S(1)} %bitcast.43, f32[4,1024,256]{2,1,0:T(8,128)S(1)} %bitcast.44), custom_call_target="tpu_custom_call" | custom-call | tf_op jit(solution)/shard_map/product/pallas_call | solution.py:238
  77.2 6.6 %all-to-all-start.2 = ((f32[16,32,1024]{2,1,0:T(8,128)}), f32[16,32,1024]{2,1,0:T(8,128)S(1)}, u32[]{:S(2)}, u32[]{:S(2)}) async-start(f32[16,32,1024]{2,1,0:T(8,128)} %bitcast.14), calls=%async_computation.2 | async-start | bytes 4194304 | tf_op jit(solution)/shard_map/all_to_all | solution.py:194
  83.8 29.7 %all-to-all-done.2 = f32[16,32,1024]{2,1,0:T(8,128)S(1)} async-done(((f32[16,32,1024]{2,1,0:T(8,128)}), f32[16,32,1024]{2,1,0:T(8,128)S(1)}, u32[]{:S(2)}, u32[]{:S(2)}) %all-to-all-start.2) | async-done | bytes 2097184 | tf_op jit(solution)/shard_map/all_to_all | solution.py:194
  114.2 4.7 %all-to-all-start.1 = ((f32[16,40,128]{2,1,0:T(8,128)}), f32[16,40,128]{2,1,0:T(8,128)S(1)}, u32[]{:S(2)}, u32[]{:S(2)}) async-start(f32[16,40,128]{2,1,0:T(8,128)} %broadcast_in_dim.10), calls=%async_computation.1 | async-start | bytes 655360 | tf_op jit(solution)/shard_map/all_to_all | solution.py:199
  119.1 8.0 %all-to-all-done.1 = f32[16,40,128]{2,1,0:T(8,128)S(1)} async-done(((f32[16,40,128]{2,1,0:T(8,128)}), f32[16,40,128]{2,1,0:T(8,128)S(1)}, u32[]{:S(2)}, u32[]{:S(2)}) %all-to-all-start.1) | async-done | bytes 327712 | tf_op jit(solution)/shard_map/all_to_all | solution.py:199
  127.0 1.6 broadcast_in_dim.11
  128.6 3.9 %all-to-all-start.3 = ((f32[16,32,1024]{2,1,0:T(8,128)}), f32[16,32,1024]{2,1,0:T(8,128)S(1)}, u32[]{:S(2)}, u32[]{:S(2)}) async-start(f32[16,32,1024]{2,1,0:T(8,128)} %broadcast_in_dim.11), calls=%async_computation.3 | async-start | bytes 4194304 | tf_op jit(solution)/shard_map/all_to_all | solution.py:199
  132.5 2.3 %collective-permute-start.16 = (f32[640,128]{1,0:T(8,128)S(1)}, f32[640,128]{1,0:T(8,128)S(1)}, u32[]{:S(2)}, u32[]{:S(2)}) collective-permute-start(f32[640,128]{1,0:T(8,128)S(1)} %bitcast.49), channel_id=1, source_target_pairs={{0,1},{1,0},{2,3},{3,2},{4,5},{5,4},{6,7},{7,6},{8,9},{9,8},{10,11... | collective-permute-start | bytes 983048 | tf_op jit(solution)/shard_map/ppermute | solution.py:203
  134.8 1.3 collective-permute-done.16.other_ref
  136.1 28.8 %factor.1.m_ref = f32[512,512]{1,0:T(8,128)S(1)} custom-call(s32[3]{0:T(128)S(1)} %pad_add_fusion.place, f32[640,128]{1,0:T(8,128)S(1)} %bitcast.50, f32[640,128]{1,0:T(8,128)S(1)} %collective-permute-done.16.other_ref), custom_call_target="tpu_custom_call" | custom-call | tf_op jit(solution)/shard_map/factor/pallas_call | solution.py:254
  164.9 1.2 copy-done.4
  166.1 1.2 copy-done.6
  167.3 5.8 %basis.1 = (bf16[1024,512]{1,0:T(8,128)(2,1)S(1)}, bf16[1024,512]{1,0:T(8,128)(2,1)S(1)}) custom-call(s32[3]{0:T(128)S(1)} %pad_add_fusion.place, bf16[1024,512]{1,0:T(8,128)(2,1)S(1)} %copy-done.4, bf16[1024,512]{1,0:T(8,128)(2,1)S(1)} %copy-done.6, f32[512,512]{1,0:T(8,128)S(1)} %factor.1.m_ref), custom_call_target="tpu_custom_call" | custom-call | tf_op jit(solution)/shard_map/basis/pallas_call | solution.py:264
  174.1 1.0 copy-done.9
  175.1 2.2 %copy-done.2 = f32[1024,4,256]{2,0,1:T(8,128)S(1)} copy-done((f32[1024,4,256]{2,0,1:T(8,128)S(1)}, f32[1024,4,256]{2,0,1:T(8,128)}, u32[]{:S(2)}) %copy-start.2) | copy-done | bytes 4194328
  177.3 1.2 copy-done.8
  178.5 1.2 copy-done.10
  179.7 7.1 %remainder.1 = (f32[4,512,256]{2,1,0:T(8,128)S(1)}, f32[4,1024,256]{2,1,0:T(8,128)S(1)}) custom-call(s32[3]{0:T(128)S(1)} %pad_add_fusion.place, bf16[1024,512]{1,0:T(8,128)(2,1)S(1)} %copy-done.8, bf16[1024,512]{1,0:T(8,128)(2,1)S(1)} %copy-done.10, f32[4,1024,256]{2,1,0:T(8,128)S(1)} %bitcast.45, f32[512,512]{1,0:T(8,128)S(1)} %factor.1.m_ref, ...), custom_call_target="tpu_custom_call" | custom-call | tf_op jit(solution)/shard_map/remainder/pallas_call | solution.py:272
  186.9 2.7 %copy.12 = f32[512,4,256]{2,1,0:T(4,128)} copy(f32[512,4,256]{2,0,1:T(8,128)S(1)} %bitcast.48) | data formatting | bytes 4194304
  189.5 4.7 %copy.13 = f32[1024,4,256]{2,1,0:T(4,128)} copy(f32[1024,4,256]{2,0,1:T(8,128)S(1)} %bitcast.47) | data formatting | bytes 8388608
  (45 shorter events, 3.3 us)
Async XLA Ops:
  3.6 2.0 %copy-start = (f32[1024,4,256]{2,0,1:T(8,128)}, f32[1024,4,256]{2,0,1:T(8,128)S(1)}, u32[]{:S(2)}) copy-start(f32[1024,4,256]{2,0,1:T(8,128)S(1)} %copy.16) | copy-start | bytes 12582916
  5.7 12.9 %collective-permute-start = (f32[128,256]{1,0:T(8,128)S(1)}, f32[128,256]{1,0:T(8,128)S(1)}, u32[]{:S(2)}, u32[]{:S(2)}) collective-permute-start(f32[128,256]{1,0:T(8,128)S(1)} %get-tuple-element.22), channel_id=1, source_target_pairs={{0,2},{1,3},{16,18},{17,19},{32,34},{33,35},{48,50},{49,51},{64,66... | collective-permute-start | bytes 393224 | tf_op jit(solution)/shard_map/ppermute | solution.py:209
  10.1 9.8 %collective-permute-start.6 = (f32[128,256]{1,0:T(8,128)S(1)}, f32[128,256]{1,0:T(8,128)S(1)}, u32[]{:S(2)}, u32[]{:S(2)}) collective-permute-start(f32[128,256]{1,0:T(8,128)S(1)} %get-tuple-element.23), channel_id=1, source_target_pairs={{0,14},{1,15},{16,30},{17,31},{32,46},{33,47},{48,62},{49,63},{64,... | collective-permute-start | bytes 393224 | tf_op jit(solution)/shard_map/ppermute | solution.py:209
  14.7 6.6 %collective-permute-start.5 = (f32[128,256]{1,0:T(8,128)S(1)}, f32[128,256]{1,0:T(8,128)S(1)}, u32[]{:S(2)}, u32[]{:S(2)}) collective-permute-start(f32[128,256]{1,0:T(8,128)S(1)} %get-tuple-element.24), channel_id=1, source_target_pairs={{0,12},{1,13},{16,28},{17,29},{32,44},{33,45},{48,60},{49,61},{64,... | collective-permute-start | bytes 393224 | tf_op jit(solution)/shard_map/ppermute | solution.py:209
  16.0 6.5 %collective-permute-start.4 = (f32[128,256]{1,0:T(8,128)S(1)}, f32[128,256]{1,0:T(8,128)S(1)}, u32[]{:S(2)}, u32[]{:S(2)}) collective-permute-start(f32[128,256]{1,0:T(8,128)S(1)} %get-tuple-element.25), channel_id=1, source_target_pairs={{0,10},{1,11},{16,26},{17,27},{32,42},{33,43},{48,58},{49,59},{64,... | collective-permute-start | bytes 393224 | tf_op jit(solution)/shard_map/ppermute | solution.py:209
  17.4 5.2 %collective-permute-start.3 = (f32[128,256]{1,0:T(8,128)S(1)}, f32[128,256]{1,0:T(8,128)S(1)}, u32[]{:S(2)}, u32[]{:S(2)}) collective-permute-start(f32[128,256]{1,0:T(8,128)S(1)} %get-tuple-element.26), channel_id=1, source_target_pairs={{0,8},{1,9},{16,24},{17,25},{32,40},{33,41},{48,56},{49,57},{64,72... | collective-permute-start | bytes 393224 | tf_op jit(solution)/shard_map/ppermute | solution.py:209
  18.7 4.9 %collective-permute-start.2 = (f32[128,256]{1,0:T(8,128)S(1)}, f32[128,256]{1,0:T(8,128)S(1)}, u32[]{:S(2)}, u32[]{:S(2)}) collective-permute-start(f32[128,256]{1,0:T(8,128)S(1)} %get-tuple-element.27), channel_id=1, source_target_pairs={{0,6},{1,7},{16,22},{17,23},{32,38},{33,39},{48,54},{49,55},{64,70... | collective-permute-start | bytes 393224 | tf_op jit(solution)/shard_map/ppermute | solution.py:209
  20.0 6.4 %collective-permute-start.1 = (f32[128,256]{1,0:T(8,128)S(1)}, f32[128,256]{1,0:T(8,128)S(1)}, u32[]{:S(2)}, u32[]{:S(2)}) collective-permute-start(f32[128,256]{1,0:T(8,128)S(1)} %get-tuple-element.28), channel_id=1, source_target_pairs={{0,4},{1,5},{16,20},{17,21},{32,36},{33,37},{48,52},{49,53},{64,68... | collective-permute-start | bytes 393224 | tf_op jit(solution)/shard_map/ppermute | solution.py:209
  27.4 5.1 %collective-permute-start.10 = (f32[128,256]{1,0:T(8,128)S(1)}, f32[128,256]{1,0:T(8,128)S(1)}, u32[]{:S(2)}, u32[]{:S(2)}) collective-permute-start(f32[128,256]{1,0:T(8,128)S(1)} %get-tuple-element.19), channel_id=1, source_target_pairs={{0,2},{1,3},{2,4},{3,5},{4,6},{5,7},{6,8},{7,9},{8,10},{9,11},{10,... | collective-permute-start | bytes 393224 | tf_op jit(solution)/shard_map/ppermute | solution.py:189
  27.5 6.0 %collective-permute-start.7 = (f32[128,256]{1,0:T(8,128)S(1)}, f32[128,256]{1,0:T(8,128)S(1)}, u32[]{:S(2)}, u32[]{:S(2)}) collective-permute-start(f32[128,256]{1,0:T(8,128)S(1)} %get-tuple-element.19), channel_id=1, source_target_pairs={{0,14},{1,15},{2,0},{3,1},{4,2},{5,3},{6,4},{7,5},{8,6},{9,7},{10,... | collective-permute-start | bytes 393224 | tf_op jit(solution)/shard_map/ppermute | solution.py:189
  32.5 5.0 %collective-permute-start.11 = (f32[128,256]{1,0:T(8,128)S(1)}, f32[128,256]{1,0:T(8,128)S(1)}, u32[]{:S(2)}, u32[]{:S(2)}) collective-permute-start(f32[128,256]{1,0:T(8,128)S(1)} %collective-permute-done.10), channel_id=1, source_target_pairs={{0,2},{1,3},{2,4},{3,5},{4,6},{5,7},{6,8},{7,9},{8,10},{9,11},{10,... | collective-permute-start | bytes 393224 | tf_op jit(solution)/shard_map/ppermute | solution.py:189
  33.5 4.0 %collective-permute-start.8 = (f32[128,256]{1,0:T(8,128)S(1)}, f32[128,256]{1,0:T(8,128)S(1)}, u32[]{:S(2)}, u32[]{:S(2)}) collective-permute-start(f32[128,256]{1,0:T(8,128)S(1)} %collective-permute-done.7), channel_id=1, source_target_pairs={{0,14},{1,15},{2,0},{3,1},{4,2},{5,3},{6,4},{7,5},{8,6},{9,7},{10,... | collective-permute-start | bytes 393224 | tf_op jit(solution)/shard_map/ppermute | solution.py:189
  37.5 5.0 %collective-permute-start.12 = (f32[128,256]{1,0:T(8,128)S(1)}, f32[128,256]{1,0:T(8,128)S(1)}, u32[]{:S(2)}, u32[]{:S(2)}) collective-permute-start(f32[128,256]{1,0:T(8,128)S(1)} %collective-permute-done.11), channel_id=1, source_target_pairs={{0,2},{1,3},{2,4},{3,5},{4,6},{5,7},{6,8},{7,9},{8,10},{9,11},{10,... | collective-permute-start | bytes 393224 | tf_op jit(solution)/shard_map/ppermute | solution.py:189
  37.5 5.0 %collective-permute-start.9 = (f32[128,256]{1,0:T(8,128)S(1)}, f32[128,256]{1,0:T(8,128)S(1)}, u32[]{:S(2)}, u32[]{:S(2)}) collective-permute-start(f32[128,256]{1,0:T(8,128)S(1)} %collective-permute-done.8), channel_id=1, source_target_pairs={{0,14},{1,15},{2,0},{3,1},{4,2},{5,3},{6,4},{7,5},{8,6},{9,7},{10,... | collective-permute-start | bytes 393224 | tf_op jit(solution)/shard_map/ppermute | solution.py:189
  42.6 5.3 %collective-permute-start.13 = (f32[64,256]{1,0:T(8,128)S(1)}, f32[64,256]{1,0:T(8,128)S(1)}, u32[]{:S(2)}, u32[]{:S(2)}) collective-permute-start(f32[64,256]{1,0:T(8,128)S(1)} %slice.86), channel_id=1, source_target_pairs={{0,2},{1,3},{2,4},{3,5},{4,6},{5,7},{6,8},{7,9},{8,10},{9,11},{10,... | collective-permute-start | bytes 196616 | tf_op jit(solution)/shard_map/ppermute | solution.py:189
  42.6 5.3 %collective-permute-start.14 = (f32[64,256]{1,0:T(8,128)S(1)}, f32[64,256]{1,0:T(8,128)S(1)}, u32[]{:S(2)}, u32[]{:S(2)}) collective-permute-start(f32[64,256]{1,0:T(8,128)S(1)} %slice.87), channel_id=1, source_target_pairs={{0,14},{1,15},{2,0},{3,1},{4,2},{5,3},{6,4},{7,5},{8,6},{9,7},{10,... | collective-permute-start | bytes 196616 | tf_op jit(solution)/shard_map/ppermute | solution.py:189
  47.9 8.3 %collective-permute-start.15 = (f32[1024,256]{1,0:T(8,128)S(1)}, f32[1024,256]{1,0:T(8,128)S(1)}, u32[]{:S(2)}, u32[]{:S(2)}) collective-permute-start(f32[1024,256]{1,0:T(8,128)S(1)} %constant_dynamic-update-slice_fusion.own_ref), channel_id=1, source_target_pairs={{0,1},{1,0},{2,3},{3,2},{4,5},{5,4},{6,7},{7,6},{8,9},{9,8},{10,11... | collective-permute-start | bytes 3145736 | tf_op jit(solution)/shard_map/ppermute | solution.py:203
  56.2 1.0 copy-start.11
  57.2 1.2 copy-start.12
  61.6 15.5 %copy-start.3 = (bf16[1024,512]{1,0:T(8,128)(2,1)}, bf16[1024,512]{1,0:T(8,128)(2,1)S(1)}, u32[]{:S(2)}) copy-start(bf16[1024,512]{1,0:T(8,128)(2,1)S(1)} %get-tuple-element.9.high_ref) | copy-start | bytes 3145732
  61.6 15.5 %copy-start.5 = (bf16[1024,512]{1,0:T(8,128)(2,1)}, bf16[1024,512]{1,0:T(8,128)(2,1)S(1)}, u32[]{:S(2)}) copy-start(bf16[1024,512]{1,0:T(8,128)(2,1)S(1)} %get-tuple-element.10.low_ref) | copy-start | bytes 3145732
  61.6 15.6 %all-to-all-start = ((f32[16,40,128]{2,1,0:T(8,128)}), f32[16,40,128]{2,1,0:T(8,128)S(1)}, u32[]{:S(2)}, u32[]{:S(2)}) async-start(f32[16,40,128]{2,1,0:T(8,128)} %bitcast.11), calls=%async_computation | async-start | bytes 655360 | tf_op jit(solution)/shard_map/all_to_all | solution.py:194
  68.4 2.2 %copy-start.1 = (f32[1024,4,256]{2,0,1:T(8,128)S(1)}, f32[1024,4,256]{2,0,1:T(8,128)}, u32[]{:S(2)}) copy-start(f32[1024,4,256]{2,0,1:T(8,128)} %copy-done) | copy-start | bytes 12582916
  77.2 36.3 %all-to-all-start.2 = ((f32[16,32,1024]{2,1,0:T(8,128)}), f32[16,32,1024]{2,1,0:T(8,128)S(1)}, u32[]{:S(2)}, u32[]{:S(2)}) async-start(f32[16,32,1024]{2,1,0:T(8,128)} %bitcast.14), calls=%async_computation.2 | async-start | bytes 4194304 | tf_op jit(solution)/shard_map/all_to_all | solution.py:194
  114.2 12.8 %all-to-all-start.1 = ((f32[16,40,128]{2,1,0:T(8,128)}), f32[16,40,128]{2,1,0:T(8,128)S(1)}, u32[]{:S(2)}, u32[]{:S(2)}) async-start(f32[16,40,128]{2,1,0:T(8,128)} %broadcast_in_dim.10), calls=%async_computation.1 | async-start | bytes 655360 | tf_op jit(solution)/shard_map/all_to_all | solution.py:199
  128.6 46.5 %all-to-all-start.3 = ((f32[16,32,1024]{2,1,0:T(8,128)}), f32[16,32,1024]{2,1,0:T(8,128)S(1)}, u32[]{:S(2)}, u32[]{:S(2)}) async-start(f32[16,32,1024]{2,1,0:T(8,128)} %broadcast_in_dim.11), calls=%async_computation.3 | async-start | bytes 4194304 | tf_op jit(solution)/shard_map/all_to_all | solution.py:199
  132.5 3.6 %collective-permute-start.16 = (f32[640,128]{1,0:T(8,128)S(1)}, f32[640,128]{1,0:T(8,128)S(1)}, u32[]{:S(2)}, u32[]{:S(2)}) collective-permute-start(f32[640,128]{1,0:T(8,128)S(1)} %bitcast.49), channel_id=1, source_target_pairs={{0,1},{1,0},{2,3},{3,2},{4,5},{5,4},{6,7},{7,6},{8,9},{9,8},{10,11... | collective-permute-start | bytes 983048 | tf_op jit(solution)/shard_map/ppermute | solution.py:203
  164.9 1.2 copy-start.4
  166.1 1.2 copy-start.6
  173.2 1.0 copy-start.7
  174.1 1.0 copy-start.9
  175.1 2.2 %copy-start.2 = (f32[1024,4,256]{2,0,1:T(8,128)S(1)}, f32[1024,4,256]{2,0,1:T(8,128)}, u32[]{:S(2)}) copy-start(f32[1024,4,256]{2,0,1:T(8,128)} %copy-done) | copy-start | bytes 12582916
  177.3 1.2 copy-start.8
  178.5 1.2 copy-start.10
where the time goes:
time: 195 us; the launch traced here: 194 us
  waiting for transfers between devices  56.6 us (29%)
  starting transfers between devices  55.8 us (29%)
  Pallas kernels  51.4 us (26%)
  local copies, waits for them, and re-layouts  28.3 us (15%)
    all_to_all x2, waiting for transfers between devices, exchange(): return lax.all_to_all(x.reshape(PEERS, rows // PEERS, width), 'row', 0, 0)  29.8 us
    pallas_call x1, Pallas kernels, on_device(): call(factor_kernel, 'factor', 12, (1,), [whole(HALF_ROWS, TILE)] * 2, who...  28.8 us
    unnamed x36, local copies, waits for them, and re-layouts  25.8 us
    ppermute x7, starting transfers between devices, share_panel(): lax.ppermute(mine[k * PIECE:(k + 1) * PIECE], 'col', [(0, 2 * k), (1, 2 *...  15.5 us
    all_to_all x2, starting transfers between devices, exchange(): return lax.all_to_all(x.reshape(PEERS, rows // PEERS, width), 'row', 0, 0)  13.3 us
    ppermute x8, waiting for transfers between devices, shift(): return lax.ppermute(x, axis, [(i, (i + by) % PEERS) for i in range(PEERS)])  10.2 us
    ppermute x8, starting transfers between devices, shift(): return lax.ppermute(x, axis, [(i, (i + by) % PEERS) for i in range(PEERS)])  10.1 us
    all_to_all x2, starting transfers between devices, everywhere(): lax.all_to_all(total, 'row', 0, 0)  8.58 us
  transfers between devices with their start and end apart: 21, of which 13 were waited for; matrix products, arithmetic and copies ran while one was open for 0% of the time, Pallas kernels for 21%

commit v1 on v0

--- a/solution.py
+++ b/solution.py
@@ -15,6 +15,8 @@
 PIECE = 128
 HALF = ((0, 0), (1, 0), (1, 1), (2, 0), (2, 1)), ((2, 2), (3, 0), (3, 1), (3, 2), (3, 3))
 HALF_ROWS = len(HALF[0]) * TILE
+SHARE = FULL // PEERS
+TILES = HALF_ROWS // 8 // PEERS
 
 highest = lax.Precision.HIGHEST
 by_rows = ((0,), (0,))
@@ -87,39 +89,54 @@
     return one_pass(a[0], b[0], dims) + (one_pass(a[0], b[1], dims) + one_pass(a[1], b[0], dims))
 
 
-def gram_kernel(place, own_ref, other_ref, high_ref, low_ref, gram_ref):
+def panel_kernel(matrix_ref, out_ref, sem):
+    copy = pltpu.make_async_copy(matrix_ref.at[:, 0, :], out_ref, sem)
+    copy.start()
+    copy.wait()
+
+
+def product_kernel(place, own_ref, other_ref, a0_ref, a1_ref, high_ref, low_ref, terms_ref, gram_ref):
+    start = pl.program_id(0) == 0
+
+    @pl.when(start)
+    def _():
+        terms_ref[...] = jnp.zeros_like(terms_ref)
+        gram_ref[...] = jnp.zeros_like(gram_ref)
+
     first = place[1] == 0
     own, other = own_ref[...], other_ref[...]
-    panel = jnp.concatenate([jnp.where(first, own, other), jnp.where(first, other, own)], axis=1)
-    parts = split(panel)
-    high_ref[...], low_ref[...] = parts
-    gram = three_pass(parts, parts, by_rows)
-    for t in range(len(HALF[0])):
-        (i, j), (p, q) = HALF[0][t], HALF[1][t]
-        here = gram[i * TILE : (i + 1) * TILE, j * TILE : (j + 1) * TILE]
-        there = gram[p * TILE : (p + 1) * TILE, q * TILE : (q + 1) * TILE]
-        gram_ref[t * TILE : (t + 1) * TILE, :] = jnp.where(first, here, there)
-
-
-def product_kernel(place, high_ref, low_ref, a0_ref, a1_ref, acc_ref):
-    @pl.when(pl.program_id(0) == 0)
+    panel = split(jnp.concatenate([jnp.where(first, own, other), jnp.where(first, other, own)], axis=1))
+    high_ref[...], low_ref[...] = panel
+    gram_ref[...] += three_pass(panel, panel, by_rows)
+    for l in range(a0_ref.shape[1]):
+        a = split(jnp.concatenate([a0_ref[:, l, :], a1_ref[:, l, :]], axis=0))
+        part = three_pass(panel, a, by_rows)
+        for r in range(PEERS):
+            terms_ref[r, :SHARE, l * BLOCK : (l + 1) * BLOCK] += part[r * SHARE : (r + 1) * SHARE]
+
+    @pl.when(pl.program_id(0) == pl.num_programs(0) - 1)
     def _():
-        acc_ref[...] = jnp.zeros_like(acc_ref)
-
-    panel = high_ref[...], low_ref[...]
-    for l in range(a0_ref.shape[0]):
-        a = split(jnp.concatenate([a0_ref[l], a1_ref[l]], axis=0))
-        acc_ref[:, l * BLOCK : (l + 1) * BLOCK] += three_pass(panel, a, by_rows)
-
-
-def factor_kernel(place, own_ref, other_ref, m_ref, s_ref, t_ref):
+        for n in range(HALF_ROWS // 8):
+            (i, j), (p, q) = (half[n // 16] for half in HALF)
+            top = n % 16 * 8
+            here = gram_ref[i * TILE + top : i * TILE + top + 8, j * TILE : (j + 1) * TILE]
+            there = gram_ref[p * TILE + top : p * TILE + top + 8, q * TILE : (q + 1) * TILE]
+            lane = n % TILES * TILE
+            terms_ref[n // TILES, SHARE:, lane : lane + TILE] = jnp.where(first, here, there)
+
+
+def factor_kernel(place, own_ref, other_ref, high_ref, low_ref, m_ref, qh_ref, ql_ref, s_ref, t_ref):
     first = place[1] == 0
     s_ref[...] = jnp.zeros_like(s_ref)
     t_ref[...] = jnp.zeros_like(t_ref)
-    for t in range(len(HALF[0])):
-        own, other = own_ref[t * TILE : (t + 1) * TILE, :], other_ref[t * TILE : (t + 1) * TILE, :]
-        for (i, j), block in zip((HALF[0][t], HALF[1][t]), (jnp.where(first, own, other), jnp.where(first, other, own))):
-            s_ref[j, i * TILE : (i + 1) * TILE, :] = block
+    for n in range(HALF_ROWS // 8):
+        (i, j), (p, q) = (half[n // 16] for half in HALF)
+        top = n % 16 * 8
+        lane = n % TILES * TILE
+        own = own_ref[n // TILES, :, lane : lane + TILE]
+        other = other_ref[n // TILES, :, lane : lane + TILE]
+        s_ref[j, i * TILE + top : i * TILE + top + 8, :] = jnp.where(first, own, other)
+        s_ref[q, p * TILE + top : p * TILE + top + 8, :] = jnp.where(first, other, own)
 
     @pl.loop(0, NB)
     def _(j):
@@ -139,10 +156,15 @@
                 s_ref[i] -= mm(low, part, by_cols)
                 t_ref[i] -= mm(part, mrow, plain)
 
-
-def basis_kernel(place, high_ref, low_ref, m_ref, qh_ref, ql_ref):
-    q = three_pass((high_ref[...], low_ref[...]), split(m_ref[...]), by_cols)
-    qh_ref[...], ql_ref[...] = split(q)
+    factor = split(m_ref[...])
+    step = 2 * PIECE
+    for g in range(0, DEPTH, 2):
+        window = slice(g * PIECE, g * PIECE + step)
+        q = split(three_pass((high_ref[window], low_ref[window]), factor, by_cols))
+        for e in range(2):
+            spot = pl.ds(pl.multiple_of(lax.rem(place[0] + g + e, DEPTH) * PIECE, PIECE), PIECE)
+            qh_ref[spot, :] = q[0][e * PIECE : (e + 1) * PIECE]
+            ql_ref[spot, :] = q[1][e * PIECE : (e + 1) * PIECE]
 
 
 def remainder_kernel(place, qh_ref, ql_ref, a_ref, m_ref, w_ref, coeff_ref, out_ref, ch_ref, cl_ref):
@@ -151,14 +173,14 @@
     @pl.when(pl.program_id(0) == 0)
     def _():
         coeffs = three_pass(split(m_ref[...]), split(w_ref[...]), plain)
-        for l in range(coeff_ref.shape[0]):
-            coeff_ref[l] = coeffs[:, l * width : (l + 1) * width]
+        for l in range(coeff_ref.shape[1]):
+            coeff_ref[:, l, :] = coeffs[:, l * width : (l + 1) * width]
         ch_ref[...], cl_ref[...] = split(coeffs)
 
     q = qh_ref[...], ql_ref[...]
-    for l in range(a_ref.shape[0]):
+    for l in range(a_ref.shape[1]):
         window = slice(l * width, (l + 1) * width)
-        out_ref[l] = a_ref[l] - three_pass(q, (ch_ref[:, window], cl_ref[:, window]), plain)
+        out_ref[:, l, :] = a_ref[:, l, :] - three_pass(q, (ch_ref[:, window], cl_ref[:, window]), plain)
 
 
 def call(kernel, name, mib, grid, ins, outs, out_shape, scratch=()):
@@ -182,21 +204,19 @@
 
 
 def bf16(*shape):
-    return jax.ShapeDtypeStruct(shape, jnp.bfloat16)
+    return pltpu.HBM(shape, jnp.bfloat16)
+
+
+def in_hbm(*arrays):
+    return [pltpu.with_memory_space_constraint(x, pltpu.HBM) for x in arrays]
 
 
 def shift(x, axis, by):
     return lax.ppermute(x, axis, [(i, (i + by) % PEERS) for i in range(PEERS)])
 
 
-def exchange(x):
-    rows, width = x.shape
-    return lax.all_to_all(x.reshape(PEERS, rows // PEERS, width), "row", 0, 0)
-
-
-def everywhere(shares):
-    total = jnp.broadcast_to(jnp.sum(shares, axis=0), shares.shape)
-    return lax.all_to_all(total, "row", 0, 0).reshape(shares.shape[0] * shares.shape[1], shares.shape[2])
+def everywhere(share):
+    return lax.all_to_all(jnp.broadcast_to(share, (PEERS,) + share.shape), "row", 0, 0)
 
 
 def swap_cores(x):
@@ -222,61 +242,52 @@
     z, core, row = col // 2, col % 2, lax.axis_index("row")
     place = jnp.stack([z, core, row]).astype(jnp.int32)
 
-    own = share_panel(matrix[:, 0, :], z)
+    mine = pl.pallas_call(
+        panel_kernel,
+        in_specs=[pl.BlockSpec(memory_space=pl.ANY)],
+        out_specs=pl.BlockSpec(memory_space=pltpu.VMEM),
+        out_shape=f32(rows, width),
+        scratch_shapes=[pltpu.SemaphoreType.DMA],
+        name="panel",
+    )(matrix)
+    own = share_panel(mine, z)
     other = swap_cores(own)
-    high, low, gram = call(
-        gram_kernel, "gram", 20, (1,),
-        [whole(rows, BLOCK), whole(rows, BLOCK)],
-        [whole(rows, FULL), whole(rows, FULL), whole(HALF_ROWS, TILE)],
-        [bf16(rows, FULL), bf16(rows, FULL), f32(HALF_ROWS, TILE)],
-    )(place, own, other)
-
-    stacked = jnp.transpose(matrix, (1, 0, 2))
+
     step = 2 * PIECE
     steps = rows // step
+    own_spec = pl.BlockSpec((step, BLOCK), lambda g, place: (g, 0))
     panel_spec = pl.BlockSpec((step, FULL), lambda g, place: (g, 0))
-    terms = call(
+    high, low, terms = call(
         product_kernel, "product", 20, (steps,),
-        [panel_spec, panel_spec]
+        [own_spec, own_spec]
         + [
-            pl.BlockSpec((blocks, PIECE, width), lambda g, place, e=e: (0, lax.rem(place[0] + 2 * g + e, DEPTH), 0))
+            pl.BlockSpec((PIECE, blocks, width), lambda g, place, e=e: (lax.rem(place[0] + 2 * g + e, DEPTH), 0, 0))
             for e in range(2)
         ],
-        whole(FULL, blocks * width),
-        f32(FULL, blocks * width),
-    )(place, high, low, stacked, stacked)
-
-    gram = exchange(gram)
-    terms = exchange(terms)
-    gram = everywhere(gram)
-    sums = everywhere(terms)
-
-    m = call(
-        factor_kernel, "factor", 12, (1,),
-        [whole(HALF_ROWS, TILE)] * 2,
-        whole(FULL, FULL),
-        f32(FULL, FULL),
+        [panel_spec, panel_spec, whole(PEERS, SHARE + 8, blocks * width)],
+        [bf16(rows, FULL), bf16(rows, FULL), f32(PEERS, SHARE + 8, blocks * width)],
+        [pltpu.VMEM((FULL, FULL), jnp.float32)],
+    )(place, own, other, *in_hbm(matrix, matrix))
+    total = jnp.sum(lax.all_to_all(terms, "row", 0, 0), axis=0)
+    gram = everywhere(total[SHARE:, : TILES * TILE])
+    sums = everywhere(total[:SHARE]).reshape(FULL, blocks * width)
+
+    m, qh, ql = call(
+        factor_kernel, "factor", 20, (1,),
+        [whole(PEERS, 8, TILES * TILE)] * 2 + [whole(rows, FULL)] * 2,
+        [whole(FULL, FULL), whole(rows, FULL), whole(rows, FULL)],
+        [f32(FULL, FULL), bf16(rows, FULL), bf16(rows, FULL)],
         [pltpu.VMEM((NB, FULL, TILE), jnp.float32), pltpu.VMEM((NB, TILE, FULL), jnp.float32)],
-    )(place, gram, swap_cores(gram))
-
-    rolled = pl.BlockSpec((PIECE, FULL), lambda g, place: (g, 0))
-    natural = pl.BlockSpec((PIECE, FULL), lambda g, place: (lax.rem(place[0] + g, DEPTH), 0))
-    qh, ql = call(
-        basis_kernel, "basis", 14, (DEPTH,),
-        [rolled, rolled, whole(FULL, FULL)],
-        [natural, natural],
-        [bf16(rows, FULL), bf16(rows, FULL)],
-    )(place, high, low, m)
-
-    a_spec = pl.BlockSpec((blocks, step, width), lambda g, place: (0, g, 0))
-    coeffs, rest = call(
+    )(place, gram, swap_cores(gram), *in_hbm(high, low))
+
+    a_spec = pl.BlockSpec((step, blocks, width), lambda g, place: (g, 0, 0))
+    return call(
         remainder_kernel, "remainder", 22, (steps,),
         [panel_spec, panel_spec, a_spec, whole(FULL, FULL), whole(FULL, blocks * width)],
-        [whole(blocks, FULL, width), a_spec],
-        [f32(blocks, FULL, width), f32(blocks, rows, width)],
+        [whole(FULL, blocks, width), a_spec],
+        [f32(FULL, blocks, width), f32(rows, blocks, width)],
         [pltpu.VMEM((FULL, blocks * width), jnp.bfloat16)] * 2,
-    )(place, qh, ql, stacked, m, sums)
-    return jnp.transpose(coeffs, (1, 0, 2)), jnp.transpose(rest, (1, 0, 2))
+    )(place, *in_hbm(qh, ql, matrix), m, sums)
 
 
 def solution(mesh):

time: 195 us -> 171 us (0.88)
  blocking collectives: 0 us -> 39.7 us
  waiting for transfers between devices: 56.6 us -> 26.7 us
  local copies, waits for them, and re-layouts: 28.3 us -> 3.73 us
  starting transfers between devices: 55.8 us -> 42 us
  Pallas kernels: 51.4 us -> 56.2 us
    all_to_all x0 -> x1, blocking collectives: none -> 39.7 us  [on_device(): total = jnp.sum(lax.all_to_all(terms, 'row', 0, 0), axis=0)]
    all_to_all x4 -> x2, waiting for transfers between devices: 37.8 us -> 7.9 us  [everywhere(): lax.all_to_all(jnp.broadcast_to(share, (PEERS,) + share.shape), 'row', 0, 0)]
    unnamed x36 -> x7, local copies, waits for them, and re-layouts: 25.8 us -> 0.07 us
    all_to_all x4 -> x2, starting transfers between devices: 21.9 us -> 7.26 us  [everywhere(): lax.all_to_all(jnp.broadcast_to(share, (PEERS,) + share.shape), 'row', 0, 0)]
    pallas_call x1, Pallas kernels: 7.12 us -> 11.5 us  [on_device(): call(remainder_kernel, 'remainder', 22, (steps,), [panel_spec, panel_spec...]
    pallas_call x4 -> x3, Pallas kernels: 44.3 us -> 44.7 us  [the longest x1 33.5 us: on_device(): call(factor_kernel, 'factor', 20, (1,), [whole(PEERS, 8, TILES * TILE)] *...]
  transfers between devices with their start and end apart: 21 -> 19, of which waited for: 13 -> 11; matrix products, arithmetic and copies ran while one was open for 0% -> 0% of each run, Pallas kernels for 21% -> 20%
where the time goes in v1:
time: 171 us; the launch traced here: 170 us
  Pallas kernels  56.2 us (33%)
  starting transfers between devices  42 us (25%)
  blocking collectives  39.7 us (23%)
  waiting for transfers between devices  26.7 us (16%)
  local copies, waits for them, and re-layouts  3.73 us (2%)
    all_to_all x1, blocking collectives, on_device(): total = jnp.sum(lax.all_to_all(terms, 'row', 0, 0), axis=0)  39.7 us
    pallas_call x1, Pallas kernels, on_device(): call(factor_kernel, 'factor', 20, (1,), [whole(PEERS, 8, TILES * TILE)] *...  33.5 us
    ppermute x7, starting transfers between devices, share_panel(): lax.ppermute(mine[k * PIECE:(k + 1) * PIECE], 'col', [(0, 2 * k), (1, 2 *...  15.5 us
    pallas_call x1, Pallas kernels, on_device(): call(remainder_kernel, 'remainder', 22, (steps,), [panel_spec, panel_spec...  11.5 us
    ppermute x8, waiting for transfers between devices, shift(): return lax.ppermute(x, axis, [(i, (i + by) % PEERS) for i in range(PEERS)])  10.2 us
    ppermute x8, starting transfers between devices, shift(): return lax.ppermute(x, axis, [(i, (i + by) % PEERS) for i in range(PEERS)])  10.1 us
    ppermute x2, starting transfers between devices, swap_cores(): return lax.ppermute(x, 'col', [(i, i ^ 1) for i in range(PEERS)])  9.1 us
    pallas_call x1, Pallas kernels, on_device(): call(product_kernel, 'product', 20, (steps,), [own_spec, own_spec] + [pl....  9.02 us
  transfers between devices with their start and end apart: 19, of which 11 were waited for; matrix products, arithmetic and copies ran while one was open for 0% of the time, Pallas kernels for 20%

profile of v1, /device:TPU:1, one launch (start us, length us, event | category | flops | bytes accessed | tf_op | source)
XLA Modules:
  0.0 170.5 jit_solution(13445464031006732112)
XLA Ops:
  0.6 2.2 %panel.1 = f32[1024,256]{1,0:T(8,128)} custom-call(f32[1024,4,256]{2,1,0:T(4,128)} %a_ref.1), custom_call_target="tpu_custom_call" | custom-call | tf_op jit(solution)/shard_map/panel/pallas_call | solution.py:245
  2.9 1.3 fusion.8
  4.2 4.4 %collective-permute-start = (f32[128,256]{1,0:T(8,128)S(1)}, f32[128,256]{1,0:T(8,128)S(1)}, u32[]{:S(2)}, u32[]{:S(2)}) collective-permute-start(f32[128,256]{1,0:T(8,128)S(1)} %get-tuple-element.16), channel_id=1, source_target_pairs={{0,2},{1,3},{16,18},{17,19},{32,34},{33,35},{48,50},{49,51},{64,66... | collective-permute-start | bytes 393224 | tf_op jit(solution)/shard_map/ppermute | solution.py:229
  8.6 4.6 %collective-permute-start.6 = (f32[128,256]{1,0:T(8,128)S(1)}, f32[128,256]{1,0:T(8,128)S(1)}, u32[]{:S(2)}, u32[]{:S(2)}) collective-permute-start(f32[128,256]{1,0:T(8,128)S(1)} %get-tuple-element.17), channel_id=1, source_target_pairs={{0,14},{1,15},{16,30},{17,31},{32,46},{33,47},{48,62},{49,63},{64,... | collective-permute-start | bytes 393224 | tf_op jit(solution)/shard_map/ppermute | solution.py:229
  13.2 1.3 collective-permute-start.5
  14.5 1.3 collective-permute-start.4
  15.8 1.3 collective-permute-start.3
  17.1 0.0 collective-permute-done
  17.1 1.3 collective-permute-start.2
  18.4 0.0 collective-permute-done.6
  18.4 1.3 collective-permute-start.1
  19.7 0.0 collective-permute-done.5
  19.7 1.2 collective-permute-done.4
  20.9 0.0 collective-permute-done.3
  20.9 1.1 collective-permute-done.2
  22.0 2.8 %collective-permute-done.1 = f32[128,256]{1,0:T(8,128)S(1)} collective-permute-done((f32[128,256]{1,0:T(8,128)S(1)}, f32[128,256]{1,0:T(8,128)S(1)}, u32[]{:S(2)}, u32[]{:S(2)}) %collective-permute-start.1) | collective-permute-done | bytes 131104 | tf_op jit(solution)/shard_map/ppermute | solution.py:229
  24.8 1.0 constant_dynamic-update-slice_fusion.8
  25.8 0.1 collective-permute-start.10
  25.9 2.7 %collective-permute-start.7 = (f32[128,256]{1,0:T(8,128)S(1)}, f32[128,256]{1,0:T(8,128)S(1)}, u32[]{:S(2)}, u32[]{:S(2)}) collective-permute-start(f32[128,256]{1,0:T(8,128)S(1)} %get-tuple-element.15), channel_id=1, source_target_pairs={{0,14},{1,15},{2,0},{3,1},{4,2},{5,3},{6,4},{7,5},{8,6},{9,7},{10,... | collective-permute-start | bytes 393224 | tf_op jit(solution)/shard_map/ppermute | solution.py:215
  28.6 2.4 %collective-permute-done.10 = f32[128,256]{1,0:T(8,128)S(1)} collective-permute-done((f32[128,256]{1,0:T(8,128)S(1)}, f32[128,256]{1,0:T(8,128)S(1)}, u32[]{:S(2)}, u32[]{:S(2)}) %collective-permute-start.10) | collective-permute-done | bytes 131104 | tf_op jit(solution)/shard_map/ppermute | solution.py:215
  30.9 0.3 collective-permute-start.11
  31.2 0.7 collective-permute-done.7
  31.9 1.7 collective-permute-start.8
  33.6 2.3 %collective-permute-done.11 = f32[128,256]{1,0:T(8,128)S(1)} collective-permute-done((f32[128,256]{1,0:T(8,128)S(1)}, f32[128,256]{1,0:T(8,128)S(1)}, u32[]{:S(2)}, u32[]{:S(2)}) %collective-permute-start.11) | collective-permute-done | bytes 131104 | tf_op jit(solution)/shard_map/ppermute | solution.py:215
  36.0 0.0 collective-permute-start.12
  36.0 0.0 collective-permute-done.8
  36.0 2.7 %collective-permute-start.9 = (f32[128,256]{1,0:T(8,128)S(1)}, f32[128,256]{1,0:T(8,128)S(1)}, u32[]{:S(2)}, u32[]{:S(2)}) collective-permute-start(f32[128,256]{1,0:T(8,128)S(1)} %collective-permute-done.8), channel_id=1, source_target_pairs={{0,14},{1,15},{2,0},{3,1},{4,2},{5,3},{6,4},{7,5},{8,6},{9,7},{10,... | collective-permute-start | bytes 393224 | tf_op jit(solution)/shard_map/ppermute | solution.py:215
  38.7 2.3 %collective-permute-done.12 = f32[128,256]{1,0:T(8,128)S(1)} collective-permute-done((f32[128,256]{1,0:T(8,128)S(1)}, f32[128,256]{1,0:T(8,128)S(1)}, u32[]{:S(2)}, u32[]{:S(2)}) %collective-permute-start.12) | collective-permute-done | bytes 131104 | tf_op jit(solution)/shard_map/ppermute | solution.py:215
  41.0 0.0 collective-permute-done.9
  41.0 2.7 %collective-permute-start.14 = (f32[64,256]{1,0:T(8,128)S(1)}, f32[64,256]{1,0:T(8,128)S(1)}, u32[]{:S(2)}, u32[]{:S(2)}) collective-permute-start(f32[64,256]{1,0:T(8,128)S(1)} %slice.57), channel_id=1, source_target_pairs={{0,14},{1,15},{2,0},{3,1},{4,2},{5,3},{6,4},{7,5},{8,6},{9,7},{10,... | collective-permute-start | bytes 196616 | tf_op jit(solution)/shard_map/ppermute | solution.py:215
  43.8 2.5 %collective-permute-done.13 = f32[64,256]{1,0:T(8,128)S(1)} collective-permute-done((f32[64,256]{1,0:T(8,128)S(1)}, f32[64,256]{1,0:T(8,128)S(1)}, u32[]{:S(2)}, u32[]{:S(2)}) %collective-permute-start.13) | collective-permute-done | bytes 65568 | tf_op jit(solution)/shard_map/ppermute | solution.py:215
  46.3 0.0 collective-permute-done.14
  46.4 6.0 %collective-permute-start.15 = (f32[1024,256]{1,0:T(8,128)S(1)}, f32[1024,256]{1,0:T(8,128)S(1)}, u32[]{:S(2)}, u32[]{:S(2)}) collective-permute-start(f32[1024,256]{1,0:T(8,128)S(1)} %constant_dynamic-update-slice_fusion.own_ref), channel_id=1, source_target_pairs={{0,1},{1,0},{2,3},{3,2},{4,5},{5,4},{6,7},{7,6},{8,9},{9,8},{10,11... | collective-permute-start | bytes 3145736 | tf_op jit(solution)/shard_map/ppermute | solution.py:223
  52.3 0.1 pad_add_fusion.place
  52.4 2.2 %collective-permute-done.15.other_ref = f32[1024,256]{1,0:T(8,128)S(1)} collective-permute-done((f32[1024,256]{1,0:T(8,128)S(1)}, f32[1024,256]{1,0:T(8,128)S(1)}, u32[]{:S(2)}, u32[]{:S(2)}) %collective-permute-start.15) | collective-permute-done | bytes 1048608 | tf_op jit(solution)/shard_map/ppermute | solution.py:223
  54.6 9.0 %product.1 = (bf16[1024,512]{1,0:T(8,128)(2,1)}, bf16[1024,512]{1,0:T(8,128)(2,1)}, f32[16,40,1024]{2,1,0:T(8,128)S(1)}) custom-call(s32[3]{0:T(128)S(1)} %pad_add_fusion.place, f32[1024,256]{1,0:T(8,128)S(1)} %constant_dynamic-update-slice_fusion.own_ref, f32[1024,256]{1,0:T(8,128)S(1)} %collective-permute-done.15.other_ref, f32[1024,4,256]{2,1,0:T(4,128)} %a_ref.1, ...), custom_call_target="tpu_custom_call" | custom-call | tf_op jit(solution)/shard_map/product/pallas_call | solution.py:260
  63.6 39.7 %all_to_all.15 = f32[16,40,1024]{2,1,0:T(8,128)S(1)} all-to-all(f32[16,40,1024]{2,1,0:T(8,128)S(1)} %get-tuple-element.8), channel_id=1, replica_groups=mesh['row'=16,'col'=16] {'row'}, dimensions={0} | all-to-all | bytes 5242880 | tf_op jit(solution)/shard_map/all_to_all | solution.py:271
  103.4 0.2 reduce_sum.9
  103.5 0.7 broadcast_in_dim.10
  104.3 3.5 %all-to-all-start.1 = ((f32[16,8,640]{2,1,0:T(8,128)}), f32[16,8,640]{2,1,0:T(8,128)S(1)}, u32[]{:S(2)}, u32[]{:S(2)}) async-start(f32[16,8,640]{2,1,0:T(8,128)} %broadcast_in_dim.10), calls=%async_computation.1 | async-start | bytes 655360 | tf_op jit(solution)/shard_map/all_to_all | solution.py:219
  107.9 7.9 %all-to-all-done.1.own_ref = f32[16,8,640]{2,1,0:T(8,128)S(1)} async-done(((f32[16,8,640]{2,1,0:T(8,128)}), f32[16,8,640]{2,1,0:T(8,128)S(1)}, u32[]{:S(2)}, u32[]{:S(2)}) %all-to-all-start.1) | async-done | bytes 327712 | tf_op jit(solution)/shard_map/all_to_all | solution.py:219
  115.8 1.6 broadcast_in_dim.11
  117.3 3.7 %all-to-all-start.2 = ((f32[16,32,1024]{2,1,0:T(8,128)}), f32[16,32,1024]{2,1,0:T(8,128)S(1)}, u32[]{:S(2)}, u32[]{:S(2)}) async-start(f32[16,32,1024]{2,1,0:T(8,128)} %broadcast_in_dim.11), calls=%async_computation.2 | async-start | bytes 4194304 | tf_op jit(solution)/shard_map/all_to_all | solution.py:219
  121.1 3.1 %collective-permute-start.16 = (f32[16,8,640]{2,1,0:T(8,128)S(1)}, f32[16,8,640]{2,1,0:T(8,128)S(1)}, u32[]{:S(2)}, u32[]{:S(2)}) collective-permute-start(f32[16,8,640]{2,1,0:T(8,128)S(1)} %all-to-all-done.1.own_ref), channel_id=1, source_target_pairs={{0,1},{1,0},{2,3},{3,2},{4,5},{5,4},{6,7},{7,6},{8,9},{9,8},{10,11... | collective-permute-start | bytes 983048 | tf_op jit(solution)/shard_map/ppermute | solution.py:223
  124.2 1.3 collective-permute-done.16.other_ref
  125.4 33.5 %factor.1 = (f32[512,512]{1,0:T(8,128)S(1)}, bf16[1024,512]{1,0:T(8,128)(2,1)}, bf16[1024,512]{1,0:T(8,128)(2,1)}) custom-call(s32[3]{0:T(128)S(1)} %pad_add_fusion.place, f32[16,8,640]{2,1,0:T(8,128)S(1)} %all-to-all-done.1.own_ref, f32[16,8,640]{2,1,0:T(8,128)S(1)} %collective-permute-done.16.other_ref, bf16[1024,512]{1,0:T(8,128)(2,1)} %get-tuple-element.9.high_ref, ...), custom_call_target="tpu_custom_call" | custom-call | tf_op jit(solution)/shard_map/factor/pallas_call | solution.py:275
  158.9 0.0 all-to-all-done.2
  158.9 11.5 %remainder.1 = (f32[512,4,256]{2,1,0:T(4,128)}, f32[1024,4,256]{2,1,0:T(4,128)}) custom-call(s32[3]{0:T(128)S(1)} %pad_add_fusion.place, bf16[1024,512]{1,0:T(8,128)(2,1)} %get-tuple-element.11.qh_ref, bf16[1024,512]{1,0:T(8,128)(2,1)} %get-tuple-element.12.ql_ref, f32[1024,4,256]{2,1,0:T(4,128)} %a_ref.1, f32[512,512]{1,0:T(8,128)S(1)} %get-tuple-element.13.m_ref, ...), custom_call_target="tpu_custom_call" | custom-call | tf_op jit(solution)/shard_map/remainder/pallas_call | solution.py:284
  (13 shorter events, 0.1 us)
Async XLA Ops:
  4.2 12.9 %collective-permute-start = (f32[128,256]{1,0:T(8,128)S(1)}, f32[128,256]{1,0:T(8,128)S(1)}, u32[]{:S(2)}, u32[]{:S(2)}) collective-permute-start(f32[128,256]{1,0:T(8,128)S(1)} %get-tuple-element.16), channel_id=1, source_target_pairs={{0,2},{1,3},{16,18},{17,19},{32,34},{33,35},{48,50},{49,51},{64,66... | collective-permute-start | bytes 393224 | tf_op jit(solution)/shard_map/ppermute | solution.py:229
  8.6 9.8 %collective-permute-start.6 = (f32[128,256]{1,0:T(8,128)S(1)}, f32[128,256]{1,0:T(8,128)S(1)}, u32[]{:S(2)}, u32[]{:S(2)}) collective-permute-start(f32[128,256]{1,0:T(8,128)S(1)} %get-tuple-element.17), channel_id=1, source_target_pairs={{0,14},{1,15},{16,30},{17,31},{32,46},{33,47},{48,62},{49,63},{64,... | collective-permute-start | bytes 393224 | tf_op jit(solution)/shard_map/ppermute | solution.py:229
  13.2 6.6 %collective-permute-start.5 = (f32[128,256]{1,0:T(8,128)S(1)}, f32[128,256]{1,0:T(8,128)S(1)}, u32[]{:S(2)}, u32[]{:S(2)}) collective-permute-start(f32[128,256]{1,0:T(8,128)S(1)} %get-tuple-element.18), channel_id=1, source_target_pairs={{0,12},{1,13},{16,28},{17,29},{32,44},{33,45},{48,60},{49,61},{64,... | collective-permute-start | bytes 393224 | tf_op jit(solution)/shard_map/ppermute | solution.py:229
  14.5 6.5 %collective-permute-start.4 = (f32[128,256]{1,0:T(8,128)S(1)}, f32[128,256]{1,0:T(8,128)S(1)}, u32[]{:S(2)}, u32[]{:S(2)}) collective-permute-start(f32[128,256]{1,0:T(8,128)S(1)} %get-tuple-element.19), channel_id=1, source_target_pairs={{0,10},{1,11},{16,26},{17,27},{32,42},{33,43},{48,58},{49,59},{64,... | collective-permute-start | bytes 393224 | tf_op jit(solution)/shard_map/ppermute | solution.py:229
  15.8 5.2 %collective-permute-start.3 = (f32[128,256]{1,0:T(8,128)S(1)}, f32[128,256]{1,0:T(8,128)S(1)}, u32[]{:S(2)}, u32[]{:S(2)}) collective-permute-start(f32[128,256]{1,0:T(8,128)S(1)} %get-tuple-element.20), channel_id=1, source_target_pairs={{0,8},{1,9},{16,24},{17,25},{32,40},{33,41},{48,56},{49,57},{64,72... | collective-permute-start | bytes 393224 | tf_op jit(solution)/shard_map/ppermute | solution.py:229
  17.1 4.9 %collective-permute-start.2 = (f32[128,256]{1,0:T(8,128)S(1)}, f32[128,256]{1,0:T(8,128)S(1)}, u32[]{:S(2)}, u32[]{:S(2)}) collective-permute-start(f32[128,256]{1,0:T(8,128)S(1)} %get-tuple-element.21), channel_id=1, source_target_pairs={{0,6},{1,7},{16,22},{17,23},{32,38},{33,39},{48,54},{49,55},{64,70... | collective-permute-start | bytes 393224 | tf_op jit(solution)/shard_map/ppermute | solution.py:229
  18.4 6.4 %collective-permute-start.1 = (f32[128,256]{1,0:T(8,128)S(1)}, f32[128,256]{1,0:T(8,128)S(1)}, u32[]{:S(2)}, u32[]{:S(2)}) collective-permute-start(f32[128,256]{1,0:T(8,128)S(1)} %get-tuple-element.22), channel_id=1, source_target_pairs={{0,4},{1,5},{16,20},{17,21},{32,36},{33,37},{48,52},{49,53},{64,68... | collective-permute-start | bytes 393224 | tf_op jit(solution)/shard_map/ppermute | solution.py:229
  25.8 5.1 %collective-permute-start.10 = (f32[128,256]{1,0:T(8,128)S(1)}, f32[128,256]{1,0:T(8,128)S(1)}, u32[]{:S(2)}, u32[]{:S(2)}) collective-permute-start(f32[128,256]{1,0:T(8,128)S(1)} %get-tuple-element.15), channel_id=1, source_target_pairs={{0,2},{1,3},{2,4},{3,5},{4,6},{5,7},{6,8},{7,9},{8,10},{9,11},{10,... | collective-permute-start | bytes 393224 | tf_op jit(solution)/shard_map/ppermute | solution.py:215
  25.9 6.0 %collective-permute-start.7 = (f32[128,256]{1,0:T(8,128)S(1)}, f32[128,256]{1,0:T(8,128)S(1)}, u32[]{:S(2)}, u32[]{:S(2)}) collective-permute-start(f32[128,256]{1,0:T(8,128)S(1)} %get-tuple-element.15), channel_id=1, source_target_pairs={{0,14},{1,15},{2,0},{3,1},{4,2},{5,3},{6,4},{7,5},{8,6},{9,7},{10,... | collective-permute-start | bytes 393224 | tf_op jit(solution)/shard_map/ppermute | solution.py:215
  30.9 5.0 %collective-permute-start.11 = (f32[128,256]{1,0:T(8,128)S(1)}, f32[128,256]{1,0:T(8,128)S(1)}, u32[]{:S(2)}, u32[]{:S(2)}) collective-permute-start(f32[128,256]{1,0:T(8,128)S(1)} %collective-permute-done.10), channel_id=1, source_target_pairs={{0,2},{1,3},{2,4},{3,5},{4,6},{5,7},{6,8},{7,9},{8,10},{9,11},{10,... | collective-permute-start | bytes 393224 | tf_op jit(solution)/shard_map/ppermute | solution.py:215
  31.9 4.0 %collective-permute-start.8 = (f32[128,256]{1,0:T(8,128)S(1)}, f32[128,256]{1,0:T(8,128)S(1)}, u32[]{:S(2)}, u32[]{:S(2)}) collective-permute-start(f32[128,256]{1,0:T(8,128)S(1)} %collective-permute-done.7), channel_id=1, source_target_pairs={{0,14},{1,15},{2,0},{3,1},{4,2},{5,3},{6,4},{7,5},{8,6},{9,7},{10,... | collective-permute-start | bytes 393224 | tf_op jit(solution)/shard_map/ppermute | solution.py:215
  36.0 5.0 %collective-permute-start.12 = (f32[128,256]{1,0:T(8,128)S(1)}, f32[128,256]{1,0:T(8,128)S(1)}, u32[]{:S(2)}, u32[]{:S(2)}) collective-permute-start(f32[128,256]{1,0:T(8,128)S(1)} %collective-permute-done.11), channel_id=1, source_target_pairs={{0,2},{1,3},{2,4},{3,5},{4,6},{5,7},{6,8},{7,9},{8,10},{9,11},{10,... | collective-permute-start | bytes 393224 | tf_op jit(solution)/shard_map/ppermute | solution.py:215
  36.0 5.0 %collective-permute-start.9 = (f32[128,256]{1,0:T(8,128)S(1)}, f32[128,256]{1,0:T(8,128)S(1)}, u32[]{:S(2)}, u32[]{:S(2)}) collective-permute-start(f32[128,256]{1,0:T(8,128)S(1)} %collective-permute-done.8), channel_id=1, source_target_pairs={{0,14},{1,15},{2,0},{3,1},{4,2},{5,3},{6,4},{7,5},{8,6},{9,7},{10,... | collective-permute-start | bytes 393224 | tf_op jit(solution)/shard_map/ppermute | solution.py:215
  41.0 5.3 %collective-permute-start.13 = (f32[64,256]{1,0:T(8,128)S(1)}, f32[64,256]{1,0:T(8,128)S(1)}, u32[]{:S(2)}, u32[]{:S(2)}) collective-permute-start(f32[64,256]{1,0:T(8,128)S(1)} %slice.56), channel_id=1, source_target_pairs={{0,2},{1,3},{2,4},{3,5},{4,6},{5,7},{6,8},{7,9},{8,10},{9,11},{10,... | collective-permute-start | bytes 196616 | tf_op jit(solution)/shard_map/ppermute | solution.py:215
  41.0 5.3 %collective-permute-start.14 = (f32[64,256]{1,0:T(8,128)S(1)}, f32[64,256]{1,0:T(8,128)S(1)}, u32[]{:S(2)}, u32[]{:S(2)}) collective-permute-start(f32[64,256]{1,0:T(8,128)S(1)} %slice.57), channel_id=1, source_target_pairs={{0,14},{1,15},{2,0},{3,1},{4,2},{5,3},{6,4},{7,5},{8,6},{9,7},{10,... | collective-permute-start | bytes 196616 | tf_op jit(solution)/shard_map/ppermute | solution.py:215
  46.4 8.3 %collective-permute-start.15 = (f32[1024,256]{1,0:T(8,128)S(1)}, f32[1024,256]{1,0:T(8,128)S(1)}, u32[]{:S(2)}, u32[]{:S(2)}) collective-permute-start(f32[1024,256]{1,0:T(8,128)S(1)} %constant_dynamic-update-slice_fusion.own_ref), channel_id=1, source_target_pairs={{0,1},{1,0},{2,3},{3,2},{4,5},{5,4},{6,7},{7,6},{8,9},{9,8},{10,11... | collective-permute-start | bytes 3145736 | tf_op jit(solution)/shard_map/ppermute | solution.py:223
  104.3 11.5 %all-to-all-start.1 = ((f32[16,8,640]{2,1,0:T(8,128)}), f32[16,8,640]{2,1,0:T(8,128)S(1)}, u32[]{:S(2)}, u32[]{:S(2)}) async-start(f32[16,8,640]{2,1,0:T(8,128)} %broadcast_in_dim.10), calls=%async_computation.1 | async-start | bytes 655360 | tf_op jit(solution)/shard_map/all_to_all | solution.py:219
  117.3 41.6 %all-to-all-start.2 = ((f32[16,32,1024]{2,1,0:T(8,128)}), f32[16,32,1024]{2,1,0:T(8,128)S(1)}, u32[]{:S(2)}, u32[]{:S(2)}) async-start(f32[16,32,1024]{2,1,0:T(8,128)} %broadcast_in_dim.11), calls=%async_computation.2 | async-start | bytes 4194304 | tf_op jit(solution)/shard_map/all_to_all | solution.py:219
  121.1 4.4 %collective-permute-start.16 = (f32[16,8,640]{2,1,0:T(8,128)S(1)}, f32[16,8,640]{2,1,0:T(8,128)S(1)}, u32[]{:S(2)}, u32[]{:S(2)}) collective-permute-start(f32[16,8,640]{2,1,0:T(8,128)S(1)} %all-to-all-done.1.own_ref), channel_id=1, source_target_pairs={{0,1},{1,0},{2,3},{3,2},{4,5},{5,4},{6,7},{7,6},{8,9},{9,8},{10,11... | collective-permute-start | bytes 983048 | tf_op jit(solution)/shard_map/ppermute | solution.py:223

commit v2 on v1

--- a/solution.py
+++ b/solution.py
@@ -8,7 +8,7 @@
 BLOCK = 256
 TILE = 128
 NB = 4
-STRIP = 4
+STRIP = 8
 FULL = NB * TILE
 PEERS = 16
 DEPTH = 8
@@ -89,13 +89,18 @@
     return one_pass(a[0], b[0], dims) + (one_pass(a[0], b[1], dims) + one_pass(a[1], b[0], dims))
 
 
-def panel_kernel(matrix_ref, out_ref, sem):
-    copy = pltpu.make_async_copy(matrix_ref.at[:, 0, :], out_ref, sem)
-    copy.start()
-    copy.wait()
-
-
-def product_kernel(place, own_ref, other_ref, a0_ref, a1_ref, high_ref, low_ref, terms_ref, gram_ref):
+def panel_kernel(matrix_ref, *refs):
+    outs, sems = refs[:-1], refs[-1]
+    copies = [
+        pltpu.make_async_copy(matrix_ref.at[k * PIECE : (k + 1) * PIECE, 0, :], out, sems.at[k]) for k, out in enumerate(outs)
+    ]
+    for copy in copies:
+        copy.start()
+    for copy in copies:
+        copy.wait()
+
+
+def product_kernel(place, own_ref, other_ref, a_ref, high_ref, low_ref, terms_ref, gram_ref):
     start = pl.program_id(0) == 0
 
     @pl.when(start)
@@ -108,8 +113,8 @@
     panel = split(jnp.concatenate([jnp.where(first, own, other), jnp.where(first, other, own)], axis=1))
     high_ref[...], low_ref[...] = panel
     gram_ref[...] += three_pass(panel, panel, by_rows)
-    for l in range(a0_ref.shape[1]):
-        a = split(jnp.concatenate([a0_ref[:, l, :], a1_ref[:, l, :]], axis=0))
+    for l in range(a_ref.shape[1]):
+        a = split(a_ref[:, l, :])
         part = three_pass(panel, a, by_rows)
         for r in range(PEERS):
             terms_ref[r, :SHARE, l * BLOCK : (l + 1) * BLOCK] += part[r * SHARE : (r + 1) * SHARE]
@@ -138,33 +143,32 @@
         s_ref[j, i * TILE + top : i * TILE + top + 8, :] = jnp.where(first, own, other)
         s_ref[q, p * TILE + top : p * TILE + top + 8, :] = jnp.where(first, other, own)
 
-    @pl.loop(0, NB)
-    def _(j):
-        d = pl.multiple_of(j * TILE, TILE)
-        mj = invert_factor(s_ref[j, pl.ds(d, TILE), :])
-        mrow = mm(mj, t_ref[j], plain)
-        lanes = lax.broadcasted_iota(jnp.int32, (TILE, FULL), 1)
-        mrow = jnp.where(lanes // TILE == j, jnp.concatenate([mj] * NB, axis=1), mrow)
-        m_ref[pl.ds(d, TILE), :] = mrow
-        rows = lax.broadcasted_iota(jnp.int32, (FULL, TILE), 0)
-        low = jnp.where(rows >= d + TILE, mm(s_ref[j], mj, by_cols), 0.0)
-        for i in range(1, NB):
-
-            @pl.when(i > j)
-            def _():
-                part = low[i * TILE : (i + 1) * TILE]
-                s_ref[i] -= mm(low, part, by_cols)
-                t_ref[i] -= mm(part, mrow, plain)
+    def update(j, i, k):
+        s_ref[k, i * TILE : (i + 1) * TILE, :] -= mm(low[i], low[k], by_cols)
+
+    for j in range(NB):
+        d = j * TILE
+        mj = invert_factor(s_ref[j, d : d + TILE, :])
+        if j:
+            done = j - 1
+            for i in range(j, NB):
+                t_ref[i, :, :d] -= mm(low[i], m_ref[done * TILE : d, :d], plain)
+                for k in range(j, i + 1):
+                    if i > j:
+                        update(done, i, k)
+            m_ref[d : d + TILE, :d] = mm(mj, t_ref[j, :, :d], plain)
+        m_ref[d : d + TILE, d : d + TILE] = mj
+        if j + 1 < NB:
+            m_ref[d : d + TILE, d + TILE :] = jnp.zeros((TILE, FULL - d - TILE), jnp.float32)
+            column = mm(s_ref[j, d + TILE :, :], mj, by_cols)
+            low = {i: column[(i - j - 1) * TILE : (i - j) * TILE] for i in range(j + 1, NB)}
+            update(j, j + 1, j + 1)
 
     factor = split(m_ref[...])
     step = 2 * PIECE
-    for g in range(0, DEPTH, 2):
-        window = slice(g * PIECE, g * PIECE + step)
-        q = split(three_pass((high_ref[window], low_ref[window]), factor, by_cols))
-        for e in range(2):
-            spot = pl.ds(pl.multiple_of(lax.rem(place[0] + g + e, DEPTH) * PIECE, PIECE), PIECE)
-            qh_ref[spot, :] = q[0][e * PIECE : (e + 1) * PIECE]
-            ql_ref[spot, :] = q[1][e * PIECE : (e + 1) * PIECE]
+    for g in range(0, qh_ref.shape[0], step):
+        window = slice(g, g + step)
+        qh_ref[window], ql_ref[window] = split(three_pass((high_ref[window], low_ref[window]), factor, by_cols))
 
 
 def remainder_kernel(place, qh_ref, ql_ref, a_ref, m_ref, w_ref, coeff_ref, out_ref, ch_ref, cl_ref):
@@ -211,10 +215,6 @@
     return [pltpu.with_memory_space_constraint(x, pltpu.HBM) for x in arrays]
 
 
-def shift(x, axis, by):
-    return lax.ppermute(x, axis, [(i, (i + by) % PEERS) for i in range(PEERS)])
-
-
 def everywhere(share):
     return lax.all_to_all(jnp.broadcast_to(share, (PEERS,) + share.shape), "row", 0, 0)
 
@@ -224,16 +224,12 @@
 
 
 def share_panel(mine, z):
-    own = jnp.where(z == 0, mine[:PIECE], jnp.zeros((PIECE, BLOCK), jnp.float32))
+    own = jnp.where(z == 0, mine[0], jnp.zeros((PIECE, BLOCK), jnp.float32))
     for k in range(1, DEPTH):
-        own = own + lax.ppermute(mine[k * PIECE : (k + 1) * PIECE], "col", [(0, 2 * k), (1, 2 * k + 1)])
-    up, down = [own], [own]
-    for _ in range(DEPTH // 2 - 1):
-        up.append(shift(up[-1], "col", 2))
-        down.append(shift(down[-1], "col", -2))
-    half = PIECE // 2
-    far = [shift(up[-1][:half], "col", 2), shift(down[-1][half:], "col", -2)]
-    return jnp.concatenate(down + far + up[:0:-1], axis=0)
+        own = own + lax.ppermute(mine[k], "col", [(0, 2 * k), (1, 2 * k + 1)])
+    groups = [[2 * k + core for k in range(DEPTH)] for core in range(2)]
+    pieces = lax.all_to_all(jnp.broadcast_to(own, (DEPTH,) + own.shape), "col", 0, 0, axis_index_groups=groups)
+    return pieces.reshape(DEPTH * PIECE, BLOCK)
 
 
 def on_device(matrix):
@@ -245,11 +241,11 @@
     mine = pl.pallas_call(
         panel_kernel,
         in_specs=[pl.BlockSpec(memory_space=pl.ANY)],
-        out_specs=pl.BlockSpec(memory_space=pltpu.VMEM),
-        out_shape=f32(rows, width),
-        scratch_shapes=[pltpu.SemaphoreType.DMA],
+        out_specs=[pl.BlockSpec(memory_space=pltpu.VMEM)] * DEPTH,
+        out_shape=[f32(PIECE, width)] * DEPTH,
+        scratch_shapes=[pltpu.SemaphoreType.DMA((DEPTH,))],
         name="panel",
-    )(matrix)
+    )(*in_hbm(matrix))
     own = share_panel(mine, z)
     other = swap_cores(own)
 
@@ -257,20 +253,17 @@
     steps = rows // step
     own_spec = pl.BlockSpec((step, BLOCK), lambda g, place: (g, 0))
     panel_spec = pl.BlockSpec((step, FULL), lambda g, place: (g, 0))
+    a_spec = pl.BlockSpec((step, blocks, width), lambda g, place: (g, 0, 0))
     high, low, terms = call(
         product_kernel, "product", 20, (steps,),
-        [own_spec, own_spec]
-        + [
-            pl.BlockSpec((PIECE, blocks, width), lambda g, place, e=e: (lax.rem(place[0] + 2 * g + e, DEPTH), 0, 0))
-            for e in range(2)
-        ],
+        [own_spec, own_spec, a_spec],
         [panel_spec, panel_spec, whole(PEERS, SHARE + 8, blocks * width)],
         [bf16(rows, FULL), bf16(rows, FULL), f32(PEERS, SHARE + 8, blocks * width)],
         [pltpu.VMEM((FULL, FULL), jnp.float32)],
-    )(place, own, other, *in_hbm(matrix, matrix))
+    )(place, own, other, *in_hbm(matrix))
     total = jnp.sum(lax.all_to_all(terms, "row", 0, 0), axis=0)
+    sums = lax.all_gather(total[:SHARE], "row", tiled=True)
     gram = everywhere(total[SHARE:, : TILES * TILE])
-    sums = everywhere(total[:SHARE]).reshape(FULL, blocks * width)
 
     m, qh, ql = call(
         factor_kernel, "factor", 20, (1,),
@@ -280,7 +273,6 @@
         [pltpu.VMEM((NB, FULL, TILE), jnp.float32), pltpu.VMEM((NB, TILE, FULL), jnp.float32)],
     )(place, gram, swap_cores(gram), *in_hbm(high, low))
 
-    a_spec = pl.BlockSpec((step, blocks, width), lambda g, place: (g, 0, 0))
     return call(
         remainder_kernel, "remainder", 22, (steps,),
         [panel_spec, panel_spec, a_spec, whole(FULL, FULL), whole(FULL, blocks * width)],

time: 171 us -> 191 us (1.12)
  blocking collectives: 39.7 us -> 80.5 us
  starting transfers between devices: 42 us -> 22.4 us
  waiting for transfers between devices: 26.7 us -> 8.89 us
  between operations: 0.87 us -> 14.2 us
  Pallas kernels: 56.2 us -> 60.9 us
    all_to_all x0 -> x2, blocking collectives: none -> 40.8 us  [the longest x1 29.5 us: share_panel(): lax.all_to_all(jnp.broadcast_to(own, (DEPTH,) + own.shape), 'col', 0, 0,...]
    pallas_call x1, Pallas kernels: 9.02 us -> 19.7 us  [on_device(): call(product_kernel, 'product', 20, (steps,), [own_spec, own_spec, a_spec...]
    ppermute x15 -> x7, starting transfers between devices: 25.6 us -> 15.5 us  [share_panel(): own = own + lax.ppermute(mine[k], 'col', [(0, 2 * k), (1, 2 * k + 1)])]
    ppermute x15 -> x7, waiting for transfers between devices: 15.3 us -> 5.41 us  [share_panel(): own = own + lax.ppermute(mine[k], 'col', [(0, 2 * k), (1, 2 * k + 1)])]
    all_to_all x2 -> x0, waiting for transfers between devices: 7.9 us -> none  [everywhere(): lax.all_to_all(jnp.broadcast_to(share, (PEERS,) + share.shape), 'row', 0, 0)]
    all_to_all x2 -> x0, starting transfers between devices: 7.26 us -> none  [everywhere(): lax.all_to_all(jnp.broadcast_to(share, (PEERS,) + share.shape), 'row', 0, 0)]
    pallas_call x1, Pallas kernels: 33.5 us -> 27.3 us  [on_device(): call(factor_kernel, 'factor', 20, (1,), [whole(PEERS, 8, TILES * TILE)] *...]
    broadcast_in_dim x2 -> x1, local copies, waits for them, and re-layouts: 2.32 us -> 0.02 us  [everywhere(): jnp.broadcast_to(share, (PEERS,) + share.shape)]
  transfers between devices with their start and end apart: 19 -> 10, of which waited for: 11 -> 4; matrix products, arithmetic and copies ran while one was open for 0% -> 0% of each run, Pallas kernels for 20% -> 14%
where the time goes in v2:
time: 191 us; the launch traced here: 190 us
  blocking collectives  80.5 us (42%)
  Pallas kernels  60.9 us (32%)
  starting transfers between devices  22.4 us (12%)
  between operations  14.2 us (7%)
  waiting for transfers between devices  8.89 us (5%)
  local copies, waits for them, and re-layouts  2.35 us (1%)
    all_to_all x1, blocking collectives, on_device(): total = jnp.sum(lax.all_to_all(terms, 'row', 0, 0), axis=0)  39.7 us
    all_to_all x1, blocking collectives, share_panel(): lax.all_to_all(jnp.broadcast_to(own, (DEPTH,) + own.shape), 'col', 0, 0,...  29.5 us
    pallas_call x1, Pallas kernels, on_device(): call(factor_kernel, 'factor', 20, (1,), [whole(PEERS, 8, TILES * TILE)] *...  27.3 us
    pallas_call x1, Pallas kernels, on_device(): call(product_kernel, 'product', 20, (steps,), [own_spec, own_spec, a_spec...  19.7 us
    ppermute x7, starting transfers between devices, share_panel(): own = own + lax.ppermute(mine[k], 'col', [(0, 2 * k), (1, 2 * k + 1)])  15.5 us
    pallas_call x1, Pallas kernels, on_device(): call(remainder_kernel, 'remainder', 22, (steps,), [panel_spec, panel_spec...  11.5 us
    all_to_all x1, blocking collectives, everywhere(): lax.all_to_all(jnp.broadcast_to(share, (PEERS,) + share.shape), 'row', 0, 0)  11.4 us
    ppermute x2, starting transfers between devices, swap_cores(): return lax.ppermute(x, 'col', [(i, i ^ 1) for i in range(PEERS)])  6.81 us
  transfers between devices with their start and end apart: 10, of which 4 were waited for; matrix products, arithmetic and copies ran while one was open for 0% of the time, Pallas kernels for 14%

profile of v2, /device:TPU:1, one launch (start us, length us, event | category | flops | bytes accessed | tf_op | source)
XLA Modules:
  0.0 190.4 jit_solution(14710271044669395320)
XLA Ops:
  7.2 0.0 all-gather.2.cloned.1.call-start
  7.2 2.3 %panel.1 = (f32[128,256]{1,0:T(8,128)}, f32[128,256]{1,0:T(8,128)}, f32[128,256]{1,0:T(8,128)}, f32[128,256]{1,0:T(8,128)}, f32[128,256]{1,0:T(8,128)}, /*index=...) custom-call(f32[1024,4,256]{2,1,0:T(4,128)} %a_ref.3), custom_call_target="tpu_custom_call" | custom-call | tf_op jit(solution)/shard_map/panel/pallas_call | solution.py:241
  9.5 4.4 %collective-permute-start = (f32[128,256]{1,0:T(8,128)}, f32[128,256]{1,0:T(8,128)S(1)}, u32[]{:S(2)}, u32[]{:S(2)}) collective-permute-start(f32[128,256]{1,0:T(8,128)} %get-tuple-element.17), channel_id=1, source_target_pairs={{0,2},{1,3},{16,18},{17,19},{32,34},{33,35},{48,50},{49,51},{64,66... | collective-permute-start | bytes 393224 | tf_op jit(solution)/shard_map/ppermute | solution.py:229
  13.9 2.0 %collective-permute-start.1 = (f32[128,256]{1,0:T(8,128)}, f32[128,256]{1,0:T(8,128)S(1)}, u32[]{:S(2)}, u32[]{:S(2)}) collective-permute-start(f32[128,256]{1,0:T(8,128)} %get-tuple-element.18), channel_id=1, source_target_pairs={{0,4},{1,5},{16,20},{17,21},{32,36},{33,37},{48,52},{49,53},{64,68... | collective-permute-start | bytes 393224 | tf_op jit(solution)/shard_map/ppermute | solution.py:229
  16.0 2.0 %collective-permute-start.2 = (f32[128,256]{1,0:T(8,128)}, f32[128,256]{1,0:T(8,128)S(1)}, u32[]{:S(2)}, u32[]{:S(2)}) collective-permute-start(f32[128,256]{1,0:T(8,128)} %get-tuple-element.19), channel_id=1, source_target_pairs={{0,6},{1,7},{16,22},{17,23},{32,38},{33,39},{48,54},{49,55},{64,70... | collective-permute-start | bytes 393224 | tf_op jit(solution)/shard_map/ppermute | solution.py:229
  18.0 3.2 %collective-permute-start.3 = (f32[128,256]{1,0:T(8,128)}, f32[128,256]{1,0:T(8,128)S(1)}, u32[]{:S(2)}, u32[]{:S(2)}) collective-permute-start(f32[128,256]{1,0:T(8,128)} %get-tuple-element.20), channel_id=1, source_target_pairs={{0,8},{1,9},{16,24},{17,25},{32,40},{33,41},{48,56},{49,57},{64,72... | collective-permute-start | bytes 393224 | tf_op jit(solution)/shard_map/ppermute | solution.py:229
  21.2 1.3 collective-permute-start.4
  22.5 0.0 collective-permute-done
  22.5 1.3 collective-permute-start.5
  23.8 0.0 collective-permute-done.1
  23.9 1.3 collective-permute-start.6
  25.2 0.0 collective-permute-done.2
  25.2 0.0 collective-permute-done.3
  25.2 0.0 collective-permute-done.4
  25.2 2.6 %collective-permute-done.5 = f32[128,256]{1,0:T(8,128)S(1)} collective-permute-done((f32[128,256]{1,0:T(8,128)}, f32[128,256]{1,0:T(8,128)S(1)}, u32[]{:S(2)}, u32[]{:S(2)}) %collective-permute-start.5) | collective-permute-done | bytes 131104 | tf_op jit(solution)/shard_map/ppermute | solution.py:229
  27.8 2.8 %collective-permute-done.6 = f32[128,256]{1,0:T(8,128)S(1)} collective-permute-done((f32[128,256]{1,0:T(8,128)}, f32[128,256]{1,0:T(8,128)S(1)}, u32[]{:S(2)}, u32[]{:S(2)}) %collective-permute-start.6) | collective-permute-done | bytes 131104 | tf_op jit(solution)/shard_map/ppermute | solution.py:229
  30.6 1.0 add_add_fusion
  31.6 0.1 broadcast_in_dim.10
  31.7 29.5 %all_to_all.15 = f32[8,128,256]{2,1,0:T(8,128)S(1)} all-to-all(f32[8,128,256]{2,1,0:T(8,128)S(1)} %broadcast_in_dim.10), channel_id=1, replica_groups={{0,2,4,6,8,10,12,14},{1,3,5,7,9,11,13,15},{16,18,20,22,24,26,28,30},{17..., dimensions={0} | all-to-all | bytes 2097152 | tf_op jit(solution)/shard_map/all_to_all | solution.py:231
  61.1 3.7 %collective-permute-start.7 = (f32[1024,256]{1,0:T(8,128)S(1)}, f32[1024,256]{1,0:T(8,128)S(1)}, u32[]{:S(2)}, u32[]{:S(2)}) collective-permute-start(f32[1024,256]{1,0:T(8,128)S(1)} %bitcast.4), channel_id=1, source_target_pairs={{0,1},{1,0},{2,3},{3,2},{4,5},{5,4},{6,7},{7,6},{8,9},{9,8},{10,11... | collective-permute-start | bytes 3145736 | tf_op jit(solution)/shard_map/ppermute | solution.py:223
  64.8 0.1 pad_add_fusion.place
  64.9 2.2 %collective-permute-done.7.other_ref = f32[1024,256]{1,0:T(8,128)S(1)} collective-permute-done((f32[1024,256]{1,0:T(8,128)S(1)}, f32[1024,256]{1,0:T(8,128)S(1)}, u32[]{:S(2)}, u32[]{:S(2)}) %collective-permute-start.7) | collective-permute-done | bytes 1048608 | tf_op jit(solution)/shard_map/ppermute | solution.py:223
  67.1 19.7 %product.1 = (bf16[1024,512]{1,0:T(8,128)(2,1)}, bf16[1024,512]{1,0:T(8,128)(2,1)}, f32[16,40,1024]{2,1,0:T(8,128)S(1)}) custom-call(s32[3]{0:T(128)S(1)} %pad_add_fusion.place, f32[1024,256]{1,0:T(8,128)S(1)} %bitcast.5, f32[1024,256]{1,0:T(8,128)S(1)} %collective-permute-done.7.other_ref, f32[1024,4,256]{2,1,0:T(4,128)} %a_ref.3), custom_call_target="tpu_custom_call" | custom-call | tf_op jit(solution)/shard_map/product/pallas_call | solution.py:257
  86.9 39.7 %all_to_all.16 = f32[16,40,1024]{2,1,0:T(8,128)S(1)} all-to-all(f32[16,40,1024]{2,1,0:T(8,128)S(1)} %get-tuple-element.24), channel_id=1, replica_groups=mesh['row'=16,'col'=16] {'row'}, dimensions={0} | all-to-all | bytes 5242880 | tf_op jit(solution)/shard_map/all_to_all | solution.py:264
  126.6 0.2 reduce_sum.9
  126.7 0.7 slice.9
  127.4 0.0 all-gather.2.cloned.1.call-update
  127.4 11.4 %all_to_all.17.own_ref = f32[16,8,640]{2,1,0:T(8,128)S(1)} all-to-all(f32[16,8,640]{2,1,0:T(8,128)S(1)} %broadcast_in_dim.11), channel_id=1, replica_groups=mesh['row'=16,'col'=16] {'row'}, dimensions={0} | all-to-all | bytes 655360 | tf_op jit(solution)/shard_map/all_to_all | solution.py:219
  138.8 3.1 %collective-permute-start.8 = (f32[16,8,640]{2,1,0:T(8,128)S(1)}, f32[16,8,640]{2,1,0:T(8,128)S(1)}, u32[]{:S(2)}, u32[]{:S(2)}) collective-permute-start(f32[16,8,640]{2,1,0:T(8,128)S(1)} %all_to_all.17.own_ref), channel_id=1, source_target_pairs={{0,1},{1,0},{2,3},{3,2},{4,5},{5,4},{6,7},{7,6},{8,9},{9,8},{10,11... | collective-permute-start | bytes 983048 | tf_op jit(solution)/shard_map/ppermute | solution.py:223
  141.9 1.3 collective-permute-done.8.other_ref
  143.2 27.3 %factor.1 = (f32[512,512]{1,0:T(8,128)S(1)}, bf16[1024,512]{1,0:T(8,128)(2,1)}, bf16[1024,512]{1,0:T(8,128)(2,1)}) custom-call(s32[3]{0:T(128)S(1)} %pad_add_fusion.place, f32[16,8,640]{2,1,0:T(8,128)S(1)} %all_to_all.17.own_ref, f32[16,8,640]{2,1,0:T(8,128)S(1)} %collective-permute-done.8.other_ref, bf16[1024,512]{1,0:T(8,128)(2,1)} %get-tuple-element.25.high_ref, ...), custom_call_target="tpu_custom_call" | custom-call | tf_op jit(solution)/shard_map/factor/pallas_call | solution.py:268
  170.4 0.0 all-gather.2.cloned.1.call-done.w_ref
  170.4 0.0 copy-start
  170.4 1.6 copy-done
  172.0 11.5 %remainder.1 = (f32[512,4,256]{2,1,0:T(4,128)}, f32[1024,4,256]{2,1,0:T(4,128)}) custom-call(s32[3]{0:T(128)S(1)} %pad_add_fusion.place, bf16[1024,512]{1,0:T(8,128)(2,1)} %get-tuple-element.27.qh_ref, bf16[1024,512]{1,0:T(8,128)(2,1)} %get-tuple-element.28.ql_ref, f32[1024,4,256]{2,1,0:T(4,128)} %a_ref.3, f32[512,512]{1,0:T(8,128)S(1)} %get-tuple-element.29.m_ref, ...), custom_call_target="tpu_custom_call" | custom-call | tf_op jit(solution)/shard_map/remainder/pallas_call | solution.py:276
  (2 shorter events, 0.0 us)
Async XLA Ops:
  7.2 163.3 %all-gather.2.cloned.1.call-start = ((), (), s32[]{:S(2)}) async-start(), calls=%async_computation.3 | async-start | bytes 2228224 | tf_op jit(solution)/shard_map/all_gather | solution.py:265
  9.5 13.0 %collective-permute-start = (f32[128,256]{1,0:T(8,128)}, f32[128,256]{1,0:T(8,128)S(1)}, u32[]{:S(2)}, u32[]{:S(2)}) collective-permute-start(f32[128,256]{1,0:T(8,128)} %get-tuple-element.17), channel_id=1, source_target_pairs={{0,2},{1,3},{16,18},{17,19},{32,34},{33,35},{48,50},{49,51},{64,66... | collective-permute-start | bytes 393224 | tf_op jit(solution)/shard_map/ppermute | solution.py:229
  13.9 9.9 %collective-permute-start.1 = (f32[128,256]{1,0:T(8,128)}, f32[128,256]{1,0:T(8,128)S(1)}, u32[]{:S(2)}, u32[]{:S(2)}) collective-permute-start(f32[128,256]{1,0:T(8,128)} %get-tuple-element.18), channel_id=1, source_target_pairs={{0,4},{1,5},{16,20},{17,21},{32,36},{33,37},{48,52},{49,53},{64,68... | collective-permute-start | bytes 393224 | tf_op jit(solution)/shard_map/ppermute | solution.py:229
  16.0 9.2 %collective-permute-start.2 = (f32[128,256]{1,0:T(8,128)}, f32[128,256]{1,0:T(8,128)S(1)}, u32[]{:S(2)}, u32[]{:S(2)}) collective-permute-start(f32[128,256]{1,0:T(8,128)} %get-tuple-element.19), channel_id=1, source_target_pairs={{0,6},{1,7},{16,22},{17,23},{32,38},{33,39},{48,54},{49,55},{64,70... | collective-permute-start | bytes 393224 | tf_op jit(solution)/shard_map/ppermute | solution.py:229
  18.0 7.2 %collective-permute-start.3 = (f32[128,256]{1,0:T(8,128)}, f32[128,256]{1,0:T(8,128)S(1)}, u32[]{:S(2)}, u32[]{:S(2)}) collective-permute-start(f32[128,256]{1,0:T(8,128)} %get-tuple-element.20), channel_id=1, source_target_pairs={{0,8},{1,9},{16,24},{17,25},{32,40},{33,41},{48,56},{49,57},{64,72... | collective-permute-start | bytes 393224 | tf_op jit(solution)/shard_map/ppermute | solution.py:229
  21.2 4.0 %collective-permute-start.4 = (f32[128,256]{1,0:T(8,128)}, f32[128,256]{1,0:T(8,128)S(1)}, u32[]{:S(2)}, u32[]{:S(2)}) collective-permute-start(f32[128,256]{1,0:T(8,128)} %get-tuple-element.21), channel_id=1, source_target_pairs={{0,10},{1,11},{16,26},{17,27},{32,42},{33,43},{48,58},{49,59},{64,... | collective-permute-start | bytes 393224 | tf_op jit(solution)/shard_map/ppermute | solution.py:229
  22.5 5.3 %collective-permute-start.5 = (f32[128,256]{1,0:T(8,128)}, f32[128,256]{1,0:T(8,128)S(1)}, u32[]{:S(2)}, u32[]{:S(2)}) collective-permute-start(f32[128,256]{1,0:T(8,128)} %get-tuple-element.22), channel_id=1, source_target_pairs={{0,12},{1,13},{16,28},{17,29},{32,44},{33,45},{48,60},{49,61},{64,... | collective-permute-start | bytes 393224 | tf_op jit(solution)/shard_map/ppermute | solution.py:229
  23.9 6.7 %collective-permute-start.6 = (f32[128,256]{1,0:T(8,128)}, f32[128,256]{1,0:T(8,128)S(1)}, u32[]{:S(2)}, u32[]{:S(2)}) collective-permute-start(f32[128,256]{1,0:T(8,128)} %get-tuple-element.23), channel_id=1, source_target_pairs={{0,14},{1,15},{16,30},{17,31},{32,46},{33,47},{48,62},{49,63},{64,... | collective-permute-start | bytes 393224 | tf_op jit(solution)/shard_map/ppermute | solution.py:229
  61.1 6.0 %collective-permute-start.7 = (f32[1024,256]{1,0:T(8,128)S(1)}, f32[1024,256]{1,0:T(8,128)S(1)}, u32[]{:S(2)}, u32[]{:S(2)}) collective-permute-start(f32[1024,256]{1,0:T(8,128)S(1)} %bitcast.4), channel_id=1, source_target_pairs={{0,1},{1,0},{2,3},{3,2},{4,5},{5,4},{6,7},{7,6},{8,9},{9,8},{10,11... | collective-permute-start | bytes 3145736 | tf_op jit(solution)/shard_map/ppermute | solution.py:223
  138.8 4.4 %collective-permute-start.8 = (f32[16,8,640]{2,1,0:T(8,128)S(1)}, f32[16,8,640]{2,1,0:T(8,128)S(1)}, u32[]{:S(2)}, u32[]{:S(2)}) collective-permute-start(f32[16,8,640]{2,1,0:T(8,128)S(1)} %all_to_all.17.own_ref), channel_id=1, source_target_pairs={{0,1},{1,0},{2,3},{3,2},{4,5},{5,4},{6,7},{7,6},{8,9},{9,8},{10,11... | collective-permute-start | bytes 983048 | tf_op jit(solution)/shard_map/ppermute | solution.py:223
  170.4 1.6 copy-start
Sparse Core Ops, SparseCore 0:
  127.5 42.6 all-gather.1

commit v3 on v2

--- a/solution.py
+++ b/solution.py
@@ -100,7 +100,7 @@
         copy.wait()
 
 
-def product_kernel(place, own_ref, other_ref, a_ref, high_ref, low_ref, terms_ref, gram_ref):
+def product_kernel(place, own_ref, other_ref, a0_ref, a1_ref, high_ref, low_ref, terms_ref, gram_ref):
     start = pl.program_id(0) == 0
 
     @pl.when(start)
@@ -113,8 +113,8 @@
     panel = split(jnp.concatenate([jnp.where(first, own, other), jnp.where(first, other, own)], axis=1))
     high_ref[...], low_ref[...] = panel
     gram_ref[...] += three_pass(panel, panel, by_rows)
-    for l in range(a_ref.shape[1]):
-        a = split(a_ref[:, l, :])
+    for l in range(a0_ref.shape[1]):
+        a = split(jnp.concatenate([a0_ref[:, l, :], a1_ref[:, l, :]], axis=0))
         part = three_pass(panel, a, by_rows)
         for r in range(PEERS):
             terms_ref[r, :SHARE, l * BLOCK : (l + 1) * BLOCK] += part[r * SHARE : (r + 1) * SHARE]
@@ -166,9 +166,13 @@
 
     factor = split(m_ref[...])
     step = 2 * PIECE
-    for g in range(0, qh_ref.shape[0], step):
-        window = slice(g, g + step)
-        qh_ref[window], ql_ref[window] = split(three_pass((high_ref[window], low_ref[window]), factor, by_cols))
+    for g in range(0, DEPTH, 2):
+        window = slice(g * PIECE, g * PIECE + step)
+        q = split(three_pass((high_ref[window], low_ref[window]), factor, by_cols))
+        for e in range(2):
+            spot = pl.ds(pl.multiple_of(lax.rem(place[0] + g + e, DEPTH) * PIECE, PIECE), PIECE)
+            qh_ref[spot, :] = q[0][e * PIECE : (e + 1) * PIECE]
+            ql_ref[spot, :] = q[1][e * PIECE : (e + 1) * PIECE]
 
 
 def remainder_kernel(place, qh_ref, ql_ref, a_ref, m_ref, w_ref, coeff_ref, out_ref, ch_ref, cl_ref):
@@ -215,6 +219,10 @@
     return [pltpu.with_memory_space_constraint(x, pltpu.HBM) for x in arrays]
 
 
+def shift(x, axis, by):
+    return lax.ppermute(x, axis, [(i, (i + by) % PEERS) for i in range(PEERS)])
+
+
 def everywhere(share):
     return lax.all_to_all(jnp.broadcast_to(share, (PEERS,) + share.shape), "row", 0, 0)
 
@@ -227,9 +235,13 @@
     own = jnp.where(z == 0, mine[0], jnp.zeros((PIECE, BLOCK), jnp.float32))
     for k in range(1, DEPTH):
         own = own + lax.ppermute(mine[k], "col", [(0, 2 * k), (1, 2 * k + 1)])
-    groups = [[2 * k + core for k in range(DEPTH)] for core in range(2)]
-    pieces = lax.all_to_all(jnp.broadcast_to(own, (DEPTH,) + own.shape), "col", 0, 0, axis_index_groups=groups)
-    return pieces.reshape(DEPTH * PIECE, BLOCK)
+    up, down = [own], [own]
+    for _ in range(DEPTH // 2 - 1):
+        up.append(shift(up[-1], "col", 2))
+        down.append(shift(down[-1], "col", -2))
+    half = PIECE // 2
+    far = [shift(up[-1][:half], "col", 2), shift(down[-1][half:], "col", -2)]
+    return jnp.concatenate(down + far + up[:0:-1], axis=0)
 
 
 def on_device(matrix):
@@ -253,17 +265,20 @@
     steps = rows // step
     own_spec = pl.BlockSpec((step, BLOCK), lambda g, place: (g, 0))
     panel_spec = pl.BlockSpec((step, FULL), lambda g, place: (g, 0))
-    a_spec = pl.BlockSpec((step, blocks, width), lambda g, place: (g, 0, 0))
     high, low, terms = call(
         product_kernel, "product", 20, (steps,),
-        [own_spec, own_spec, a_spec],
+        [own_spec, own_spec]
+        + [
+            pl.BlockSpec((PIECE, blocks, width), lambda g, place, e=e: (lax.rem(place[0] + 2 * g + e, DEPTH), 0, 0))
+            for e in range(2)
+        ],
         [panel_spec, panel_spec, whole(PEERS, SHARE + 8, blocks * width)],
         [bf16(rows, FULL), bf16(rows, FULL), f32(PEERS, SHARE + 8, blocks * width)],
         [pltpu.VMEM((FULL, FULL), jnp.float32)],
-    )(place, own, other, *in_hbm(matrix))
+    )(place, own, other, *in_hbm(matrix, matrix))
     total = jnp.sum(lax.all_to_all(terms, "row", 0, 0), axis=0)
-    sums = lax.all_gather(total[:SHARE], "row", tiled=True)
     gram = everywhere(total[SHARE:, : TILES * TILE])
+    sums = everywhere(total[:SHARE]).reshape(FULL, blocks * width)
 
     m, qh, ql = call(
         factor_kernel, "factor", 20, (1,),
@@ -273,6 +288,7 @@
         [pltpu.VMEM((NB, FULL, TILE), jnp.float32), pltpu.VMEM((NB, TILE, FULL), jnp.float32)],
     )(place, gram, swap_cores(gram), *in_hbm(high, low))
 
+    a_spec = pl.BlockSpec((step, blocks, width), lambda g, place: (g, 0, 0))
     return call(
         remainder_kernel, "remainder", 22, (steps,),
         [panel_spec, panel_spec, a_spec, whole(FULL, FULL), whole(FULL, blocks * width)],

time: 191 us -> 164 us (0.86)
  blocking collectives: 80.5 us -> 39.7 us
  starting transfers between devices: 22.4 us -> 42.7 us
  waiting for transfers between devices: 8.89 us -> 26.3 us
  between operations: 14.2 us -> 0.87 us
  Pallas kernels: 60.9 us -> 50.2 us
    all_to_all x2 -> x0, blocking collectives: 40.8 us -> none  [the longest x1 29.5 us: share_panel(): lax.all_to_all(jnp.broadcast_to(own, (DEPTH,) + own.shape), 'col', 0, 0,...]
    ppermute x0 -> x8, starting transfers between devices: none -> 10.8 us  [shift(): return lax.ppermute(x, axis, [(i, (i + by) % PEERS) for i in range(PEERS)])]
    pallas_call x1, Pallas kernels: 19.7 us -> 9.02 us  [on_device(): call(product_kernel, 'product', 20, (steps,), [own_spec, own_spec] + [pl....]
    ppermute x0 -> x8, waiting for transfers between devices: none -> 9.53 us  [shift(): return lax.ppermute(x, axis, [(i, (i + by) % PEERS) for i in range(PEERS)])]
    all_to_all x0 -> x2, waiting for transfers between devices: none -> 7.9 us  [everywhere(): lax.all_to_all(jnp.broadcast_to(share, (PEERS,) + share.shape), 'row', 0, 0)]
    all_to_all x0 -> x2, starting transfers between devices: none -> 7.26 us  [everywhere(): lax.all_to_all(jnp.broadcast_to(share, (PEERS,) + share.shape), 'row', 0, 0)]
    broadcast_in_dim x1 -> x2, local copies, waits for them, and re-layouts: 0.02 us -> 2.32 us  [everywhere(): jnp.broadcast_to(share, (PEERS,) + share.shape)]
    ppermute x2, starting transfers between devices: 6.81 us -> 9.1 us  [swap_cores(): return lax.ppermute(x, 'col', [(i, i ^ 1) for i in range(PEERS)])]
  transfers between devices with their start and end apart: 10 -> 19, of which waited for: 4 -> 9; matrix products, arithmetic and copies ran while one was open for 0% -> 0% of each run, Pallas kernels for 14% -> 17%
where the time goes in v3:
time: 164 us; the launch traced here: 163 us
  Pallas kernels  50.2 us (31%)
  starting transfers between devices  42.7 us (26%)
  blocking collectives  39.7 us (24%)
  waiting for transfers between devices  26.3 us (16%)
  local copies, waits for them, and re-layouts  2.42 us (1%)
    all_to_all x1, blocking collectives, on_device(): total = jnp.sum(lax.all_to_all(terms, 'row', 0, 0), axis=0)  39.7 us
    pallas_call x1, Pallas kernels, on_device(): call(factor_kernel, 'factor', 20, (1,), [whole(PEERS, 8, TILES * TILE)] *...  27.3 us
    ppermute x7, starting transfers between devices, share_panel(): own = own + lax.ppermute(mine[k], 'col', [(0, 2 * k), (1, 2 * k + 1)])  15.5 us
    pallas_call x1, Pallas kernels, on_device(): call(remainder_kernel, 'remainder', 22, (steps,), [panel_spec, panel_spec...  11.5 us
    ppermute x8, starting transfers between devices, shift(): return lax.ppermute(x, axis, [(i, (i + by) % PEERS) for i in range(PEERS)])  10.8 us
    ppermute x8, waiting for transfers between devices, shift(): return lax.ppermute(x, axis, [(i, (i + by) % PEERS) for i in range(PEERS)])  9.53 us
    ppermute x2, starting transfers between devices, swap_cores(): return lax.ppermute(x, 'col', [(i, i ^ 1) for i in range(PEERS)])  9.1 us
    pallas_call x1, Pallas kernels, on_device(): call(product_kernel, 'product', 20, (steps,), [own_spec, own_spec] + [pl....  9.02 us
  transfers between devices with their start and end apart: 19, of which 9 were waited for; matrix products, arithmetic and copies ran while one was open for 0% of the time, Pallas kernels for 17%

profile of v3, /device:TPU:1, one launch (start us, length us, event | category | flops | bytes accessed | tf_op | source)
XLA Modules:
  0.0 163.5 jit_solution(1691909878862352399)
XLA Ops:
  0.6 2.3 %panel.1 = (f32[128,256]{1,0:T(8,128)}, f32[128,256]{1,0:T(8,128)}, f32[128,256]{1,0:T(8,128)}, f32[128,256]{1,0:T(8,128)}, f32[128,256]{1,0:T(8,128)}, /*index=...) custom-call(f32[1024,4,256]{2,1,0:T(4,128)} %a_ref.1), custom_call_target="tpu_custom_call" | custom-call | tf_op jit(solution)/shard_map/panel/pallas_call | solution.py:253
  3.0 4.4 %collective-permute-start = (f32[128,256]{1,0:T(8,128)}, f32[128,256]{1,0:T(8,128)S(1)}, u32[]{:S(2)}, u32[]{:S(2)}) collective-permute-start(f32[128,256]{1,0:T(8,128)} %get-tuple-element.17), channel_id=1, source_target_pairs={{0,2},{1,3},{16,18},{17,19},{32,34},{33,35},{48,50},{49,51},{64,66... | collective-permute-start | bytes 393224 | tf_op jit(solution)/shard_map/ppermute | solution.py:237
  7.4 2.0 %collective-permute-start.1 = (f32[128,256]{1,0:T(8,128)}, f32[128,256]{1,0:T(8,128)S(1)}, u32[]{:S(2)}, u32[]{:S(2)}) collective-permute-start(f32[128,256]{1,0:T(8,128)} %get-tuple-element.18), channel_id=1, source_target_pairs={{0,4},{1,5},{16,20},{17,21},{32,36},{33,37},{48,52},{49,53},{64,68... | collective-permute-start | bytes 393224 | tf_op jit(solution)/shard_map/ppermute | solution.py:237
  9.4 2.0 %collective-permute-start.2 = (f32[128,256]{1,0:T(8,128)}, f32[128,256]{1,0:T(8,128)S(1)}, u32[]{:S(2)}, u32[]{:S(2)}) collective-permute-start(f32[128,256]{1,0:T(8,128)} %get-tuple-element.19), channel_id=1, source_target_pairs={{0,6},{1,7},{16,22},{17,23},{32,38},{33,39},{48,54},{49,55},{64,70... | collective-permute-start | bytes 393224 | tf_op jit(solution)/shard_map/ppermute | solution.py:237
  11.4 3.2 %collective-permute-start.3 = (f32[128,256]{1,0:T(8,128)}, f32[128,256]{1,0:T(8,128)S(1)}, u32[]{:S(2)}, u32[]{:S(2)}) collective-permute-start(f32[128,256]{1,0:T(8,128)} %get-tuple-element.20), channel_id=1, source_target_pairs={{0,8},{1,9},{16,24},{17,25},{32,40},{33,41},{48,56},{49,57},{64,72... | collective-permute-start | bytes 393224 | tf_op jit(solution)/shard_map/ppermute | solution.py:237
  14.7 1.3 collective-permute-start.4
  16.0 0.0 collective-permute-done
  16.0 1.3 collective-permute-start.5
  17.3 0.0 collective-permute-done.1
  17.3 1.3 collective-permute-start.6
  18.6 0.0 collective-permute-done.2
  18.6 0.0 collective-permute-done.3
  18.6 0.0 collective-permute-done.4
  18.6 2.6 %collective-permute-done.5 = f32[128,256]{1,0:T(8,128)S(1)} collective-permute-done((f32[128,256]{1,0:T(8,128)}, f32[128,256]{1,0:T(8,128)S(1)}, u32[]{:S(2)}, u32[]{:S(2)}) %collective-permute-start.5) | collective-permute-done | bytes 131104 | tf_op jit(solution)/shard_map/ppermute | solution.py:237
  21.2 2.8 %collective-permute-done.6 = f32[128,256]{1,0:T(8,128)S(1)} collective-permute-done((f32[128,256]{1,0:T(8,128)}, f32[128,256]{1,0:T(8,128)S(1)}, u32[]{:S(2)}, u32[]{:S(2)}) %collective-permute-start.6) | collective-permute-done | bytes 131104 | tf_op jit(solution)/shard_map/ppermute | solution.py:237
  24.0 1.0 constant_dynamic-update-slice_fusion.8
  25.0 0.1 collective-permute-start.10
  25.1 2.7 %collective-permute-start.7 = (f32[128,256]{1,0:T(8,128)S(1)}, f32[128,256]{1,0:T(8,128)S(1)}, u32[]{:S(2)}, u32[]{:S(2)}) collective-permute-start(f32[128,256]{1,0:T(8,128)S(1)} %get-tuple-element.31), channel_id=1, source_target_pairs={{0,14},{1,15},{2,0},{3,1},{4,2},{5,3},{6,4},{7,5},{8,6},{9,7},{10,... | collective-permute-start | bytes 393224 | tf_op jit(solution)/shard_map/ppermute | solution.py:223
  27.8 2.4 %collective-permute-done.10 = f32[128,256]{1,0:T(8,128)S(1)} collective-permute-done((f32[128,256]{1,0:T(8,128)S(1)}, f32[128,256]{1,0:T(8,128)S(1)}, u32[]{:S(2)}, u32[]{:S(2)}) %collective-permute-start.10) | collective-permute-done | bytes 131104 | tf_op jit(solution)/shard_map/ppermute | solution.py:223
  30.1 0.0 collective-permute-start.11
  30.1 0.0 collective-permute-done.7
  30.1 2.7 %collective-permute-start.8 = (f32[128,256]{1,0:T(8,128)S(1)}, f32[128,256]{1,0:T(8,128)S(1)}, u32[]{:S(2)}, u32[]{:S(2)}) collective-permute-start(f32[128,256]{1,0:T(8,128)S(1)} %collective-permute-done.7), channel_id=1, source_target_pairs={{0,14},{1,15},{2,0},{3,1},{4,2},{5,3},{6,4},{7,5},{8,6},{9,7},{10,... | collective-permute-start | bytes 393224 | tf_op jit(solution)/shard_map/ppermute | solution.py:223
  32.8 2.3 %collective-permute-done.11 = f32[128,256]{1,0:T(8,128)S(1)} collective-permute-done((f32[128,256]{1,0:T(8,128)S(1)}, f32[128,256]{1,0:T(8,128)S(1)}, u32[]{:S(2)}, u32[]{:S(2)}) %collective-permute-start.11) | collective-permute-done | bytes 131104 | tf_op jit(solution)/shard_map/ppermute | solution.py:223
  35.1 0.0 collective-permute-start.12
  35.1 0.0 collective-permute-done.8
  35.2 2.7 %collective-permute-start.9 = (f32[128,256]{1,0:T(8,128)S(1)}, f32[128,256]{1,0:T(8,128)S(1)}, u32[]{:S(2)}, u32[]{:S(2)}) collective-permute-start(f32[128,256]{1,0:T(8,128)S(1)} %collective-permute-done.8), channel_id=1, source_target_pairs={{0,14},{1,15},{2,0},{3,1},{4,2},{5,3},{6,4},{7,5},{8,6},{9,7},{10,... | collective-permute-start | bytes 393224 | tf_op jit(solution)/shard_map/ppermute | solution.py:223
  37.9 2.3 %collective-permute-done.12 = f32[128,256]{1,0:T(8,128)S(1)} collective-permute-done((f32[128,256]{1,0:T(8,128)S(1)}, f32[128,256]{1,0:T(8,128)S(1)}, u32[]{:S(2)}, u32[]{:S(2)}) %collective-permute-start.12) | collective-permute-done | bytes 131104 | tf_op jit(solution)/shard_map/ppermute | solution.py:223
  40.2 0.0 collective-permute-start.13
  40.2 0.0 collective-permute-done.9
  40.2 2.7 %collective-permute-start.14 = (f32[64,256]{1,0:T(8,128)S(1)}, f32[64,256]{1,0:T(8,128)S(1)}, u32[]{:S(2)}, u32[]{:S(2)}) collective-permute-start(f32[64,256]{1,0:T(8,128)S(1)} %slice.17), channel_id=1, source_target_pairs={{0,14},{1,15},{2,0},{3,1},{4,2},{5,3},{6,4},{7,5},{8,6},{9,7},{10,... | collective-permute-start | bytes 196616 | tf_op jit(solution)/shard_map/ppermute | solution.py:223
  43.0 2.5 %collective-permute-done.13 = f32[64,256]{1,0:T(8,128)S(1)} collective-permute-done((f32[64,256]{1,0:T(8,128)S(1)}, f32[64,256]{1,0:T(8,128)S(1)}, u32[]{:S(2)}, u32[]{:S(2)}) %collective-permute-start.13) | collective-permute-done | bytes 65568 | tf_op jit(solution)/shard_map/ppermute | solution.py:223
  45.5 0.0 collective-permute-done.14
  45.6 6.0 %collective-permute-start.15 = (f32[1024,256]{1,0:T(8,128)S(1)}, f32[1024,256]{1,0:T(8,128)S(1)}, u32[]{:S(2)}, u32[]{:S(2)}) collective-permute-start(f32[1024,256]{1,0:T(8,128)S(1)} %constant_dynamic-update-slice_fusion.own_ref), channel_id=1, source_target_pairs={{0,1},{1,0},{2,3},{3,2},{4,5},{5,4},{6,7},{7,6},{8,9},{9,8},{10,11... | collective-permute-start | bytes 3145736 | tf_op jit(solution)/shard_map/ppermute | solution.py:231
  51.5 0.1 pad_add_fusion.place
  51.6 2.2 %collective-permute-done.15.other_ref = f32[1024,256]{1,0:T(8,128)S(1)} collective-permute-done((f32[1024,256]{1,0:T(8,128)S(1)}, f32[1024,256]{1,0:T(8,128)S(1)}, u32[]{:S(2)}, u32[]{:S(2)}) %collective-permute-start.15) | collective-permute-done | bytes 1048608 | tf_op jit(solution)/shard_map/ppermute | solution.py:231
  53.8 9.0 %product.1 = (bf16[1024,512]{1,0:T(8,128)(2,1)}, bf16[1024,512]{1,0:T(8,128)(2,1)}, f32[16,40,1024]{2,1,0:T(8,128)S(1)}) custom-call(s32[3]{0:T(128)S(1)} %pad_add_fusion.place, f32[1024,256]{1,0:T(8,128)S(1)} %constant_dynamic-update-slice_fusion.own_ref, f32[1024,256]{1,0:T(8,128)S(1)} %collective-permute-done.15.other_ref, f32[1024,4,256]{2,1,0:T(4,128)} %a_ref.1, ...), custom_call_target="tpu_custom_call" | custom-call | tf_op jit(solution)/shard_map/product/pallas_call | solution.py:268
  62.8 39.7 %all_to_all.15 = f32[16,40,1024]{2,1,0:T(8,128)S(1)} all-to-all(f32[16,40,1024]{2,1,0:T(8,128)S(1)} %get-tuple-element.24), channel_id=1, replica_groups=mesh['row'=16,'col'=16] {'row'}, dimensions={0} | all-to-all | bytes 5242880 | tf_op jit(solution)/shard_map/all_to_all | solution.py:279
  102.6 0.2 reduce_sum.9
  102.7 0.7 broadcast_in_dim.10
  103.5 3.5 %all-to-all-start.1 = ((f32[16,8,640]{2,1,0:T(8,128)}), f32[16,8,640]{2,1,0:T(8,128)S(1)}, u32[]{:S(2)}, u32[]{:S(2)}) async-start(f32[16,8,640]{2,1,0:T(8,128)} %broadcast_in_dim.10), calls=%async_computation.1 | async-start | bytes 655360 | tf_op jit(solution)/shard_map/all_to_all | solution.py:227
  107.1 7.9 %all-to-all-done.1.own_ref = f32[16,8,640]{2,1,0:T(8,128)S(1)} async-done(((f32[16,8,640]{2,1,0:T(8,128)}), f32[16,8,640]{2,1,0:T(8,128)S(1)}, u32[]{:S(2)}, u32[]{:S(2)}) %all-to-all-start.1) | async-done | bytes 327712 | tf_op jit(solution)/shard_map/all_to_all | solution.py:227
  114.9 1.6 broadcast_in_dim.11
  116.5 3.7 %all-to-all-start.2 = ((f32[16,32,1024]{2,1,0:T(8,128)}), f32[16,32,1024]{2,1,0:T(8,128)S(1)}, u32[]{:S(2)}, u32[]{:S(2)}) async-start(f32[16,32,1024]{2,1,0:T(8,128)} %broadcast_in_dim.11), calls=%async_computation.2 | async-start | bytes 4194304 | tf_op jit(solution)/shard_map/all_to_all | solution.py:227
  120.3 3.1 %collective-permute-start.16 = (f32[16,8,640]{2,1,0:T(8,128)S(1)}, f32[16,8,640]{2,1,0:T(8,128)S(1)}, u32[]{:S(2)}, u32[]{:S(2)}) collective-permute-start(f32[16,8,640]{2,1,0:T(8,128)S(1)} %all-to-all-done.1.own_ref), channel_id=1, source_target_pairs={{0,1},{1,0},{2,3},{3,2},{4,5},{5,4},{6,7},{7,6},{8,9},{9,8},{10,11... | collective-permute-start | bytes 983048 | tf_op jit(solution)/shard_map/ppermute | solution.py:231
  123.4 1.3 collective-permute-done.16.other_ref
  124.6 27.3 %factor.1 = (f32[512,512]{1,0:T(8,128)S(1)}, bf16[1024,512]{1,0:T(8,128)(2,1)}, bf16[1024,512]{1,0:T(8,128)(2,1)}) custom-call(s32[3]{0:T(128)S(1)} %pad_add_fusion.place, f32[16,8,640]{2,1,0:T(8,128)S(1)} %all-to-all-done.1.own_ref, f32[16,8,640]{2,1,0:T(8,128)S(1)} %collective-permute-done.16.other_ref, bf16[1024,512]{1,0:T(8,128)(2,1)} %get-tuple-element.25.high_ref, ...), custom_call_target="tpu_custom_call" | custom-call | tf_op jit(solution)/shard_map/factor/pallas_call | solution.py:283
  151.9 0.0 all-to-all-done.2
  151.9 11.5 %remainder.1 = (f32[512,4,256]{2,1,0:T(4,128)}, f32[1024,4,256]{2,1,0:T(4,128)}) custom-call(s32[3]{0:T(128)S(1)} %pad_add_fusion.place, bf16[1024,512]{1,0:T(8,128)(2,1)} %get-tuple-element.27.qh_ref, bf16[1024,512]{1,0:T(8,128)(2,1)} %get-tuple-element.28.ql_ref, f32[1024,4,256]{2,1,0:T(4,128)} %a_ref.1, f32[512,512]{1,0:T(8,128)S(1)} %get-tuple-element.29.m_ref, ...), custom_call_target="tpu_custom_call" | custom-call | tf_op jit(solution)/shard_map/remainder/pallas_call | solution.py:292
  (12 shorter events, 0.1 us)
Async XLA Ops:
  3.0 13.0 %collective-permute-start = (f32[128,256]{1,0:T(8,128)}, f32[128,256]{1,0:T(8,128)S(1)}, u32[]{:S(2)}, u32[]{:S(2)}) collective-permute-start(f32[128,256]{1,0:T(8,128)} %get-tuple-element.17), channel_id=1, source_target_pairs={{0,2},{1,3},{16,18},{17,19},{32,34},{33,35},{48,50},{49,51},{64,66... | collective-permute-start | bytes 393224 | tf_op jit(solution)/shard_map/ppermute | solution.py:237
  7.4 9.9 %collective-permute-start.1 = (f32[128,256]{1,0:T(8,128)}, f32[128,256]{1,0:T(8,128)S(1)}, u32[]{:S(2)}, u32[]{:S(2)}) collective-permute-start(f32[128,256]{1,0:T(8,128)} %get-tuple-element.18), channel_id=1, source_target_pairs={{0,4},{1,5},{16,20},{17,21},{32,36},{33,37},{48,52},{49,53},{64,68... | collective-permute-start | bytes 393224 | tf_op jit(solution)/shard_map/ppermute | solution.py:237
  9.4 9.2 %collective-permute-start.2 = (f32[128,256]{1,0:T(8,128)}, f32[128,256]{1,0:T(8,128)S(1)}, u32[]{:S(2)}, u32[]{:S(2)}) collective-permute-start(f32[128,256]{1,0:T(8,128)} %get-tuple-element.19), channel_id=1, source_target_pairs={{0,6},{1,7},{16,22},{17,23},{32,38},{33,39},{48,54},{49,55},{64,70... | collective-permute-start | bytes 393224 | tf_op jit(solution)/shard_map/ppermute | solution.py:237
  11.4 7.2 %collective-permute-start.3 = (f32[128,256]{1,0:T(8,128)}, f32[128,256]{1,0:T(8,128)S(1)}, u32[]{:S(2)}, u32[]{:S(2)}) collective-permute-start(f32[128,256]{1,0:T(8,128)} %get-tuple-element.20), channel_id=1, source_target_pairs={{0,8},{1,9},{16,24},{17,25},{32,40},{33,41},{48,56},{49,57},{64,72... | collective-permute-start | bytes 393224 | tf_op jit(solution)/shard_map/ppermute | solution.py:237
  14.7 4.0 %collective-permute-start.4 = (f32[128,256]{1,0:T(8,128)}, f32[128,256]{1,0:T(8,128)S(1)}, u32[]{:S(2)}, u32[]{:S(2)}) collective-permute-start(f32[128,256]{1,0:T(8,128)} %get-tuple-element.21), channel_id=1, source_target_pairs={{0,10},{1,11},{16,26},{17,27},{32,42},{33,43},{48,58},{49,59},{64,... | collective-permute-start | bytes 393224 | tf_op jit(solution)/shard_map/ppermute | solution.py:237
  16.0 5.3 %collective-permute-start.5 = (f32[128,256]{1,0:T(8,128)}, f32[128,256]{1,0:T(8,128)S(1)}, u32[]{:S(2)}, u32[]{:S(2)}) collective-permute-start(f32[128,256]{1,0:T(8,128)} %get-tuple-element.22), channel_id=1, source_target_pairs={{0,12},{1,13},{16,28},{17,29},{32,44},{33,45},{48,60},{49,61},{64,... | collective-permute-start | bytes 393224 | tf_op jit(solution)/shard_map/ppermute | solution.py:237
  17.3 6.7 %collective-permute-start.6 = (f32[128,256]{1,0:T(8,128)}, f32[128,256]{1,0:T(8,128)S(1)}, u32[]{:S(2)}, u32[]{:S(2)}) collective-permute-start(f32[128,256]{1,0:T(8,128)} %get-tuple-element.23), channel_id=1, source_target_pairs={{0,14},{1,15},{16,30},{17,31},{32,46},{33,47},{48,62},{49,63},{64,... | collective-permute-start | bytes 393224 | tf_op jit(solution)/shard_map/ppermute | solution.py:237
  25.0 5.1 %collective-permute-start.10 = (f32[128,256]{1,0:T(8,128)S(1)}, f32[128,256]{1,0:T(8,128)S(1)}, u32[]{:S(2)}, u32[]{:S(2)}) collective-permute-start(f32[128,256]{1,0:T(8,128)S(1)} %get-tuple-element.31), channel_id=1, source_target_pairs={{0,2},{1,3},{2,4},{3,5},{4,6},{5,7},{6,8},{7,9},{8,10},{9,11},{10,... | collective-permute-start | bytes 393224 | tf_op jit(solution)/shard_map/ppermute | solution.py:223
  25.1 5.0 %collective-permute-start.7 = (f32[128,256]{1,0:T(8,128)S(1)}, f32[128,256]{1,0:T(8,128)S(1)}, u32[]{:S(2)}, u32[]{:S(2)}) collective-permute-start(f32[128,256]{1,0:T(8,128)S(1)} %get-tuple-element.31), channel_id=1, source_target_pairs={{0,14},{1,15},{2,0},{3,1},{4,2},{5,3},{6,4},{7,5},{8,6},{9,7},{10,... | collective-permute-start | bytes 393224 | tf_op jit(solution)/shard_map/ppermute | solution.py:223
  30.1 5.0 %collective-permute-start.11 = (f32[128,256]{1,0:T(8,128)S(1)}, f32[128,256]{1,0:T(8,128)S(1)}, u32[]{:S(2)}, u32[]{:S(2)}) collective-permute-start(f32[128,256]{1,0:T(8,128)S(1)} %collective-permute-done.10), channel_id=1, source_target_pairs={{0,2},{1,3},{2,4},{3,5},{4,6},{5,7},{6,8},{7,9},{8,10},{9,11},{10,... | collective-permute-start | bytes 393224 | tf_op jit(solution)/shard_map/ppermute | solution.py:223
  30.1 5.0 %collective-permute-start.8 = (f32[128,256]{1,0:T(8,128)S(1)}, f32[128,256]{1,0:T(8,128)S(1)}, u32[]{:S(2)}, u32[]{:S(2)}) collective-permute-start(f32[128,256]{1,0:T(8,128)S(1)} %collective-permute-done.7), channel_id=1, source_target_pairs={{0,14},{1,15},{2,0},{3,1},{4,2},{5,3},{6,4},{7,5},{8,6},{9,7},{10,... | collective-permute-start | bytes 393224 | tf_op jit(solution)/shard_map/ppermute | solution.py:223
  35.1 5.0 %collective-permute-start.12 = (f32[128,256]{1,0:T(8,128)S(1)}, f32[128,256]{1,0:T(8,128)S(1)}, u32[]{:S(2)}, u32[]{:S(2)}) collective-permute-start(f32[128,256]{1,0:T(8,128)S(1)} %collective-permute-done.11), channel_id=1, source_target_pairs={{0,2},{1,3},{2,4},{3,5},{4,6},{5,7},{6,8},{7,9},{8,10},{9,11},{10,... | collective-permute-start | bytes 393224 | tf_op jit(solution)/shard_map/ppermute | solution.py:223
  35.2 5.0 %collective-permute-start.9 = (f32[128,256]{1,0:T(8,128)S(1)}, f32[128,256]{1,0:T(8,128)S(1)}, u32[]{:S(2)}, u32[]{:S(2)}) collective-permute-start(f32[128,256]{1,0:T(8,128)S(1)} %collective-permute-done.8), channel_id=1, source_target_pairs={{0,14},{1,15},{2,0},{3,1},{4,2},{5,3},{6,4},{7,5},{8,6},{9,7},{10,... | collective-permute-start | bytes 393224 | tf_op jit(solution)/shard_map/ppermute | solution.py:223
  40.2 5.3 %collective-permute-start.13 = (f32[64,256]{1,0:T(8,128)S(1)}, f32[64,256]{1,0:T(8,128)S(1)}, u32[]{:S(2)}, u32[]{:S(2)}) collective-permute-start(f32[64,256]{1,0:T(8,128)S(1)} %slice.16), channel_id=1, source_target_pairs={{0,2},{1,3},{2,4},{3,5},{4,6},{5,7},{6,8},{7,9},{8,10},{9,11},{10,... | collective-permute-start | bytes 196616 | tf_op jit(solution)/shard_map/ppermute | solution.py:223
  40.2 5.3 %collective-permute-start.14 = (f32[64,256]{1,0:T(8,128)S(1)}, f32[64,256]{1,0:T(8,128)S(1)}, u32[]{:S(2)}, u32[]{:S(2)}) collective-permute-start(f32[64,256]{1,0:T(8,128)S(1)} %slice.17), channel_id=1, source_target_pairs={{0,14},{1,15},{2,0},{3,1},{4,2},{5,3},{6,4},{7,5},{8,6},{9,7},{10,... | collective-permute-start | bytes 196616 | tf_op jit(solution)/shard_map/ppermute | solution.py:223
  45.6 8.3 %collective-permute-start.15 = (f32[1024,256]{1,0:T(8,128)S(1)}, f32[1024,256]{1,0:T(8,128)S(1)}, u32[]{:S(2)}, u32[]{:S(2)}) collective-permute-start(f32[1024,256]{1,0:T(8,128)S(1)} %constant_dynamic-update-slice_fusion.own_ref), channel_id=1, source_target_pairs={{0,1},{1,0},{2,3},{3,2},{4,5},{5,4},{6,7},{7,6},{8,9},{9,8},{10,11... | collective-permute-start | bytes 3145736 | tf_op jit(solution)/shard_map/ppermute | solution.py:231
  103.5 11.5 %all-to-all-start.1 = ((f32[16,8,640]{2,1,0:T(8,128)}), f32[16,8,640]{2,1,0:T(8,128)S(1)}, u32[]{:S(2)}, u32[]{:S(2)}) async-start(f32[16,8,640]{2,1,0:T(8,128)} %broadcast_in_dim.10), calls=%async_computation.1 | async-start | bytes 655360 | tf_op jit(solution)/shard_map/all_to_all | solution.py:227
  116.5 35.4 %all-to-all-start.2 = ((f32[16,32,1024]{2,1,0:T(8,128)}), f32[16,32,1024]{2,1,0:T(8,128)S(1)}, u32[]{:S(2)}, u32[]{:S(2)}) async-start(f32[16,32,1024]{2,1,0:T(8,128)} %broadcast_in_dim.11), calls=%async_computation.2 | async-start | bytes 4194304 | tf_op jit(solution)/shard_map/all_to_all | solution.py:227
  120.3 4.4 %collective-permute-start.16 = (f32[16,8,640]{2,1,0:T(8,128)S(1)}, f32[16,8,640]{2,1,0:T(8,128)S(1)}, u32[]{:S(2)}, u32[]{:S(2)}) collective-permute-start(f32[16,8,640]{2,1,0:T(8,128)S(1)} %all-to-all-done.1.own_ref), channel_id=1, source_target_pairs={{0,1},{1,0},{2,3},{3,2},{4,5},{5,4},{6,7},{7,6},{8,9},{9,8},{10,11... | collective-permute-start | bytes 983048 | tf_op jit(solution)/shard_map/ppermute | solution.py:231

commit v4 on v3

--- a/solution.py
+++ b/solution.py
@@ -117,7 +117,9 @@
         a = split(jnp.concatenate([a0_ref[:, l, :], a1_ref[:, l, :]], axis=0))
         part = three_pass(panel, a, by_rows)
         for r in range(PEERS):
-            terms_ref[r, :SHARE, l * BLOCK : (l + 1) * BLOCK] += part[r * SHARE : (r + 1) * SHARE]
+            for e in range(BLOCK // TILE):
+                spot = slice((l * BLOCK // TILE + e) * SHARE, (l * BLOCK // TILE + e + 1) * SHARE)
+                terms_ref[r, spot, :] += part[r * SHARE : (r + 1) * SHARE, e * TILE : (e + 1) * TILE]
 
     @pl.when(pl.program_id(0) == pl.num_programs(0) - 1)
     def _():
@@ -126,8 +128,8 @@
             top = n % 16 * 8
             here = gram_ref[i * TILE + top : i * TILE + top + 8, j * TILE : (j + 1) * TILE]
             there = gram_ref[p * TILE + top : p * TILE + top + 8, q * TILE : (q + 1) * TILE]
-            lane = n % TILES * TILE
-            terms_ref[n // TILES, SHARE:, lane : lane + TILE] = jnp.where(first, here, there)
+            spot = terms_ref.shape[1] + (n % TILES - TILES) * 8
+            terms_ref[n // TILES, spot : spot + 8, :] = jnp.where(first, here, there)
 
 
 def factor_kernel(place, own_ref, other_ref, high_ref, low_ref, m_ref, qh_ref, ql_ref, s_ref, t_ref):
@@ -137,9 +139,9 @@
     for n in range(HALF_ROWS // 8):
         (i, j), (p, q) = (half[n // 16] for half in HALF)
         top = n % 16 * 8
-        lane = n % TILES * TILE
-        own = own_ref[n // TILES, :, lane : lane + TILE]
-        other = other_ref[n // TILES, :, lane : lane + TILE]
+        spot = slice(n % TILES * 8, n % TILES * 8 + 8)
+        own = own_ref[n // TILES, spot, :]
+        other = other_ref[n // TILES, spot, :]
         s_ref[j, i * TILE + top : i * TILE + top + 8, :] = jnp.where(first, own, other)
         s_ref[q, p * TILE + top : p * TILE + top + 8, :] = jnp.where(first, other, own)
 
@@ -177,13 +179,17 @@
 
 def remainder_kernel(place, qh_ref, ql_ref, a_ref, m_ref, w_ref, coeff_ref, out_ref, ch_ref, cl_ref):
     width = a_ref.shape[2]
+    each = width // TILE
 
     @pl.when(pl.program_id(0) == 0)
     def _():
-        coeffs = three_pass(split(m_ref[...]), split(w_ref[...]), plain)
+        factor = split(m_ref[...])
         for l in range(coeff_ref.shape[1]):
-            coeff_ref[:, l, :] = coeffs[:, l * width : (l + 1) * width]
-        ch_ref[...], cl_ref[...] = split(coeffs)
+            tiles = [w_ref[:, t * SHARE : (t + 1) * SHARE, :].reshape(FULL, TILE) for t in range(l * each, (l + 1) * each)]
+            coeffs = three_pass(factor, split(jnp.concatenate(tiles, axis=1)), plain)
+            coeff_ref[:, l, :] = coeffs
+            window = slice(l * width, (l + 1) * width)
+            ch_ref[:, window], cl_ref[:, window] = split(coeffs)
 
     q = qh_ref[...], ql_ref[...]
     for l in range(a_ref.shape[1]):
@@ -233,7 +239,7 @@
 
 def share_panel(mine, z):
     own = jnp.where(z == 0, mine[0], jnp.zeros((PIECE, BLOCK), jnp.float32))
-    for k in range(1, DEPTH):
+    for k in (3, 5, 4, 2, 6, 1, 7):
         own = own + lax.ppermute(mine[k], "col", [(0, 2 * k), (1, 2 * k + 1)])
     up, down = [own], [own]
     for _ in range(DEPTH // 2 - 1):
@@ -265,6 +271,7 @@
     steps = rows // step
     own_spec = pl.BlockSpec((step, BLOCK), lambda g, place: (g, 0))
     panel_spec = pl.BlockSpec((step, FULL), lambda g, place: (g, 0))
+    share_rows = SHARE * blocks * width // TILE
     high, low, terms = call(
         product_kernel, "product", 20, (steps,),
         [own_spec, own_spec]
@@ -272,17 +279,17 @@
             pl.BlockSpec((PIECE, blocks, width), lambda g, place, e=e: (lax.rem(place[0] + 2 * g + e, DEPTH), 0, 0))
             for e in range(2)
         ],
-        [panel_spec, panel_spec, whole(PEERS, SHARE + 8, blocks * width)],
-        [bf16(rows, FULL), bf16(rows, FULL), f32(PEERS, SHARE + 8, blocks * width)],
+        [panel_spec, panel_spec, whole(PEERS, share_rows + TILES * 8, TILE)],
+        [bf16(rows, FULL), bf16(rows, FULL), f32(PEERS, share_rows + TILES * 8, TILE)],
         [pltpu.VMEM((FULL, FULL), jnp.float32)],
     )(place, own, other, *in_hbm(matrix, matrix))
     total = jnp.sum(lax.all_to_all(terms, "row", 0, 0), axis=0)
-    gram = everywhere(total[SHARE:, : TILES * TILE])
-    sums = everywhere(total[:SHARE]).reshape(FULL, blocks * width)
+    gram = everywhere(total[share_rows:])
+    sums = everywhere(total[:share_rows])
 
     m, qh, ql = call(
         factor_kernel, "factor", 20, (1,),
-        [whole(PEERS, 8, TILES * TILE)] * 2 + [whole(rows, FULL)] * 2,
+        [whole(PEERS, TILES * 8, TILE)] * 2 + [whole(rows, FULL)] * 2,
         [whole(FULL, FULL), whole(rows, FULL), whole(rows, FULL)],
         [f32(FULL, FULL), bf16(rows, FULL), bf16(rows, FULL)],
         [pltpu.VMEM((NB, FULL, TILE), jnp.float32), pltpu.VMEM((NB, TILE, FULL), jnp.float32)],
@@ -291,7 +298,7 @@
     a_spec = pl.BlockSpec((step, blocks, width), lambda g, place: (g, 0, 0))
     return call(
         remainder_kernel, "remainder", 22, (steps,),
-        [panel_spec, panel_spec, a_spec, whole(FULL, FULL), whole(FULL, blocks * width)],
+        [panel_spec, panel_spec, a_spec, whole(FULL, FULL), whole(PEERS, share_rows, TILE)],
         [whole(FULL, blocks, width), a_spec],
         [f32(FULL, blocks, width), f32(rows, blocks, width)],
         [pltpu.VMEM((FULL, blocks * width), jnp.bfloat16)] * 2,

time: 164 us -> 160 us (0.976)
  waiting for transfers between devices: 26.3 us -> 23.8 us
  blocking collectives: 39.7 us -> 37.9 us
    ppermute x7, waiting for transfers between devices: 5.42 us -> 2.8 us  [share_panel(): own = own + lax.ppermute(mine[k], 'col', [(0, 2 * k), (1, 2 * k + 1)])]
    all_to_all x1, blocking collectives: 39.7 us -> 37.9 us  [on_device(): total = jnp.sum(lax.all_to_all(terms, 'row', 0, 0), axis=0)]
  transfers between devices with their start and end apart: 19 -> 19, of which waited for: 9 -> 8; matrix products, arithmetic and copies ran while one was open for 0% -> 0% of each run, Pallas kernels for 17% -> 17%
where the time goes in v4:
time: 160 us
  Pallas kernels  50.3 us (31%)
  starting transfers between devices  43.1 us (27%)
  blocking collectives  37.9 us (24%)
  waiting for transfers between devices  23.8 us (15%)
  local copies, waits for them, and re-layouts  2.37 us (1%)
    all_to_all x1, blocking collectives, on_device(): total = jnp.sum(lax.all_to_all(terms, 'row', 0, 0), axis=0)  37.9 us
    pallas_call x1, Pallas kernels, on_device(): call(factor_kernel, 'factor', 20, (1,), [whole(PEERS, TILES * 8, TILE)] *...  27.3 us
    ppermute x7, starting transfers between devices, share_panel(): own = own + lax.ppermute(mine[k], 'col', [(0, 2 * k), (1, 2 * k + 1)])  16.4 us
    pallas_call x1, Pallas kernels, on_device(): call(remainder_kernel, 'remainder', 22, (steps,), [panel_spec, panel_spec...  11.7 us
    ppermute x8, starting transfers between devices, shift(): return lax.ppermute(x, axis, [(i, (i + by) % PEERS) for i in range(PEERS)])  10.8 us
    ppermute x8, waiting for transfers between devices, shift(): return lax.ppermute(x, axis, [(i, (i + by) % PEERS) for i in range(PEERS)])  9.53 us
    pallas_call x1, Pallas kernels, on_device(): call(product_kernel, 'product', 20, (steps,), [own_spec, own_spec] + [pl....  9.02 us
    ppermute x2, starting transfers between devices, swap_cores(): return lax.ppermute(x, 'col', [(i, i ^ 1) for i in range(PEERS)])  8.66 us
  transfers between devices with their start and end apart: 19, of which 8 were waited for; matrix products, arithmetic and copies ran while one was open for 0% of the time, Pallas kernels for 17%

profile of v4, /device:TPU:1, one launch (start us, length us, event | category | flops | bytes accessed | tf_op | source)
XLA Modules:
  0.0 159.6 jit_solution(10342463907203763843)
XLA Ops:
  0.6 2.3 %panel.1 = (f32[128,256]{1,0:T(8,128)}, f32[128,256]{1,0:T(8,128)}, f32[128,256]{1,0:T(8,128)}, f32[128,256]{1,0:T(8,128)}, f32[128,256]{1,0:T(8,128)}, /*index=...) custom-call(f32[1024,4,256]{2,1,0:T(4,128)} %a_ref.1), custom_call_target="tpu_custom_call" | custom-call | tf_op jit(solution)/shard_map/panel/pallas_call | solution.py:259
  3.0 7.1 %collective-permute-start = (f32[128,256]{1,0:T(8,128)}, f32[128,256]{1,0:T(8,128)S(1)}, u32[]{:S(2)}, u32[]{:S(2)}) collective-permute-start(f32[128,256]{1,0:T(8,128)} %get-tuple-element.17), channel_id=1, source_target_pairs={{0,6},{1,7},{16,22},{17,23},{32,38},{33,39},{48,54},{49,55},{64,70... | collective-permute-start | bytes 393224 | tf_op jit(solution)/shard_map/ppermute | solution.py:243
  10.1 2.8 %collective-permute-start.1 = (f32[128,256]{1,0:T(8,128)}, f32[128,256]{1,0:T(8,128)S(1)}, u32[]{:S(2)}, u32[]{:S(2)}) collective-permute-start(f32[128,256]{1,0:T(8,128)} %get-tuple-element.18), channel_id=1, source_target_pairs={{0,10},{1,11},{16,26},{17,27},{32,42},{33,43},{48,58},{49,59},{64,... | collective-permute-start | bytes 393224 | tf_op jit(solution)/shard_map/ppermute | solution.py:243
  12.9 1.3 collective-permute-start.2
  14.2 1.3 collective-permute-start.3
  15.5 1.3 collective-permute-start.4
  16.8 0.0 collective-permute-done
  16.8 1.3 collective-permute-start.5
  18.1 0.0 collective-permute-done.1
  18.1 1.3 collective-permute-start.6
  19.4 0.0 collective-permute-done.2
  19.4 0.0 collective-permute-done.3
  19.4 0.0 collective-permute-done.4
  19.4 2.8 %collective-permute-done.5 = f32[128,256]{1,0:T(8,128)S(1)} collective-permute-done((f32[128,256]{1,0:T(8,128)}, f32[128,256]{1,0:T(8,128)S(1)}, u32[]{:S(2)}, u32[]{:S(2)}) %collective-permute-start.5) | collective-permute-done | bytes 131104 | tf_op jit(solution)/shard_map/ppermute | solution.py:243
  22.2 0.0 collective-permute-done.6
  22.2 1.0 constant_dynamic-update-slice_fusion.8
  23.2 1.3 collective-permute-start.10
  24.5 1.5 collective-permute-start.7
  26.0 2.4 %collective-permute-done.10 = f32[128,256]{1,0:T(8,128)S(1)} collective-permute-done((f32[128,256]{1,0:T(8,128)S(1)}, f32[128,256]{1,0:T(8,128)S(1)}, u32[]{:S(2)}, u32[]{:S(2)}) %collective-permute-start.10) | collective-permute-done | bytes 131104 | tf_op jit(solution)/shard_map/ppermute | solution.py:229
  28.3 0.0 collective-permute-start.11
  28.3 0.0 collective-permute-done.7
  28.3 2.7 %collective-permute-start.8 = (f32[128,256]{1,0:T(8,128)S(1)}, f32[128,256]{1,0:T(8,128)S(1)}, u32[]{:S(2)}, u32[]{:S(2)}) collective-permute-start(f32[128,256]{1,0:T(8,128)S(1)} %collective-permute-done.7), channel_id=1, source_target_pairs={{0,14},{1,15},{2,0},{3,1},{4,2},{5,3},{6,4},{7,5},{8,6},{9,7},{10,... | collective-permute-start | bytes 393224 | tf_op jit(solution)/shard_map/ppermute | solution.py:229
  31.0 2.3 %collective-permute-done.11 = f32[128,256]{1,0:T(8,128)S(1)} collective-permute-done((f32[128,256]{1,0:T(8,128)S(1)}, f32[128,256]{1,0:T(8,128)S(1)}, u32[]{:S(2)}, u32[]{:S(2)}) %collective-permute-start.11) | collective-permute-done | bytes 131104 | tf_op jit(solution)/shard_map/ppermute | solution.py:229
  33.3 0.0 collective-permute-start.12
  33.4 0.0 collective-permute-done.8
  33.4 2.7 %collective-permute-start.9 = (f32[128,256]{1,0:T(8,128)S(1)}, f32[128,256]{1,0:T(8,128)S(1)}, u32[]{:S(2)}, u32[]{:S(2)}) collective-permute-start(f32[128,256]{1,0:T(8,128)S(1)} %collective-permute-done.8), channel_id=1, source_target_pairs={{0,14},{1,15},{2,0},{3,1},{4,2},{5,3},{6,4},{7,5},{8,6},{9,7},{10,... | collective-permute-start | bytes 393224 | tf_op jit(solution)/shard_map/ppermute | solution.py:229
  36.1 2.3 %collective-permute-done.12 = f32[128,256]{1,0:T(8,128)S(1)} collective-permute-done((f32[128,256]{1,0:T(8,128)S(1)}, f32[128,256]{1,0:T(8,128)S(1)}, u32[]{:S(2)}, u32[]{:S(2)}) %collective-permute-start.12) | collective-permute-done | bytes 131104 | tf_op jit(solution)/shard_map/ppermute | solution.py:229
  38.4 0.0 collective-permute-start.13
  38.4 0.0 collective-permute-done.9
  38.4 2.7 %collective-permute-start.14 = (f32[64,256]{1,0:T(8,128)S(1)}, f32[64,256]{1,0:T(8,128)S(1)}, u32[]{:S(2)}, u32[]{:S(2)}) collective-permute-start(f32[64,256]{1,0:T(8,128)S(1)} %slice.17), channel_id=1, source_target_pairs={{0,14},{1,15},{2,0},{3,1},{4,2},{5,3},{6,4},{7,5},{8,6},{9,7},{10,... | collective-permute-start | bytes 196616 | tf_op jit(solution)/shard_map/ppermute | solution.py:229
  41.2 2.5 %collective-permute-done.13 = f32[64,256]{1,0:T(8,128)S(1)} collective-permute-done((f32[64,256]{1,0:T(8,128)S(1)}, f32[64,256]{1,0:T(8,128)S(1)}, u32[]{:S(2)}, u32[]{:S(2)}) %collective-permute-start.13) | collective-permute-done | bytes 65568 | tf_op jit(solution)/shard_map/ppermute | solution.py:229
  43.7 0.0 collective-permute-done.14
  43.8 6.0 %collective-permute-start.15 = (f32[1024,256]{1,0:T(8,128)S(1)}, f32[1024,256]{1,0:T(8,128)S(1)}, u32[]{:S(2)}, u32[]{:S(2)}) collective-permute-start(f32[1024,256]{1,0:T(8,128)S(1)} %constant_dynamic-update-slice_fusion.own_ref), channel_id=1, source_target_pairs={{0,1},{1,0},{2,3},{3,2},{4,5},{5,4},{6,7},{7,6},{8,9},{9,8},{10,11... | collective-permute-start | bytes 3145736 | tf_op jit(solution)/shard_map/ppermute | solution.py:237
  49.7 0.1 pad_add_fusion.place
  49.8 2.2 %collective-permute-done.15.other_ref = f32[1024,256]{1,0:T(8,128)S(1)} collective-permute-done((f32[1024,256]{1,0:T(8,128)S(1)}, f32[1024,256]{1,0:T(8,128)S(1)}, u32[]{:S(2)}, u32[]{:S(2)}) %collective-permute-start.15) | collective-permute-done | bytes 1048608 | tf_op jit(solution)/shard_map/ppermute | solution.py:237
  52.0 9.0 %product.1 = (bf16[1024,512]{1,0:T(8,128)(2,1)}, bf16[1024,512]{1,0:T(8,128)(2,1)}, f32[16,296,128]{2,1,0:T(8,128)S(1)}) custom-call(s32[3]{0:T(128)S(1)} %pad_add_fusion.place, f32[1024,256]{1,0:T(8,128)S(1)} %constant_dynamic-update-slice_fusion.own_ref, f32[1024,256]{1,0:T(8,128)S(1)} %collective-permute-done.15.other_ref, f32[1024,4,256]{2,1,0:T(4,128)} %a_ref.1, ...), custom_call_target="tpu_custom_call" | custom-call | tf_op jit(solution)/shard_map/product/pallas_call | solution.py:275
  61.0 37.9 %all_to_all.15 = f32[16,296,128]{2,1,0:T(8,128)S(1)} all-to-all(f32[16,296,128]{2,1,0:T(8,128)S(1)} %get-tuple-element.24), channel_id=1, replica_groups=mesh['row'=16,'col'=16] {'row'}, dimensions={0} | all-to-all | bytes 4849664 | tf_op jit(solution)/shard_map/all_to_all | solution.py:286
  99.0 0.1 reduce_sum.9
  99.1 0.7 broadcast_in_dim.10
  99.8 3.5 %all-to-all-start.1 = ((f32[16,40,128]{2,1,0:T(8,128)}), f32[16,40,128]{2,1,0:T(8,128)S(1)}, u32[]{:S(2)}, u32[]{:S(2)}) async-start(f32[16,40,128]{2,1,0:T(8,128)} %broadcast_in_dim.10), calls=%async_computation.1 | async-start | bytes 655360 | tf_op jit(solution)/shard_map/all_to_all | solution.py:233
  103.4 8.0 %all-to-all-done.1.own_ref = f32[16,40,128]{2,1,0:T(8,128)S(1)} async-done(((f32[16,40,128]{2,1,0:T(8,128)}), f32[16,40,128]{2,1,0:T(8,128)S(1)}, u32[]{:S(2)}, u32[]{:S(2)}) %all-to-all-start.1) | async-done | bytes 327712 | tf_op jit(solution)/shard_map/all_to_all | solution.py:233
  111.5 1.5 broadcast_in_dim.11
  113.0 3.7 %all-to-all-start.2 = ((f32[16,256,128]{2,1,0:T(8,128)}), f32[16,256,128]{2,1,0:T(8,128)S(1)}, u32[]{:S(2)}, u32[]{:S(2)}) async-start(f32[16,256,128]{2,1,0:T(8,128)} %broadcast_in_dim.11), calls=%async_computation.2 | async-start | bytes 4194304 | tf_op jit(solution)/shard_map/all_to_all | solution.py:233
  116.7 2.7 %collective-permute-start.16 = (f32[16,40,128]{2,1,0:T(8,128)S(1)}, f32[16,40,128]{2,1,0:T(8,128)S(1)}, u32[]{:S(2)}, u32[]{:S(2)}) collective-permute-start(f32[16,40,128]{2,1,0:T(8,128)S(1)} %all-to-all-done.1.own_ref), channel_id=1, source_target_pairs={{0,1},{1,0},{2,3},{3,2},{4,5},{5,4},{6,7},{7,6},{8,9},{9,8},{10,11... | collective-permute-start | bytes 983048 | tf_op jit(solution)/shard_map/ppermute | solution.py:237
  119.4 1.3 collective-permute-done.16.other_ref
  120.6 27.3 %factor.1 = (f32[512,512]{1,0:T(8,128)S(1)}, bf16[1024,512]{1,0:T(8,128)(2,1)}, bf16[1024,512]{1,0:T(8,128)(2,1)}) custom-call(s32[3]{0:T(128)S(1)} %pad_add_fusion.place, f32[16,40,128]{2,1,0:T(8,128)S(1)} %all-to-all-done.1.own_ref, f32[16,40,128]{2,1,0:T(8,128)S(1)} %collective-permute-done.16.other_ref, bf16[1024,512]{1,0:T(8,128)(2,1)} %get-tuple-element.25.high_ref, ...), custom_call_target="tpu_custom_call" | custom-call | tf_op jit(solution)/shard_map/factor/pallas_call | solution.py:290
  147.9 0.0 all-to-all-done.2.w_ref
  147.9 11.7 %remainder.1 = (f32[512,4,256]{2,1,0:T(4,128)}, f32[1024,4,256]{2,1,0:T(4,128)}) custom-call(s32[3]{0:T(128)S(1)} %pad_add_fusion.place, bf16[1024,512]{1,0:T(8,128)(2,1)} %get-tuple-element.27.qh_ref, bf16[1024,512]{1,0:T(8,128)(2,1)} %get-tuple-element.28.ql_ref, f32[1024,4,256]{2,1,0:T(4,128)} %a_ref.1, f32[512,512]{1,0:T(8,128)S(1)} %get-tuple-element.29.m_ref, ...), custom_call_target="tpu_custom_call" | custom-call | tf_op jit(solution)/shard_map/remainder/pallas_call | solution.py:299
  (12 shorter events, 0.1 us)
Async XLA Ops:
  3.0 13.8 %collective-permute-start = (f32[128,256]{1,0:T(8,128)}, f32[128,256]{1,0:T(8,128)S(1)}, u32[]{:S(2)}, u32[]{:S(2)}) collective-permute-start(f32[128,256]{1,0:T(8,128)} %get-tuple-element.17), channel_id=1, source_target_pairs={{0,6},{1,7},{16,22},{17,23},{32,38},{33,39},{48,54},{49,55},{64,70... | collective-permute-start | bytes 393224 | tf_op jit(solution)/shard_map/ppermute | solution.py:243
  10.1 8.0 %collective-permute-start.1 = (f32[128,256]{1,0:T(8,128)}, f32[128,256]{1,0:T(8,128)S(1)}, u32[]{:S(2)}, u32[]{:S(2)}) collective-permute-start(f32[128,256]{1,0:T(8,128)} %get-tuple-element.18), channel_id=1, source_target_pairs={{0,10},{1,11},{16,26},{17,27},{32,42},{33,43},{48,58},{49,59},{64,... | collective-permute-start | bytes 393224 | tf_op jit(solution)/shard_map/ppermute | solution.py:243
  12.9 6.6 %collective-permute-start.2 = (f32[128,256]{1,0:T(8,128)}, f32[128,256]{1,0:T(8,128)S(1)}, u32[]{:S(2)}, u32[]{:S(2)}) collective-permute-start(f32[128,256]{1,0:T(8,128)} %get-tuple-element.19), channel_id=1, source_target_pairs={{0,8},{1,9},{16,24},{17,25},{32,40},{33,41},{48,56},{49,57},{64,72... | collective-permute-start | bytes 393224 | tf_op jit(solution)/shard_map/ppermute | solution.py:243
  14.2 5.3 %collective-permute-start.3 = (f32[128,256]{1,0:T(8,128)}, f32[128,256]{1,0:T(8,128)S(1)}, u32[]{:S(2)}, u32[]{:S(2)}) collective-permute-start(f32[128,256]{1,0:T(8,128)} %get-tuple-element.20), channel_id=1, source_target_pairs={{0,4},{1,5},{16,20},{17,21},{32,36},{33,37},{48,52},{49,53},{64,68... | collective-permute-start | bytes 393224 | tf_op jit(solution)/shard_map/ppermute | solution.py:243
  15.5 4.0 %collective-permute-start.4 = (f32[128,256]{1,0:T(8,128)}, f32[128,256]{1,0:T(8,128)S(1)}, u32[]{:S(2)}, u32[]{:S(2)}) collective-permute-start(f32[128,256]{1,0:T(8,128)} %get-tuple-element.21), channel_id=1, source_target_pairs={{0,12},{1,13},{16,28},{17,29},{32,44},{33,45},{48,60},{49,61},{64,... | collective-permute-start | bytes 393224 | tf_op jit(solution)/shard_map/ppermute | solution.py:243
  16.8 5.5 %collective-permute-start.5 = (f32[128,256]{1,0:T(8,128)}, f32[128,256]{1,0:T(8,128)S(1)}, u32[]{:S(2)}, u32[]{:S(2)}) collective-permute-start(f32[128,256]{1,0:T(8,128)} %get-tuple-element.22), channel_id=1, source_target_pairs={{0,2},{1,3},{16,18},{17,19},{32,34},{33,35},{48,50},{49,51},{64,66... | collective-permute-start | bytes 393224 | tf_op jit(solution)/shard_map/ppermute | solution.py:243
  18.1 4.1 %collective-permute-start.6 = (f32[128,256]{1,0:T(8,128)}, f32[128,256]{1,0:T(8,128)S(1)}, u32[]{:S(2)}, u32[]{:S(2)}) collective-permute-start(f32[128,256]{1,0:T(8,128)} %get-tuple-element.23), channel_id=1, source_target_pairs={{0,14},{1,15},{16,30},{17,31},{32,46},{33,47},{48,62},{49,63},{64,... | collective-permute-start | bytes 393224 | tf_op jit(solution)/shard_map/ppermute | solution.py:243
  23.2 5.1 %collective-permute-start.10 = (f32[128,256]{1,0:T(8,128)S(1)}, f32[128,256]{1,0:T(8,128)S(1)}, u32[]{:S(2)}, u32[]{:S(2)}) collective-permute-start(f32[128,256]{1,0:T(8,128)S(1)} %get-tuple-element.31), channel_id=1, source_target_pairs={{0,2},{1,3},{2,4},{3,5},{4,6},{5,7},{6,8},{7,9},{8,10},{9,11},{10,... | collective-permute-start | bytes 393224 | tf_op jit(solution)/shard_map/ppermute | solution.py:229
  24.5 3.8 %collective-permute-start.7 = (f32[128,256]{1,0:T(8,128)S(1)}, f32[128,256]{1,0:T(8,128)S(1)}, u32[]{:S(2)}, u32[]{:S(2)}) collective-permute-start(f32[128,256]{1,0:T(8,128)S(1)} %get-tuple-element.31), channel_id=1, source_target_pairs={{0,14},{1,15},{2,0},{3,1},{4,2},{5,3},{6,4},{7,5},{8,6},{9,7},{10,... | collective-permute-start | bytes 393224 | tf_op jit(solution)/shard_map/ppermute | solution.py:229
  28.3 5.0 %collective-permute-start.11 = (f32[128,256]{1,0:T(8,128)S(1)}, f32[128,256]{1,0:T(8,128)S(1)}, u32[]{:S(2)}, u32[]{:S(2)}) collective-permute-start(f32[128,256]{1,0:T(8,128)S(1)} %collective-permute-done.10), channel_id=1, source_target_pairs={{0,2},{1,3},{2,4},{3,5},{4,6},{5,7},{6,8},{7,9},{8,10},{9,11},{10,... | collective-permute-start | bytes 393224 | tf_op jit(solution)/shard_map/ppermute | solution.py:229
  28.3 5.0 %collective-permute-start.8 = (f32[128,256]{1,0:T(8,128)S(1)}, f32[128,256]{1,0:T(8,128)S(1)}, u32[]{:S(2)}, u32[]{:S(2)}) collective-permute-start(f32[128,256]{1,0:T(8,128)S(1)} %collective-permute-done.7), channel_id=1, source_target_pairs={{0,14},{1,15},{2,0},{3,1},{4,2},{5,3},{6,4},{7,5},{8,6},{9,7},{10,... | collective-permute-start | bytes 393224 | tf_op jit(solution)/shard_map/ppermute | solution.py:229
  33.3 5.0 %collective-permute-start.12 = (f32[128,256]{1,0:T(8,128)S(1)}, f32[128,256]{1,0:T(8,128)S(1)}, u32[]{:S(2)}, u32[]{:S(2)}) collective-permute-start(f32[128,256]{1,0:T(8,128)S(1)} %collective-permute-done.11), channel_id=1, source_target_pairs={{0,2},{1,3},{2,4},{3,5},{4,6},{5,7},{6,8},{7,9},{8,10},{9,11},{10,... | collective-permute-start | bytes 393224 | tf_op jit(solution)/shard_map/ppermute | solution.py:229
  33.4 5.0 %collective-permute-start.9 = (f32[128,256]{1,0:T(8,128)S(1)}, f32[128,256]{1,0:T(8,128)S(1)}, u32[]{:S(2)}, u32[]{:S(2)}) collective-permute-start(f32[128,256]{1,0:T(8,128)S(1)} %collective-permute-done.8), channel_id=1, source_target_pairs={{0,14},{1,15},{2,0},{3,1},{4,2},{5,3},{6,4},{7,5},{8,6},{9,7},{10,... | collective-permute-start | bytes 393224 | tf_op jit(solution)/shard_map/ppermute | solution.py:229
  38.4 5.3 %collective-permute-start.13 = (f32[64,256]{1,0:T(8,128)S(1)}, f32[64,256]{1,0:T(8,128)S(1)}, u32[]{:S(2)}, u32[]{:S(2)}) collective-permute-start(f32[64,256]{1,0:T(8,128)S(1)} %slice.16), channel_id=1, source_target_pairs={{0,2},{1,3},{2,4},{3,5},{4,6},{5,7},{6,8},{7,9},{8,10},{9,11},{10,... | collective-permute-start | bytes 196616 | tf_op jit(solution)/shard_map/ppermute | solution.py:229
  38.4 5.3 %collective-permute-start.14 = (f32[64,256]{1,0:T(8,128)S(1)}, f32[64,256]{1,0:T(8,128)S(1)}, u32[]{:S(2)}, u32[]{:S(2)}) collective-permute-start(f32[64,256]{1,0:T(8,128)S(1)} %slice.17), channel_id=1, source_target_pairs={{0,14},{1,15},{2,0},{3,1},{4,2},{5,3},{6,4},{7,5},{8,6},{9,7},{10,... | collective-permute-start | bytes 196616 | tf_op jit(solution)/shard_map/ppermute | solution.py:229
  43.8 8.3 %collective-permute-start.15 = (f32[1024,256]{1,0:T(8,128)S(1)}, f32[1024,256]{1,0:T(8,128)S(1)}, u32[]{:S(2)}, u32[]{:S(2)}) collective-permute-start(f32[1024,256]{1,0:T(8,128)S(1)} %constant_dynamic-update-slice_fusion.own_ref), channel_id=1, source_target_pairs={{0,1},{1,0},{2,3},{3,2},{4,5},{5,4},{6,7},{7,6},{8,9},{9,8},{10,11... | collective-permute-start | bytes 3145736 | tf_op jit(solution)/shard_map/ppermute | solution.py:237
  99.8 11.6 %all-to-all-start.1 = ((f32[16,40,128]{2,1,0:T(8,128)}), f32[16,40,128]{2,1,0:T(8,128)S(1)}, u32[]{:S(2)}, u32[]{:S(2)}) async-start(f32[16,40,128]{2,1,0:T(8,128)} %broadcast_in_dim.10), calls=%async_computation.1 | async-start | bytes 655360 | tf_op jit(solution)/shard_map/all_to_all | solution.py:233
  113.0 34.9 %all-to-all-start.2 = ((f32[16,256,128]{2,1,0:T(8,128)}), f32[16,256,128]{2,1,0:T(8,128)S(1)}, u32[]{:S(2)}, u32[]{:S(2)}) async-start(f32[16,256,128]{2,1,0:T(8,128)} %broadcast_in_dim.11), calls=%async_computation.2 | async-start | bytes 4194304 | tf_op jit(solution)/shard_map/all_to_all | solution.py:233
  116.7 3.9 %collective-permute-start.16 = (f32[16,40,128]{2,1,0:T(8,128)S(1)}, f32[16,40,128]{2,1,0:T(8,128)S(1)}, u32[]{:S(2)}, u32[]{:S(2)}) collective-permute-start(f32[16,40,128]{2,1,0:T(8,128)S(1)} %all-to-all-done.1.own_ref), channel_id=1, source_target_pairs={{0,1},{1,0},{2,3},{3,2},{4,5},{5,4},{6,7},{7,6},{8,9},{9,8},{10,11... | collective-permute-start | bytes 983048 | tf_op jit(solution)/shard_map/ppermute | solution.py:237

commit v5 on v4

--- a/solution.py
+++ b/solution.py
@@ -132,6 +132,16 @@
             terms_ref[n // TILES, spot : spot + 8, :] = jnp.where(first, here, there)
 
 
+def total_kernel(place, terms_ref, gram_ref, sums_ref):
+    peers, split_row = sums_ref.shape[:2]
+    total = terms_ref[0]
+    for r in range(1, peers):
+        total = total + terms_ref[r]
+    for r in range(peers):
+        sums_ref[r] = total[:split_row]
+        gram_ref[r] = total[split_row:]
+
+
 def factor_kernel(place, own_ref, other_ref, high_ref, low_ref, m_ref, qh_ref, ql_ref, s_ref, t_ref):
     first = place[1] == 0
     s_ref[...] = jnp.zeros_like(s_ref)
@@ -229,8 +239,8 @@
     return lax.ppermute(x, axis, [(i, (i + by) % PEERS) for i in range(PEERS)])
 
 
-def everywhere(share):
-    return lax.all_to_all(jnp.broadcast_to(share, (PEERS,) + share.shape), "row", 0, 0)
+def exchange(x):
+    return lax.all_to_all(x, "row", 0, 0)
 
 
 def swap_cores(x):
@@ -239,8 +249,9 @@
 
 def share_panel(mine, z):
     own = jnp.where(z == 0, mine[0], jnp.zeros((PIECE, BLOCK), jnp.float32))
-    for k in (3, 5, 4, 2, 6, 1, 7):
+    for k in (1, 7, 2, 6, 4, 3, 5):
         own = own + lax.ppermute(mine[k], "col", [(0, 2 * k), (1, 2 * k + 1)])
+    own = lax.optimization_barrier(own)
     up, down = [own], [own]
     for _ in range(DEPTH // 2 - 1):
         up.append(shift(up[-1], "col", 2))
@@ -283,9 +294,15 @@
         [bf16(rows, FULL), bf16(rows, FULL), f32(PEERS, share_rows + TILES * 8, TILE)],
         [pltpu.VMEM((FULL, FULL), jnp.float32)],
     )(place, own, other, *in_hbm(matrix, matrix))
-    total = jnp.sum(lax.all_to_all(terms, "row", 0, 0), axis=0)
-    gram = everywhere(total[share_rows:])
-    sums = everywhere(total[:share_rows])
+    gram_rows = TILES * 8
+    gram, sums = call(
+        total_kernel, "total", 16, (1,),
+        [whole(PEERS, share_rows + gram_rows, TILE)],
+        [whole(PEERS, gram_rows, TILE), whole(PEERS, share_rows, TILE)],
+        [f32(PEERS, gram_rows, TILE), pltpu.HBM((PEERS, share_rows, TILE), jnp.float32)],
+    )(place, exchange(terms))
+    gram = exchange(gram)
+    sums = exchange(sums)
 
     m, qh, ql = call(
         factor_kernel, "factor", 20, (1,),

time: 160 us -> 158 us (0.988)
  blocking collectives: 37.9 us -> 49.1 us
  waiting for transfers between devices: 23.8 us -> 15.6 us
  starting transfers between devices: 43.1 us -> 38.5 us
  local copies, waits for them, and re-layouts: 2.37 us -> 0.1 us
  Pallas kernels: 50.3 us -> 52.4 us
    all_to_all x1 -> x2, blocking collectives: 37.9 us -> 49.1 us  [exchange(): return lax.all_to_all(x, 'row', 0, 0)]
    all_to_all x2 -> x1, waiting for transfers between devices: 8.04 us -> 0.01 us  [exchange(): return lax.all_to_all(x, 'row', 0, 0)]
    all_to_all x2 -> x1, starting transfers between devices: 7.26 us -> 3.72 us  [exchange(): return lax.all_to_all(x, 'row', 0, 0)]
    broadcast_in_dim x2 -> x0, local copies, waits for them, and re-layouts: 2.27 us -> none  [everywhere(): jnp.broadcast_to(share, (PEERS,) + share.shape)]
    pallas_call x0 -> x1, Pallas kernels: none -> 2.08 us  [on_device(): call(total_kernel, 'total', 16, (1,), [whole(PEERS, share_rows + gram_row...]
  transfers between devices with their start and end apart: 19 -> 18, of which waited for: 8 -> 8; matrix products, arithmetic and copies ran while one was open for 0% -> 0% of each run, Pallas kernels for 17% -> 17%
where the time goes in v5:
time: 158 us
  Pallas kernels  52.4 us (33%)
  blocking collectives  49.1 us (31%)
  starting transfers between devices  38.5 us (24%)
  waiting for transfers between devices  15.6 us (10%)
    all_to_all x2, blocking collectives, exchange(): return lax.all_to_all(x, 'row', 0, 0)  49.1 us
    pallas_call x1, Pallas kernels, on_device(): call(factor_kernel, 'factor', 20, (1,), [whole(PEERS, TILES * 8, TILE)] *...  27.3 us
    ppermute x7, starting transfers between devices, share_panel(): own = own + lax.ppermute(mine[k], 'col', [(0, 2 * k), (1, 2 * k + 1)])  15.5 us
    pallas_call x1, Pallas kernels, on_device(): call(remainder_kernel, 'remainder', 22, (steps,), [panel_spec, panel_spec...  11.7 us
    ppermute x8, starting transfers between devices, shift(): return lax.ppermute(x, axis, [(i, (i + by) % PEERS) for i in range(PEERS)])  10.8 us
    ppermute x8, waiting for transfers between devices, shift(): return lax.ppermute(x, axis, [(i, (i + by) % PEERS) for i in range(PEERS)])  9.11 us
    pallas_call x1, Pallas kernels, on_device(): call(product_kernel, 'product', 20, (steps,), [own_spec, own_spec] + [pl....  9.02 us
    ppermute x2, starting transfers between devices, swap_cores(): return lax.ppermute(x, 'col', [(i, i ^ 1) for i in range(PEERS)])  8.45 us
  transfers between devices with their start and end apart: 18, of which 8 were waited for; matrix products, arithmetic and copies ran while one was open for 0% of the time, Pallas kernels for 17%

profile of v5, /device:TPU:1, one launch (start us, length us, event | category | flops | bytes accessed | tf_op | source)
XLA Modules:
  0.0 157.6 jit_solution(15874155244279288749)
XLA Ops:
  0.6 2.3 %panel.1 = (f32[128,256]{1,0:T(8,128)}, f32[128,256]{1,0:T(8,128)}, f32[128,256]{1,0:T(8,128)}, f32[128,256]{1,0:T(8,128)}, f32[128,256]{1,0:T(8,128)}, /*index=...) custom-call(f32[1024,4,256]{2,1,0:T(4,128)} %a_ref.1), custom_call_target="tpu_custom_call" | custom-call | tf_op jit(solution)/shard_map/panel/pallas_call | solution.py:270
  3.0 4.4 %collective-permute-start = (f32[128,256]{1,0:T(8,128)}, f32[128,256]{1,0:T(8,128)S(1)}, u32[]{:S(2)}, u32[]{:S(2)}) collective-permute-start(f32[128,256]{1,0:T(8,128)} %get-tuple-element.19), channel_id=1, source_target_pairs={{0,2},{1,3},{16,18},{17,19},{32,34},{33,35},{48,50},{49,51},{64,66... | collective-permute-start | bytes 393224 | tf_op jit(solution)/shard_map/ppermute | solution.py:253
  7.3 4.6 %collective-permute-start.1 = (f32[128,256]{1,0:T(8,128)}, f32[128,256]{1,0:T(8,128)S(1)}, u32[]{:S(2)}, u32[]{:S(2)}) collective-permute-start(f32[128,256]{1,0:T(8,128)} %get-tuple-element.20), channel_id=1, source_target_pairs={{0,14},{1,15},{16,30},{17,31},{32,46},{33,47},{48,62},{49,63},{64,... | collective-permute-start | bytes 393224 | tf_op jit(solution)/shard_map/ppermute | solution.py:253
  12.0 1.3 collective-permute-start.2
  13.3 1.3 collective-permute-start.3
  14.6 1.3 collective-permute-start.4
  15.9 0.0 collective-permute-done
  15.9 1.3 collective-permute-start.5
  17.2 0.0 collective-permute-done.1
  17.2 1.3 collective-permute-start.6
  18.5 0.0 collective-permute-done.2
  18.5 0.0 collective-permute-done.3
  18.5 0.2 collective-permute-done.4
  18.7 2.9 %collective-permute-done.5 = f32[128,256]{1,0:T(8,128)S(1)} collective-permute-done((f32[128,256]{1,0:T(8,128)}, f32[128,256]{1,0:T(8,128)S(1)}, u32[]{:S(2)}, u32[]{:S(2)}) %collective-permute-start.5) | collective-permute-done | bytes 131104 | tf_op jit(solution)/shard_map/ppermute | solution.py:253
  21.6 0.0 collective-permute-done.6
  21.6 1.0 add_add_fusion
  22.6 0.1 collective-permute-start.10
  22.7 2.7 %collective-permute-start.7 = (f32[128,256]{1,0:T(8,128)S(1)}, f32[128,256]{1,0:T(8,128)S(1)}, u32[]{:S(2)}, u32[]{:S(2)}) collective-permute-start(f32[128,256]{1,0:T(8,128)S(1)} %add_add_fusion), channel_id=1, source_target_pairs={{0,14},{1,15},{2,0},{3,1},{4,2},{5,3},{6,4},{7,5},{8,6},{9,7},{10,... | collective-permute-start | bytes 393224 | tf_op jit(solution)/shard_map/ppermute | solution.py:239
  25.3 2.4 %collective-permute-done.10 = f32[128,256]{1,0:T(8,128)S(1)} collective-permute-done((f32[128,256]{1,0:T(8,128)S(1)}, f32[128,256]{1,0:T(8,128)S(1)}, u32[]{:S(2)}, u32[]{:S(2)}) %collective-permute-start.10) | collective-permute-done | bytes 131104 | tf_op jit(solution)/shard_map/ppermute | solution.py:239
  27.7 0.0 collective-permute-start.11
  27.7 0.0 collective-permute-done.7
  27.7 2.7 %collective-permute-start.8 = (f32[128,256]{1,0:T(8,128)S(1)}, f32[128,256]{1,0:T(8,128)S(1)}, u32[]{:S(2)}, u32[]{:S(2)}) collective-permute-start(f32[128,256]{1,0:T(8,128)S(1)} %collective-permute-done.7), channel_id=1, source_target_pairs={{0,14},{1,15},{2,0},{3,1},{4,2},{5,3},{6,4},{7,5},{8,6},{9,7},{10,... | collective-permute-start | bytes 393224 | tf_op jit(solution)/shard_map/ppermute | solution.py:239
  30.4 2.3 %collective-permute-done.11 = f32[128,256]{1,0:T(8,128)S(1)} collective-permute-done((f32[128,256]{1,0:T(8,128)S(1)}, f32[128,256]{1,0:T(8,128)S(1)}, u32[]{:S(2)}, u32[]{:S(2)}) %collective-permute-start.11) | collective-permute-done | bytes 131104 | tf_op jit(solution)/shard_map/ppermute | solution.py:239
  32.7 0.0 collective-permute-start.12
  32.7 0.0 collective-permute-done.8
  32.7 2.7 %collective-permute-start.9 = (f32[128,256]{1,0:T(8,128)S(1)}, f32[128,256]{1,0:T(8,128)S(1)}, u32[]{:S(2)}, u32[]{:S(2)}) collective-permute-start(f32[128,256]{1,0:T(8,128)S(1)} %collective-permute-done.8), channel_id=1, source_target_pairs={{0,14},{1,15},{2,0},{3,1},{4,2},{5,3},{6,4},{7,5},{8,6},{9,7},{10,... | collective-permute-start | bytes 393224 | tf_op jit(solution)/shard_map/ppermute | solution.py:239
  35.4 2.3 %collective-permute-done.12 = f32[128,256]{1,0:T(8,128)S(1)} collective-permute-done((f32[128,256]{1,0:T(8,128)S(1)}, f32[128,256]{1,0:T(8,128)S(1)}, u32[]{:S(2)}, u32[]{:S(2)}) %collective-permute-start.12) | collective-permute-done | bytes 131104 | tf_op jit(solution)/shard_map/ppermute | solution.py:239
  37.7 0.0 collective-permute-start.13
  37.7 0.0 collective-permute-done.9
  37.8 2.7 %collective-permute-start.14 = (f32[64,256]{1,0:T(8,128)S(1)}, f32[64,256]{1,0:T(8,128)S(1)}, u32[]{:S(2)}, u32[]{:S(2)}) collective-permute-start(f32[64,256]{1,0:T(8,128)S(1)} %slice.9), channel_id=1, source_target_pairs={{0,14},{1,15},{2,0},{3,1},{4,2},{5,3},{6,4},{7,5},{8,6},{9,7},{10,... | collective-permute-start | bytes 196616 | tf_op jit(solution)/shard_map/ppermute | solution.py:239
  40.5 2.1 %collective-permute-done.13 = f32[64,256]{1,0:T(8,128)S(1)} collective-permute-done((f32[64,256]{1,0:T(8,128)S(1)}, f32[64,256]{1,0:T(8,128)S(1)}, u32[]{:S(2)}, u32[]{:S(2)}) %collective-permute-start.13) | collective-permute-done | bytes 65568 | tf_op jit(solution)/shard_map/ppermute | solution.py:239
  42.6 0.0 collective-permute-done.14
  42.7 6.0 %collective-permute-start.15 = (f32[1024,256]{1,0:T(8,128)S(1)}, f32[1024,256]{1,0:T(8,128)S(1)}, u32[]{:S(2)}, u32[]{:S(2)}) collective-permute-start(f32[1024,256]{1,0:T(8,128)S(1)} %constant_dynamic-update-slice_fusion.own_ref), channel_id=1, source_target_pairs={{0,1},{1,0},{2,3},{3,2},{4,5},{5,4},{6,7},{7,6},{8,9},{9,8},{10,11... | collective-permute-start | bytes 3145736 | tf_op jit(solution)/shard_map/ppermute | solution.py:247
  48.7 0.1 pad_add_fusion.place
  48.7 2.2 %collective-permute-done.15.other_ref = f32[1024,256]{1,0:T(8,128)S(1)} collective-permute-done((f32[1024,256]{1,0:T(8,128)S(1)}, f32[1024,256]{1,0:T(8,128)S(1)}, u32[]{:S(2)}, u32[]{:S(2)}) %collective-permute-start.15) | collective-permute-done | bytes 1048608 | tf_op jit(solution)/shard_map/ppermute | solution.py:247
  50.9 9.0 %product.1 = (bf16[1024,512]{1,0:T(8,128)(2,1)}, bf16[1024,512]{1,0:T(8,128)(2,1)}, f32[16,296,128]{2,1,0:T(8,128)S(1)}) custom-call(s32[3]{0:T(128)S(1)} %pad_add_fusion.place, f32[1024,256]{1,0:T(8,128)S(1)} %constant_dynamic-update-slice_fusion.own_ref, f32[1024,256]{1,0:T(8,128)S(1)} %collective-permute-done.15.other_ref, f32[1024,4,256]{2,1,0:T(4,128)} %a_ref.1, ...), custom_call_target="tpu_custom_call" | custom-call | tf_op jit(solution)/shard_map/product/pallas_call | solution.py:286
  60.0 37.9 %all_to_all.15.terms_ref = f32[16,296,128]{2,1,0:T(8,128)S(1)} all-to-all(f32[16,296,128]{2,1,0:T(8,128)S(1)} %get-tuple-element.26), channel_id=1, replica_groups=mesh['row'=16,'col'=16] {'row'}, dimensions={0} | all-to-all | bytes 4849664 | tf_op jit(solution)/shard_map/all_to_all | solution.py:243
  97.9 2.1 %total.1 = (f32[16,40,128]{2,1,0:T(8,128)S(1)}, f32[16,256,128]{2,1,0:T(8,128)}) custom-call(s32[3]{0:T(128)S(1)} %pad_add_fusion.place, f32[16,296,128]{2,1,0:T(8,128)S(1)} %all_to_all.15.terms_ref), custom_call_target="tpu_custom_call" | custom-call | tf_op jit(solution)/shard_map/total/pallas_call | solution.py:298
  100.0 11.2 %all_to_all.16.own_ref = f32[16,40,128]{2,1,0:T(8,128)S(1)} all-to-all(f32[16,40,128]{2,1,0:T(8,128)S(1)} %get-tuple-element.27), channel_id=1, replica_groups=mesh['row'=16,'col'=16] {'row'}, dimensions={0} | all-to-all | bytes 655360 | tf_op jit(solution)/shard_map/all_to_all | solution.py:243
  111.2 3.7 %all-to-all-start.2 = ((f32[16,256,128]{2,1,0:T(8,128)}), f32[16,256,128]{2,1,0:T(8,128)S(1)}, u32[]{:S(2)}, u32[]{:S(2)}) async-start(f32[16,256,128]{2,1,0:T(8,128)} %get-tuple-element.33), calls=%async_computation.2 | async-start | bytes 4194304 | tf_op jit(solution)/shard_map/all_to_all | solution.py:243
  114.9 2.5 %collective-permute-start.16 = (f32[16,40,128]{2,1,0:T(8,128)S(1)}, f32[16,40,128]{2,1,0:T(8,128)S(1)}, u32[]{:S(2)}, u32[]{:S(2)}) collective-permute-start(f32[16,40,128]{2,1,0:T(8,128)S(1)} %all_to_all.16.own_ref), channel_id=1, source_target_pairs={{0,1},{1,0},{2,3},{3,2},{4,5},{5,4},{6,7},{7,6},{8,9},{9,8},{10,11... | collective-permute-start | bytes 983048 | tf_op jit(solution)/shard_map/ppermute | solution.py:247
  117.4 1.3 collective-permute-done.16.other_ref
  118.6 27.3 %factor.1 = (f32[512,512]{1,0:T(8,128)S(1)}, bf16[1024,512]{1,0:T(8,128)(2,1)}, bf16[1024,512]{1,0:T(8,128)(2,1)}) custom-call(s32[3]{0:T(128)S(1)} %pad_add_fusion.place, f32[16,40,128]{2,1,0:T(8,128)S(1)} %all_to_all.16.own_ref, f32[16,40,128]{2,1,0:T(8,128)S(1)} %collective-permute-done.16.other_ref, bf16[1024,512]{1,0:T(8,128)(2,1)} %get-tuple-element.28.high_ref, ...), custom_call_target="tpu_custom_call" | custom-call | tf_op jit(solution)/shard_map/factor/pallas_call | solution.py:307
  145.9 0.0 all-to-all-done.2.w_ref
  145.9 11.7 %remainder.1 = (f32[512,4,256]{2,1,0:T(4,128)}, f32[1024,4,256]{2,1,0:T(4,128)}) custom-call(s32[3]{0:T(128)S(1)} %pad_add_fusion.place, bf16[1024,512]{1,0:T(8,128)(2,1)} %get-tuple-element.30.qh_ref, bf16[1024,512]{1,0:T(8,128)(2,1)} %get-tuple-element.31.ql_ref, f32[1024,4,256]{2,1,0:T(4,128)} %a_ref.1, f32[512,512]{1,0:T(8,128)S(1)} %get-tuple-element.32.m_ref, ...), custom_call_target="tpu_custom_call" | custom-call | tf_op jit(solution)/shard_map/remainder/pallas_call | solution.py:316
  (11 shorter events, 0.1 us)
Async XLA Ops:
  3.0 12.9 %collective-permute-start = (f32[128,256]{1,0:T(8,128)}, f32[128,256]{1,0:T(8,128)S(1)}, u32[]{:S(2)}, u32[]{:S(2)}) collective-permute-start(f32[128,256]{1,0:T(8,128)} %get-tuple-element.19), channel_id=1, source_target_pairs={{0,2},{1,3},{16,18},{17,19},{32,34},{33,35},{48,50},{49,51},{64,66... | collective-permute-start | bytes 393224 | tf_op jit(solution)/shard_map/ppermute | solution.py:253
  7.3 9.8 %collective-permute-start.1 = (f32[128,256]{1,0:T(8,128)}, f32[128,256]{1,0:T(8,128)S(1)}, u32[]{:S(2)}, u32[]{:S(2)}) collective-permute-start(f32[128,256]{1,0:T(8,128)} %get-tuple-element.20), channel_id=1, source_target_pairs={{0,14},{1,15},{16,30},{17,31},{32,46},{33,47},{48,62},{49,63},{64,... | collective-permute-start | bytes 393224 | tf_op jit(solution)/shard_map/ppermute | solution.py:253
  12.0 6.6 %collective-permute-start.2 = (f32[128,256]{1,0:T(8,128)}, f32[128,256]{1,0:T(8,128)S(1)}, u32[]{:S(2)}, u32[]{:S(2)}) collective-permute-start(f32[128,256]{1,0:T(8,128)} %get-tuple-element.21), channel_id=1, source_target_pairs={{0,4},{1,5},{16,20},{17,21},{32,36},{33,37},{48,52},{49,53},{64,68... | collective-permute-start | bytes 393224 | tf_op jit(solution)/shard_map/ppermute | solution.py:253
  13.3 5.3 %collective-permute-start.3 = (f32[128,256]{1,0:T(8,128)}, f32[128,256]{1,0:T(8,128)S(1)}, u32[]{:S(2)}, u32[]{:S(2)}) collective-permute-start(f32[128,256]{1,0:T(8,128)} %get-tuple-element.22), channel_id=1, source_target_pairs={{0,12},{1,13},{16,28},{17,29},{32,44},{33,45},{48,60},{49,61},{64,... | collective-permute-start | bytes 393224 | tf_op jit(solution)/shard_map/ppermute | solution.py:253
  14.6 4.2 %collective-permute-start.4 = (f32[128,256]{1,0:T(8,128)}, f32[128,256]{1,0:T(8,128)S(1)}, u32[]{:S(2)}, u32[]{:S(2)}) collective-permute-start(f32[128,256]{1,0:T(8,128)} %get-tuple-element.23), channel_id=1, source_target_pairs={{0,8},{1,9},{16,24},{17,25},{32,40},{33,41},{48,56},{49,57},{64,72... | collective-permute-start | bytes 393224 | tf_op jit(solution)/shard_map/ppermute | solution.py:253
  15.9 5.7 %collective-permute-start.5 = (f32[128,256]{1,0:T(8,128)}, f32[128,256]{1,0:T(8,128)S(1)}, u32[]{:S(2)}, u32[]{:S(2)}) collective-permute-start(f32[128,256]{1,0:T(8,128)} %get-tuple-element.24), channel_id=1, source_target_pairs={{0,6},{1,7},{16,22},{17,23},{32,38},{33,39},{48,54},{49,55},{64,70... | collective-permute-start | bytes 393224 | tf_op jit(solution)/shard_map/ppermute | solution.py:253
  17.2 4.4 %collective-permute-start.6 = (f32[128,256]{1,0:T(8,128)}, f32[128,256]{1,0:T(8,128)S(1)}, u32[]{:S(2)}, u32[]{:S(2)}) collective-permute-start(f32[128,256]{1,0:T(8,128)} %get-tuple-element.25), channel_id=1, source_target_pairs={{0,10},{1,11},{16,26},{17,27},{32,42},{33,43},{48,58},{49,59},{64,... | collective-permute-start | bytes 393224 | tf_op jit(solution)/shard_map/ppermute | solution.py:253
  22.6 5.1 %collective-permute-start.10 = (f32[128,256]{1,0:T(8,128)S(1)}, f32[128,256]{1,0:T(8,128)S(1)}, u32[]{:S(2)}, u32[]{:S(2)}) collective-permute-start(f32[128,256]{1,0:T(8,128)S(1)} %add_add_fusion), channel_id=1, source_target_pairs={{0,2},{1,3},{2,4},{3,5},{4,6},{5,7},{6,8},{7,9},{8,10},{9,11},{10,... | collective-permute-start | bytes 393224 | tf_op jit(solution)/shard_map/ppermute | solution.py:239
  22.7 5.0 %collective-permute-start.7 = (f32[128,256]{1,0:T(8,128)S(1)}, f32[128,256]{1,0:T(8,128)S(1)}, u32[]{:S(2)}, u32[]{:S(2)}) collective-permute-start(f32[128,256]{1,0:T(8,128)S(1)} %add_add_fusion), channel_id=1, source_target_pairs={{0,14},{1,15},{2,0},{3,1},{4,2},{5,3},{6,4},{7,5},{8,6},{9,7},{10,... | collective-permute-start | bytes 393224 | tf_op jit(solution)/shard_map/ppermute | solution.py:239
  27.7 5.0 %collective-permute-start.11 = (f32[128,256]{1,0:T(8,128)S(1)}, f32[128,256]{1,0:T(8,128)S(1)}, u32[]{:S(2)}, u32[]{:S(2)}) collective-permute-start(f32[128,256]{1,0:T(8,128)S(1)} %collective-permute-done.10), channel_id=1, source_target_pairs={{0,2},{1,3},{2,4},{3,5},{4,6},{5,7},{6,8},{7,9},{8,10},{9,11},{10,... | collective-permute-start | bytes 393224 | tf_op jit(solution)/shard_map/ppermute | solution.py:239
  27.7 5.0 %collective-permute-start.8 = (f32[128,256]{1,0:T(8,128)S(1)}, f32[128,256]{1,0:T(8,128)S(1)}, u32[]{:S(2)}, u32[]{:S(2)}) collective-permute-start(f32[128,256]{1,0:T(8,128)S(1)} %collective-permute-done.7), channel_id=1, source_target_pairs={{0,14},{1,15},{2,0},{3,1},{4,2},{5,3},{6,4},{7,5},{8,6},{9,7},{10,... | collective-permute-start | bytes 393224 | tf_op jit(solution)/shard_map/ppermute | solution.py:239
  32.7 5.0 %collective-permute-start.12 = (f32[128,256]{1,0:T(8,128)S(1)}, f32[128,256]{1,0:T(8,128)S(1)}, u32[]{:S(2)}, u32[]{:S(2)}) collective-permute-start(f32[128,256]{1,0:T(8,128)S(1)} %collective-permute-done.11), channel_id=1, source_target_pairs={{0,2},{1,3},{2,4},{3,5},{4,6},{5,7},{6,8},{7,9},{8,10},{9,11},{10,... | collective-permute-start | bytes 393224 | tf_op jit(solution)/shard_map/ppermute | solution.py:239
  32.7 5.0 %collective-permute-start.9 = (f32[128,256]{1,0:T(8,128)S(1)}, f32[128,256]{1,0:T(8,128)S(1)}, u32[]{:S(2)}, u32[]{:S(2)}) collective-permute-start(f32[128,256]{1,0:T(8,128)S(1)} %collective-permute-done.8), channel_id=1, source_target_pairs={{0,14},{1,15},{2,0},{3,1},{4,2},{5,3},{6,4},{7,5},{8,6},{9,7},{10,... | collective-permute-start | bytes 393224 | tf_op jit(solution)/shard_map/ppermute | solution.py:239
  37.7 4.9 %collective-permute-start.13 = (f32[64,256]{1,0:T(8,128)S(1)}, f32[64,256]{1,0:T(8,128)S(1)}, u32[]{:S(2)}, u32[]{:S(2)}) collective-permute-start(f32[64,256]{1,0:T(8,128)S(1)} %slice.8), channel_id=1, source_target_pairs={{0,2},{1,3},{2,4},{3,5},{4,6},{5,7},{6,8},{7,9},{8,10},{9,11},{10,... | collective-permute-start | bytes 196616 | tf_op jit(solution)/shard_map/ppermute | solution.py:239
  37.8 4.9 %collective-permute-start.14 = (f32[64,256]{1,0:T(8,128)S(1)}, f32[64,256]{1,0:T(8,128)S(1)}, u32[]{:S(2)}, u32[]{:S(2)}) collective-permute-start(f32[64,256]{1,0:T(8,128)S(1)} %slice.9), channel_id=1, source_target_pairs={{0,14},{1,15},{2,0},{3,1},{4,2},{5,3},{6,4},{7,5},{8,6},{9,7},{10,... | collective-permute-start | bytes 196616 | tf_op jit(solution)/shard_map/ppermute | solution.py:239
  42.7 8.3 %collective-permute-start.15 = (f32[1024,256]{1,0:T(8,128)S(1)}, f32[1024,256]{1,0:T(8,128)S(1)}, u32[]{:S(2)}, u32[]{:S(2)}) collective-permute-start(f32[1024,256]{1,0:T(8,128)S(1)} %constant_dynamic-update-slice_fusion.own_ref), channel_id=1, source_target_pairs={{0,1},{1,0},{2,3},{3,2},{4,5},{5,4},{6,7},{7,6},{8,9},{9,8},{10,11... | collective-permute-start | bytes 3145736 | tf_op jit(solution)/shard_map/ppermute | solution.py:247
  111.2 34.7 %all-to-all-start.2 = ((f32[16,256,128]{2,1,0:T(8,128)}), f32[16,256,128]{2,1,0:T(8,128)S(1)}, u32[]{:S(2)}, u32[]{:S(2)}) async-start(f32[16,256,128]{2,1,0:T(8,128)} %get-tuple-element.33), calls=%async_computation.2 | async-start | bytes 4194304 | tf_op jit(solution)/shard_map/all_to_all | solution.py:243
  114.9 3.7 %collective-permute-start.16 = (f32[16,40,128]{2,1,0:T(8,128)S(1)}, f32[16,40,128]{2,1,0:T(8,128)S(1)}, u32[]{:S(2)}, u32[]{:S(2)}) collective-permute-start(f32[16,40,128]{2,1,0:T(8,128)S(1)} %all_to_all.16.own_ref), channel_id=1, source_target_pairs={{0,1},{1,0},{2,3},{3,2},{4,5},{5,4},{6,7},{7,6},{8,9},{9,8},{10,11... | collective-permute-start | bytes 983048 | tf_op jit(solution)/shard_map/ppermute | solution.py:247

commit v6 on v5

--- a/solution.py
+++ b/solution.py
@@ -112,7 +112,7 @@
     own, other = own_ref[...], other_ref[...]
     panel = split(jnp.concatenate([jnp.where(first, own, other), jnp.where(first, other, own)], axis=1))
     high_ref[...], low_ref[...] = panel
-    gram_ref[...] += three_pass(panel, panel, by_rows)
+    gram_ref[...] += three_pass(panel, panel, by_rows) + one_pass(panel[1], panel[1], by_rows)
     for l in range(a0_ref.shape[1]):
         a = split(jnp.concatenate([a0_ref[:, l, :], a1_ref[:, l, :]], axis=0))
         part = three_pass(panel, a, by_rows)
@@ -164,11 +164,11 @@
         if j:
             done = j - 1
             for i in range(j, NB):
-                t_ref[i, :, :d] -= mm(low[i], m_ref[done * TILE : d, :d], plain)
+                t_ref[i, :, :d] -= three_pass(split(low[i]), split(m_ref[done * TILE : d, :d]), plain)
                 for k in range(j, i + 1):
                     if i > j:
                         update(done, i, k)
-            m_ref[d : d + TILE, :d] = mm(mj, t_ref[j, :, :d], plain)
+            m_ref[d : d + TILE, :d] = three_pass(split(mj), split(t_ref[j, :, :d]), plain)
         m_ref[d : d + TILE, d : d + TILE] = mj
         if j + 1 < NB:
             m_ref[d : d + TILE, d + TILE :] = jnp.zeros((TILE, FULL - d - TILE), jnp.float32)
@@ -187,24 +187,30 @@
             ql_ref[spot, :] = q[1][e * PIECE : (e + 1) * PIECE]
 
 
-def remainder_kernel(place, qh_ref, ql_ref, a_ref, m_ref, w_ref, coeff_ref, out_ref, ch_ref, cl_ref):
+def remainder_kernel(place, qh_ref, ql_ref, a_ref, m_ref, w_ref, coeff_ref, out_ref, ch_ref, cl_ref, c_ref, sem):
     width = a_ref.shape[2]
     each = width // TILE
+    copy = pltpu.make_async_copy(c_ref, coeff_ref, sem)
 
     @pl.when(pl.program_id(0) == 0)
     def _():
         factor = split(m_ref[...])
-        for l in range(coeff_ref.shape[1]):
+        for l in range(c_ref.shape[1]):
             tiles = [w_ref[:, t * SHARE : (t + 1) * SHARE, :].reshape(FULL, TILE) for t in range(l * each, (l + 1) * each)]
             coeffs = three_pass(factor, split(jnp.concatenate(tiles, axis=1)), plain)
-            coeff_ref[:, l, :] = coeffs
+            c_ref[:, l, :] = coeffs
             window = slice(l * width, (l + 1) * width)
             ch_ref[:, window], cl_ref[:, window] = split(coeffs)
+        copy.start()
 
     q = qh_ref[...], ql_ref[...]
     for l in range(a_ref.shape[1]):
         window = slice(l * width, (l + 1) * width)
         out_ref[:, l, :] = a_ref[:, l, :] - three_pass(q, (ch_ref[:, window], cl_ref[:, window]), plain)
+
+    @pl.when(pl.program_id(0) == pl.num_programs(0) - 1)
+    def _():
+        copy.wait()
 
 
 def call(kernel, name, mib, grid, ins, outs, out_shape, scratch=()):
@@ -316,9 +322,10 @@
     return call(
         remainder_kernel, "remainder", 22, (steps,),
         [panel_spec, panel_spec, a_spec, whole(FULL, FULL), whole(PEERS, share_rows, TILE)],
-        [whole(FULL, blocks, width), a_spec],
+        [pl.BlockSpec(memory_space=pl.ANY), a_spec],
         [f32(FULL, blocks, width), f32(rows, blocks, width)],
-        [pltpu.VMEM((FULL, blocks * width), jnp.bfloat16)] * 2,
+        [pltpu.VMEM((FULL, blocks * width), jnp.bfloat16)] * 2
+        + [pltpu.VMEM((FULL, blocks, width), jnp.float32), pltpu.SemaphoreType.DMA],
     )(place, *in_hbm(qh, ql, matrix), m, sums)
 
 

time: 158 us -> 158 us (level)
  no operation moved by 1% of the time
where the time goes in v6:
time: 158 us
  Pallas kernels  52.6 us (33%)
  blocking collectives  49.1 us (31%)
  starting transfers between devices  38.5 us (24%)
  waiting for transfers between devices  15.6 us (10%)
    all_to_all x2, blocking collectives, exchange(): return lax.all_to_all(x, 'row', 0, 0)  49.1 us
    pallas_call x1, Pallas kernels, on_device(): call(factor_kernel, 'factor', 20, (1,), [whole(PEERS, TILES * 8, TILE)] *...  27.1 us
    ppermute x7, starting transfers between devices, share_panel(): own = own + lax.ppermute(mine[k], 'col', [(0, 2 * k), (1, 2 * k + 1)])  15.5 us
    pallas_call x1, Pallas kernels, on_device(): call(remainder_kernel, 'remainder', 22, (steps,), [panel_spec, panel_spec...  11.5 us
    ppermute x8, starting transfers between devices, shift(): return lax.ppermute(x, axis, [(i, (i + by) % PEERS) for i in range(PEERS)])  10.8 us
    pallas_call x1, Pallas kernels, on_device(): call(product_kernel, 'product', 20, (steps,), [own_spec, own_spec] + [pl....  9.52 us
    ppermute x8, waiting for transfers between devices, shift(): return lax.ppermute(x, axis, [(i, (i + by) % PEERS) for i in range(PEERS)])  9.11 us
    ppermute x2, starting transfers between devices, swap_cores(): return lax.ppermute(x, 'col', [(i, i ^ 1) for i in range(PEERS)])  8.45 us
  transfers between devices with their start and end apart: 18, of which 8 were waited for; matrix products, arithmetic and copies ran while one was open for 0% of the time, Pallas kernels for 17%

profile of v6, /device:TPU:1, one launch (start us, length us, event | category | flops | bytes accessed | tf_op | source)
XLA Modules:
  0.0 158.0 jit_solution(14226603692660983165)
XLA Ops:
  0.6 2.3 %panel.1 = (f32[128,256]{1,0:T(8,128)}, f32[128,256]{1,0:T(8,128)}, f32[128,256]{1,0:T(8,128)}, f32[128,256]{1,0:T(8,128)}, f32[128,256]{1,0:T(8,128)}, /*index=...) custom-call(f32[1024,4,256]{2,1,0:T(4,128)} %a_ref.1), custom_call_target="tpu_custom_call" | custom-call | tf_op jit(solution)/shard_map/panel/pallas_call | solution.py:276
  3.0 4.4 %collective-permute-start = (f32[128,256]{1,0:T(8,128)}, f32[128,256]{1,0:T(8,128)S(1)}, u32[]{:S(2)}, u32[]{:S(2)}) collective-permute-start(f32[128,256]{1,0:T(8,128)} %get-tuple-element.19), channel_id=1, source_target_pairs={{0,2},{1,3},{16,18},{17,19},{32,34},{33,35},{48,50},{49,51},{64,66... | collective-permute-start | bytes 393224 | tf_op jit(solution)/shard_map/ppermute | solution.py:259
  7.3 4.6 %collective-permute-start.1 = (f32[128,256]{1,0:T(8,128)}, f32[128,256]{1,0:T(8,128)S(1)}, u32[]{:S(2)}, u32[]{:S(2)}) collective-permute-start(f32[128,256]{1,0:T(8,128)} %get-tuple-element.20), channel_id=1, source_target_pairs={{0,14},{1,15},{16,30},{17,31},{32,46},{33,47},{48,62},{49,63},{64,... | collective-permute-start | bytes 393224 | tf_op jit(solution)/shard_map/ppermute | solution.py:259
  12.0 1.3 collective-permute-start.2
  13.3 1.3 collective-permute-start.3
  14.6 1.3 collective-permute-start.4
  15.9 0.0 collective-permute-done
  15.9 1.3 collective-permute-start.5
  17.2 0.0 collective-permute-done.1
  17.2 1.3 collective-permute-start.6
  18.5 0.0 collective-permute-done.2
  18.5 0.0 collective-permute-done.3
  18.5 0.2 collective-permute-done.4
  18.7 2.9 %collective-permute-done.5 = f32[128,256]{1,0:T(8,128)S(1)} collective-permute-done((f32[128,256]{1,0:T(8,128)}, f32[128,256]{1,0:T(8,128)S(1)}, u32[]{:S(2)}, u32[]{:S(2)}) %collective-permute-start.5) | collective-permute-done | bytes 131104 | tf_op jit(solution)/shard_map/ppermute | solution.py:259
  21.6 0.0 collective-permute-done.6
  21.6 1.0 add_add_fusion
  22.6 0.1 collective-permute-start.10
  22.7 2.7 %collective-permute-start.7 = (f32[128,256]{1,0:T(8,128)S(1)}, f32[128,256]{1,0:T(8,128)S(1)}, u32[]{:S(2)}, u32[]{:S(2)}) collective-permute-start(f32[128,256]{1,0:T(8,128)S(1)} %add_add_fusion), channel_id=1, source_target_pairs={{0,14},{1,15},{2,0},{3,1},{4,2},{5,3},{6,4},{7,5},{8,6},{9,7},{10,... | collective-permute-start | bytes 393224 | tf_op jit(solution)/shard_map/ppermute | solution.py:245
  25.3 2.4 %collective-permute-done.10 = f32[128,256]{1,0:T(8,128)S(1)} collective-permute-done((f32[128,256]{1,0:T(8,128)S(1)}, f32[128,256]{1,0:T(8,128)S(1)}, u32[]{:S(2)}, u32[]{:S(2)}) %collective-permute-start.10) | collective-permute-done | bytes 131104 | tf_op jit(solution)/shard_map/ppermute | solution.py:245
  27.7 0.0 collective-permute-start.11
  27.7 0.0 collective-permute-done.7
  27.7 2.7 %collective-permute-start.8 = (f32[128,256]{1,0:T(8,128)S(1)}, f32[128,256]{1,0:T(8,128)S(1)}, u32[]{:S(2)}, u32[]{:S(2)}) collective-permute-start(f32[128,256]{1,0:T(8,128)S(1)} %collective-permute-done.7), channel_id=1, source_target_pairs={{0,14},{1,15},{2,0},{3,1},{4,2},{5,3},{6,4},{7,5},{8,6},{9,7},{10,... | collective-permute-start | bytes 393224 | tf_op jit(solution)/shard_map/ppermute | solution.py:245
  30.4 2.3 %collective-permute-done.11 = f32[128,256]{1,0:T(8,128)S(1)} collective-permute-done((f32[128,256]{1,0:T(8,128)S(1)}, f32[128,256]{1,0:T(8,128)S(1)}, u32[]{:S(2)}, u32[]{:S(2)}) %collective-permute-start.11) | collective-permute-done | bytes 131104 | tf_op jit(solution)/shard_map/ppermute | solution.py:245
  32.7 0.0 collective-permute-start.12
  32.7 0.0 collective-permute-done.8
  32.7 2.7 %collective-permute-start.9 = (f32[128,256]{1,0:T(8,128)S(1)}, f32[128,256]{1,0:T(8,128)S(1)}, u32[]{:S(2)}, u32[]{:S(2)}) collective-permute-start(f32[128,256]{1,0:T(8,128)S(1)} %collective-permute-done.8), channel_id=1, source_target_pairs={{0,14},{1,15},{2,0},{3,1},{4,2},{5,3},{6,4},{7,5},{8,6},{9,7},{10,... | collective-permute-start | bytes 393224 | tf_op jit(solution)/shard_map/ppermute | solution.py:245
  35.4 2.3 %collective-permute-done.12 = f32[128,256]{1,0:T(8,128)S(1)} collective-permute-done((f32[128,256]{1,0:T(8,128)S(1)}, f32[128,256]{1,0:T(8,128)S(1)}, u32[]{:S(2)}, u32[]{:S(2)}) %collective-permute-start.12) | collective-permute-done | bytes 131104 | tf_op jit(solution)/shard_map/ppermute | solution.py:245
  37.7 0.0 collective-permute-start.13
  37.7 0.0 collective-permute-done.9
  37.8 2.7 %collective-permute-start.14 = (f32[64,256]{1,0:T(8,128)S(1)}, f32[64,256]{1,0:T(8,128)S(1)}, u32[]{:S(2)}, u32[]{:S(2)}) collective-permute-start(f32[64,256]{1,0:T(8,128)S(1)} %slice.9), channel_id=1, source_target_pairs={{0,14},{1,15},{2,0},{3,1},{4,2},{5,3},{6,4},{7,5},{8,6},{9,7},{10,... | collective-permute-start | bytes 196616 | tf_op jit(solution)/shard_map/ppermute | solution.py:245
  40.5 2.1 %collective-permute-done.13 = f32[64,256]{1,0:T(8,128)S(1)} collective-permute-done((f32[64,256]{1,0:T(8,128)S(1)}, f32[64,256]{1,0:T(8,128)S(1)}, u32[]{:S(2)}, u32[]{:S(2)}) %collective-permute-start.13) | collective-permute-done | bytes 65568 | tf_op jit(solution)/shard_map/ppermute | solution.py:245
  42.6 0.0 collective-permute-done.14
  42.7 6.0 %collective-permute-start.15 = (f32[1024,256]{1,0:T(8,128)S(1)}, f32[1024,256]{1,0:T(8,128)S(1)}, u32[]{:S(2)}, u32[]{:S(2)}) collective-permute-start(f32[1024,256]{1,0:T(8,128)S(1)} %constant_dynamic-update-slice_fusion.own_ref), channel_id=1, source_target_pairs={{0,1},{1,0},{2,3},{3,2},{4,5},{5,4},{6,7},{7,6},{8,9},{9,8},{10,11... | collective-permute-start | bytes 3145736 | tf_op jit(solution)/shard_map/ppermute | solution.py:253
  48.7 0.1 pad_add_fusion.place
  48.7 2.2 %collective-permute-done.15.other_ref = f32[1024,256]{1,0:T(8,128)S(1)} collective-permute-done((f32[1024,256]{1,0:T(8,128)S(1)}, f32[1024,256]{1,0:T(8,128)S(1)}, u32[]{:S(2)}, u32[]{:S(2)}) %collective-permute-start.15) | collective-permute-done | bytes 1048608 | tf_op jit(solution)/shard_map/ppermute | solution.py:253
  50.9 9.5 %product.1 = (bf16[1024,512]{1,0:T(8,128)(2,1)}, bf16[1024,512]{1,0:T(8,128)(2,1)}, f32[16,296,128]{2,1,0:T(8,128)S(1)}) custom-call(s32[3]{0:T(128)S(1)} %pad_add_fusion.place, f32[1024,256]{1,0:T(8,128)S(1)} %constant_dynamic-update-slice_fusion.own_ref, f32[1024,256]{1,0:T(8,128)S(1)} %collective-permute-done.15.other_ref, f32[1024,4,256]{2,1,0:T(4,128)} %a_ref.1, ...), custom_call_target="tpu_custom_call" | custom-call | tf_op jit(solution)/shard_map/product/pallas_call | solution.py:292
  60.5 37.9 %all_to_all.15.terms_ref = f32[16,296,128]{2,1,0:T(8,128)S(1)} all-to-all(f32[16,296,128]{2,1,0:T(8,128)S(1)} %get-tuple-element.26), channel_id=1, replica_groups=mesh['row'=16,'col'=16] {'row'}, dimensions={0} | all-to-all | bytes 4849664 | tf_op jit(solution)/shard_map/all_to_all | solution.py:249
  98.4 2.1 %total.1 = (f32[16,40,128]{2,1,0:T(8,128)S(1)}, f32[16,256,128]{2,1,0:T(8,128)}) custom-call(s32[3]{0:T(128)S(1)} %pad_add_fusion.place, f32[16,296,128]{2,1,0:T(8,128)S(1)} %all_to_all.15.terms_ref), custom_call_target="tpu_custom_call" | custom-call | tf_op jit(solution)/shard_map/total/pallas_call | solution.py:304
  100.4 11.2 %all_to_all.16.own_ref = f32[16,40,128]{2,1,0:T(8,128)S(1)} all-to-all(f32[16,40,128]{2,1,0:T(8,128)S(1)} %get-tuple-element.27), channel_id=1, replica_groups=mesh['row'=16,'col'=16] {'row'}, dimensions={0} | all-to-all | bytes 655360 | tf_op jit(solution)/shard_map/all_to_all | solution.py:249
  111.6 3.7 %all-to-all-start.2 = ((f32[16,256,128]{2,1,0:T(8,128)}), f32[16,256,128]{2,1,0:T(8,128)S(1)}, u32[]{:S(2)}, u32[]{:S(2)}) async-start(f32[16,256,128]{2,1,0:T(8,128)} %get-tuple-element.33), calls=%async_computation.2 | async-start | bytes 4194304 | tf_op jit(solution)/shard_map/all_to_all | solution.py:249
  115.4 2.5 %collective-permute-start.16 = (f32[16,40,128]{2,1,0:T(8,128)S(1)}, f32[16,40,128]{2,1,0:T(8,128)S(1)}, u32[]{:S(2)}, u32[]{:S(2)}) collective-permute-start(f32[16,40,128]{2,1,0:T(8,128)S(1)} %all_to_all.16.own_ref), channel_id=1, source_target_pairs={{0,1},{1,0},{2,3},{3,2},{4,5},{5,4},{6,7},{7,6},{8,9},{9,8},{10,11... | collective-permute-start | bytes 983048 | tf_op jit(solution)/shard_map/ppermute | solution.py:253
  117.9 1.3 collective-permute-done.16.other_ref
  119.1 27.1 %factor.1 = (f32[512,512]{1,0:T(8,128)S(1)}, bf16[1024,512]{1,0:T(8,128)(2,1)}, bf16[1024,512]{1,0:T(8,128)(2,1)}) custom-call(s32[3]{0:T(128)S(1)} %pad_add_fusion.place, f32[16,40,128]{2,1,0:T(8,128)S(1)} %all_to_all.16.own_ref, f32[16,40,128]{2,1,0:T(8,128)S(1)} %collective-permute-done.16.other_ref, bf16[1024,512]{1,0:T(8,128)(2,1)} %get-tuple-element.28.high_ref, ...), custom_call_target="tpu_custom_call" | custom-call | tf_op jit(solution)/shard_map/factor/pallas_call | solution.py:313
  146.3 0.0 all-to-all-done.2.w_ref
  146.3 11.5 %remainder.1 = (f32[512,4,256]{2,1,0:T(4,128)}, f32[1024,4,256]{2,1,0:T(4,128)}) custom-call(s32[3]{0:T(128)S(1)} %pad_add_fusion.place, bf16[1024,512]{1,0:T(8,128)(2,1)} %get-tuple-element.30.qh_ref, bf16[1024,512]{1,0:T(8,128)(2,1)} %get-tuple-element.31.ql_ref, f32[1024,4,256]{2,1,0:T(4,128)} %a_ref.1, f32[512,512]{1,0:T(8,128)S(1)} %get-tuple-element.32.m_ref, ...), custom_call_target="tpu_custom_call" | custom-call | tf_op jit(solution)/shard_map/remainder/pallas_call | solution.py:322
  (11 shorter events, 0.1 us)
Async XLA Ops:
  3.0 12.9 %collective-permute-start = (f32[128,256]{1,0:T(8,128)}, f32[128,256]{1,0:T(8,128)S(1)}, u32[]{:S(2)}, u32[]{:S(2)}) collective-permute-start(f32[128,256]{1,0:T(8,128)} %get-tuple-element.19), channel_id=1, source_target_pairs={{0,2},{1,3},{16,18},{17,19},{32,34},{33,35},{48,50},{49,51},{64,66... | collective-permute-start | bytes 393224 | tf_op jit(solution)/shard_map/ppermute | solution.py:259
  7.3 9.8 %collective-permute-start.1 = (f32[128,256]{1,0:T(8,128)}, f32[128,256]{1,0:T(8,128)S(1)}, u32[]{:S(2)}, u32[]{:S(2)}) collective-permute-start(f32[128,256]{1,0:T(8,128)} %get-tuple-element.20), channel_id=1, source_target_pairs={{0,14},{1,15},{16,30},{17,31},{32,46},{33,47},{48,62},{49,63},{64,... | collective-permute-start | bytes 393224 | tf_op jit(solution)/shard_map/ppermute | solution.py:259
  12.0 6.6 %collective-permute-start.2 = (f32[128,256]{1,0:T(8,128)}, f32[128,256]{1,0:T(8,128)S(1)}, u32[]{:S(2)}, u32[]{:S(2)}) collective-permute-start(f32[128,256]{1,0:T(8,128)} %get-tuple-element.21), channel_id=1, source_target_pairs={{0,4},{1,5},{16,20},{17,21},{32,36},{33,37},{48,52},{49,53},{64,68... | collective-permute-start | bytes 393224 | tf_op jit(solution)/shard_map/ppermute | solution.py:259
  13.3 5.3 %collective-permute-start.3 = (f32[128,256]{1,0:T(8,128)}, f32[128,256]{1,0:T(8,128)S(1)}, u32[]{:S(2)}, u32[]{:S(2)}) collective-permute-start(f32[128,256]{1,0:T(8,128)} %get-tuple-element.22), channel_id=1, source_target_pairs={{0,12},{1,13},{16,28},{17,29},{32,44},{33,45},{48,60},{49,61},{64,... | collective-permute-start | bytes 393224 | tf_op jit(solution)/shard_map/ppermute | solution.py:259
  14.6 4.2 %collective-permute-start.4 = (f32[128,256]{1,0:T(8,128)}, f32[128,256]{1,0:T(8,128)S(1)}, u32[]{:S(2)}, u32[]{:S(2)}) collective-permute-start(f32[128,256]{1,0:T(8,128)} %get-tuple-element.23), channel_id=1, source_target_pairs={{0,8},{1,9},{16,24},{17,25},{32,40},{33,41},{48,56},{49,57},{64,72... | collective-permute-start | bytes 393224 | tf_op jit(solution)/shard_map/ppermute | solution.py:259
  15.9 5.7 %collective-permute-start.5 = (f32[128,256]{1,0:T(8,128)}, f32[128,256]{1,0:T(8,128)S(1)}, u32[]{:S(2)}, u32[]{:S(2)}) collective-permute-start(f32[128,256]{1,0:T(8,128)} %get-tuple-element.24), channel_id=1, source_target_pairs={{0,6},{1,7},{16,22},{17,23},{32,38},{33,39},{48,54},{49,55},{64,70... | collective-permute-start | bytes 393224 | tf_op jit(solution)/shard_map/ppermute | solution.py:259
  17.2 4.4 %collective-permute-start.6 = (f32[128,256]{1,0:T(8,128)}, f32[128,256]{1,0:T(8,128)S(1)}, u32[]{:S(2)}, u32[]{:S(2)}) collective-permute-start(f32[128,256]{1,0:T(8,128)} %get-tuple-element.25), channel_id=1, source_target_pairs={{0,10},{1,11},{16,26},{17,27},{32,42},{33,43},{48,58},{49,59},{64,... | collective-permute-start | bytes 393224 | tf_op jit(solution)/shard_map/ppermute | solution.py:259
  22.6 5.1 %collective-permute-start.10 = (f32[128,256]{1,0:T(8,128)S(1)}, f32[128,256]{1,0:T(8,128)S(1)}, u32[]{:S(2)}, u32[]{:S(2)}) collective-permute-start(f32[128,256]{1,0:T(8,128)S(1)} %add_add_fusion), channel_id=1, source_target_pairs={{0,2},{1,3},{2,4},{3,5},{4,6},{5,7},{6,8},{7,9},{8,10},{9,11},{10,... | collective-permute-start | bytes 393224 | tf_op jit(solution)/shard_map/ppermute | solution.py:245
  22.7 5.0 %collective-permute-start.7 = (f32[128,256]{1,0:T(8,128)S(1)}, f32[128,256]{1,0:T(8,128)S(1)}, u32[]{:S(2)}, u32[]{:S(2)}) collective-permute-start(f32[128,256]{1,0:T(8,128)S(1)} %add_add_fusion), channel_id=1, source_target_pairs={{0,14},{1,15},{2,0},{3,1},{4,2},{5,3},{6,4},{7,5},{8,6},{9,7},{10,... | collective-permute-start | bytes 393224 | tf_op jit(solution)/shard_map/ppermute | solution.py:245
  27.7 5.0 %collective-permute-start.11 = (f32[128,256]{1,0:T(8,128)S(1)}, f32[128,256]{1,0:T(8,128)S(1)}, u32[]{:S(2)}, u32[]{:S(2)}) collective-permute-start(f32[128,256]{1,0:T(8,128)S(1)} %collective-permute-done.10), channel_id=1, source_target_pairs={{0,2},{1,3},{2,4},{3,5},{4,6},{5,7},{6,8},{7,9},{8,10},{9,11},{10,... | collective-permute-start | bytes 393224 | tf_op jit(solution)/shard_map/ppermute | solution.py:245
  27.7 5.0 %collective-permute-start.8 = (f32[128,256]{1,0:T(8,128)S(1)}, f32[128,256]{1,0:T(8,128)S(1)}, u32[]{:S(2)}, u32[]{:S(2)}) collective-permute-start(f32[128,256]{1,0:T(8,128)S(1)} %collective-permute-done.7), channel_id=1, source_target_pairs={{0,14},{1,15},{2,0},{3,1},{4,2},{5,3},{6,4},{7,5},{8,6},{9,7},{10,... | collective-permute-start | bytes 393224 | tf_op jit(solution)/shard_map/ppermute | solution.py:245
  32.7 5.0 %collective-permute-start.12 = (f32[128,256]{1,0:T(8,128)S(1)}, f32[128,256]{1,0:T(8,128)S(1)}, u32[]{:S(2)}, u32[]{:S(2)}) collective-permute-start(f32[128,256]{1,0:T(8,128)S(1)} %collective-permute-done.11), channel_id=1, source_target_pairs={{0,2},{1,3},{2,4},{3,5},{4,6},{5,7},{6,8},{7,9},{8,10},{9,11},{10,... | collective-permute-start | bytes 393224 | tf_op jit(solution)/shard_map/ppermute | solution.py:245
  32.7 5.0 %collective-permute-start.9 = (f32[128,256]{1,0:T(8,128)S(1)}, f32[128,256]{1,0:T(8,128)S(1)}, u32[]{:S(2)}, u32[]{:S(2)}) collective-permute-start(f32[128,256]{1,0:T(8,128)S(1)} %collective-permute-done.8), channel_id=1, source_target_pairs={{0,14},{1,15},{2,0},{3,1},{4,2},{5,3},{6,4},{7,5},{8,6},{9,7},{10,... | collective-permute-start | bytes 393224 | tf_op jit(solution)/shard_map/ppermute | solution.py:245
  37.7 4.9 %collective-permute-start.13 = (f32[64,256]{1,0:T(8,128)S(1)}, f32[64,256]{1,0:T(8,128)S(1)}, u32[]{:S(2)}, u32[]{:S(2)}) collective-permute-start(f32[64,256]{1,0:T(8,128)S(1)} %slice.8), channel_id=1, source_target_pairs={{0,2},{1,3},{2,4},{3,5},{4,6},{5,7},{6,8},{7,9},{8,10},{9,11},{10,... | collective-permute-start | bytes 196616 | tf_op jit(solution)/shard_map/ppermute | solution.py:245
  37.8 4.9 %collective-permute-start.14 = (f32[64,256]{1,0:T(8,128)S(1)}, f32[64,256]{1,0:T(8,128)S(1)}, u32[]{:S(2)}, u32[]{:S(2)}) collective-permute-start(f32[64,256]{1,0:T(8,128)S(1)} %slice.9), channel_id=1, source_target_pairs={{0,14},{1,15},{2,0},{3,1},{4,2},{5,3},{6,4},{7,5},{8,6},{9,7},{10,... | collective-permute-start | bytes 196616 | tf_op jit(solution)/shard_map/ppermute | solution.py:245
  42.7 8.3 %collective-permute-start.15 = (f32[1024,256]{1,0:T(8,128)S(1)}, f32[1024,256]{1,0:T(8,128)S(1)}, u32[]{:S(2)}, u32[]{:S(2)}) collective-permute-start(f32[1024,256]{1,0:T(8,128)S(1)} %constant_dynamic-update-slice_fusion.own_ref), channel_id=1, source_target_pairs={{0,1},{1,0},{2,3},{3,2},{4,5},{5,4},{6,7},{7,6},{8,9},{9,8},{10,11... | collective-permute-start | bytes 3145736 | tf_op jit(solution)/shard_map/ppermute | solution.py:253
  111.6 34.6 %all-to-all-start.2 = ((f32[16,256,128]{2,1,0:T(8,128)}), f32[16,256,128]{2,1,0:T(8,128)S(1)}, u32[]{:S(2)}, u32[]{:S(2)}) async-start(f32[16,256,128]{2,1,0:T(8,128)} %get-tuple-element.33), calls=%async_computation.2 | async-start | bytes 4194304 | tf_op jit(solution)/shard_map/all_to_all | solution.py:249
  115.4 3.7 %collective-permute-start.16 = (f32[16,40,128]{2,1,0:T(8,128)S(1)}, f32[16,40,128]{2,1,0:T(8,128)S(1)}, u32[]{:S(2)}, u32[]{:S(2)}) collective-permute-start(f32[16,40,128]{2,1,0:T(8,128)S(1)} %all_to_all.16.own_ref), channel_id=1, source_target_pairs={{0,1},{1,0},{2,3},{3,2},{4,5},{5,4},{6,7},{7,6},{8,9},{9,8},{10,11... | collective-permute-start | bytes 983048 | tf_op jit(solution)/shard_map/ppermute | solution.py:253

commit v7 on v6

--- a/solution.py
+++ b/solution.py
@@ -13,6 +13,8 @@
 PEERS = 16
 DEPTH = 8
 PIECE = 128
+NEAR = (1, 7)
+FAR = (2, 6, 4, 3, 5, 0)
 HALF = ((0, 0), (1, 0), (1, 1), (2, 0), (2, 1)), ((2, 2), (3, 0), (3, 1), (3, 2), (3, 3))
 HALF_ROWS = len(HALF[0]) * TILE
 SHARE = FULL // PEERS
@@ -89,15 +91,28 @@
     return one_pass(a[0], b[0], dims) + (one_pass(a[0], b[1], dims) + one_pass(a[1], b[0], dims))
 
 
-def panel_kernel(matrix_ref, *refs):
-    outs, sems = refs[:-1], refs[-1]
-    copies = [
-        pltpu.make_async_copy(matrix_ref.at[k * PIECE : (k + 1) * PIECE, 0, :], out, sems.at[k]) for k, out in enumerate(outs)
-    ]
-    for copy in copies:
-        copy.start()
-    for copy in copies:
-        copy.wait()
+def panel_rows(matrix, pieces):
+    rows, blocks, width = matrix.shape
+
+    def kernel(matrix_ref, *refs):
+        copies = [
+            pltpu.make_async_copy(matrix_ref.at[k * PIECE : (k + 1) * PIECE, 0, :], out, refs[-1].at[i])
+            for i, (k, out) in enumerate(zip(pieces, refs[:-1]))
+        ]
+        for copy in copies:
+            copy.start()
+        for copy in copies:
+            copy.wait()
+
+    outs = pl.pallas_call(
+        kernel,
+        in_specs=[pl.BlockSpec(memory_space=pl.ANY)],
+        out_specs=[pl.BlockSpec(memory_space=pltpu.VMEM)] * len(pieces),
+        out_shape=[f32(PIECE, width)] * len(pieces),
+        scratch_shapes=[pltpu.SemaphoreType.DMA((len(pieces),))],
+        name="panel",
+    )(*in_hbm(matrix))
+    return dict(zip(pieces, outs))
 
 
 def product_kernel(place, own_ref, other_ref, a0_ref, a1_ref, high_ref, low_ref, terms_ref, gram_ref):
@@ -255,7 +270,7 @@
 
 def share_panel(mine, z):
     own = jnp.where(z == 0, mine[0], jnp.zeros((PIECE, BLOCK), jnp.float32))
-    for k in (1, 7, 2, 6, 4, 3, 5):
+    for k in NEAR + FAR[:-1]:
         own = own + lax.ppermute(mine[k], "col", [(0, 2 * k), (1, 2 * k + 1)])
     own = lax.optimization_barrier(own)
     up, down = [own], [own]
@@ -273,14 +288,7 @@
     z, core, row = col // 2, col % 2, lax.axis_index("row")
     place = jnp.stack([z, core, row]).astype(jnp.int32)
 
-    mine = pl.pallas_call(
-        panel_kernel,
-        in_specs=[pl.BlockSpec(memory_space=pl.ANY)],
-        out_specs=[pl.BlockSpec(memory_space=pltpu.VMEM)] * DEPTH,
-        out_shape=[f32(PIECE, width)] * DEPTH,
-        scratch_shapes=[pltpu.SemaphoreType.DMA((DEPTH,))],
-        name="panel",
-    )(*in_hbm(matrix))
+    mine = panel_rows(matrix, NEAR) | panel_rows(matrix, FAR)
     own = share_panel(mine, z)
     other = swap_cores(own)
 

time: 158 us -> 160 us (1.013)
    pallas_call x1 -> x2, Pallas kernels: 2.32 us -> 3.83 us  [panel_rows(): pl.pallas_call(kernel, in_specs=[pl.BlockSpec(memory_space=pl.ANY)], out_...]
  transfers between devices with their start and end apart: 18 -> 18, of which waited for: 8 -> 8; matrix products, arithmetic and copies ran while one was open for 0% -> 0% of each run, Pallas kernels for 17% -> 18%
where the time goes in v7:
time: 160 us; the launch traced here: 159 us
  Pallas kernels  54.1 us (34%)
  blocking collectives  49.1 us (31%)
  starting transfers between devices  38.5 us (24%)
  waiting for transfers between devices  15.6 us (10%)
    all_to_all x2, blocking collectives, exchange(): return lax.all_to_all(x, 'row', 0, 0)  49.1 us
    pallas_call x1, Pallas kernels, on_device(): call(factor_kernel, 'factor', 20, (1,), [whole(PEERS, TILES * 8, TILE)] *...  27.1 us
    ppermute x7, starting transfers between devices, share_panel(): own = own + lax.ppermute(mine[k], 'col', [(0, 2 * k), (1, 2 * k + 1)])  15.5 us
    pallas_call x1, Pallas kernels, on_device(): call(remainder_kernel, 'remainder', 22, (steps,), [panel_spec, panel_spec...  11.5 us
    ppermute x8, starting transfers between devices, shift(): return lax.ppermute(x, axis, [(i, (i + by) % PEERS) for i in range(PEERS)])  10.8 us
    pallas_call x1, Pallas kernels, on_device(): call(product_kernel, 'product', 20, (steps,), [own_spec, own_spec] + [pl....  9.51 us
    ppermute x8, waiting for transfers between devices, shift(): return lax.ppermute(x, axis, [(i, (i + by) % PEERS) for i in range(PEERS)])  9.11 us
    ppermute x2, starting transfers between devices, swap_cores(): return lax.ppermute(x, 'col', [(i, i ^ 1) for i in range(PEERS)])  8.45 us
  transfers between devices with their start and end apart: 18, of which 8 were waited for; matrix products, arithmetic and copies ran while one was open for 0% of the time, Pallas kernels for 18%

profile of v7, /device:TPU:1, one launch (start us, length us, event | category | flops | bytes accessed | tf_op | source)
XLA Modules:
  0.0 159.5 jit_solution(11172952758506642044)
XLA Ops:
  0.6 1.7 %panel.3 = (f32[128,256]{1,0:T(8,128)}, f32[128,256]{1,0:T(8,128)}) custom-call(f32[1024,4,256]{2,1,0:T(4,128)} %a_ref.1), custom_call_target="tpu_custom_call" | custom-call | tf_op jit(solution)/shard_map/panel/pallas_call | solution.py:107
  2.3 4.4 %collective-permute-start = (f32[128,256]{1,0:T(8,128)}, f32[128,256]{1,0:T(8,128)S(1)}, u32[]{:S(2)}, u32[]{:S(2)}) collective-permute-start(f32[128,256]{1,0:T(8,128)} %get-tuple-element.19), channel_id=1, source_target_pairs={{0,2},{1,3},{16,18},{17,19},{32,34},{33,35},{48,50},{49,51},{64,66... | collective-permute-start | bytes 393224 | tf_op jit(solution)/shard_map/ppermute | solution.py:274
  6.7 4.6 %collective-permute-start.1 = (f32[128,256]{1,0:T(8,128)}, f32[128,256]{1,0:T(8,128)S(1)}, u32[]{:S(2)}, u32[]{:S(2)}) collective-permute-start(f32[128,256]{1,0:T(8,128)} %get-tuple-element.20), channel_id=1, source_target_pairs={{0,14},{1,15},{16,30},{17,31},{32,46},{33,47},{48,62},{49,63},{64,... | collective-permute-start | bytes 393224 | tf_op jit(solution)/shard_map/ppermute | solution.py:274
  11.3 2.1 %panel.2 = (f32[128,256]{1,0:T(8,128)}, f32[128,256]{1,0:T(8,128)}, f32[128,256]{1,0:T(8,128)}, f32[128,256]{1,0:T(8,128)}, f32[128,256]{1,0:T(8,128)}, /*index=5*/f32[128,256]{1,0:T(8,128)}) custom-call(f32[1024,4,256]{2,1,0:T(4,128)} %a_ref.1), custom_call_target="tpu_custom_call" | custom-call | tf_op jit(solution)/shard_map/panel/pallas_call | solution.py:107
  13.5 1.3 collective-permute-start.2
  14.8 1.3 collective-permute-start.3
  16.1 1.3 collective-permute-start.4
  17.4 0.0 collective-permute-done
  17.4 1.3 collective-permute-start.5
  18.7 0.0 collective-permute-done.1
  18.7 1.3 collective-permute-start.6
  20.0 0.0 collective-permute-done.2
  20.0 0.0 collective-permute-done.3
  20.1 0.2 collective-permute-done.4
  20.2 2.9 %collective-permute-done.5 = f32[128,256]{1,0:T(8,128)S(1)} collective-permute-done((f32[128,256]{1,0:T(8,128)}, f32[128,256]{1,0:T(8,128)S(1)}, u32[]{:S(2)}, u32[]{:S(2)}) %collective-permute-start.5) | collective-permute-done | bytes 131104 | tf_op jit(solution)/shard_map/ppermute | solution.py:274
  23.1 0.0 collective-permute-done.6
  23.1 1.0 add_add_fusion
  24.1 0.1 collective-permute-start.10
  24.2 2.7 %collective-permute-start.7 = (f32[128,256]{1,0:T(8,128)S(1)}, f32[128,256]{1,0:T(8,128)S(1)}, u32[]{:S(2)}, u32[]{:S(2)}) collective-permute-start(f32[128,256]{1,0:T(8,128)S(1)} %add_add_fusion), channel_id=1, source_target_pairs={{0,14},{1,15},{2,0},{3,1},{4,2},{5,3},{6,4},{7,5},{8,6},{9,7},{10,... | collective-permute-start | bytes 393224 | tf_op jit(solution)/shard_map/ppermute | solution.py:260
  26.8 2.4 %collective-permute-done.10 = f32[128,256]{1,0:T(8,128)S(1)} collective-permute-done((f32[128,256]{1,0:T(8,128)S(1)}, f32[128,256]{1,0:T(8,128)S(1)}, u32[]{:S(2)}, u32[]{:S(2)}) %collective-permute-start.10) | collective-permute-done | bytes 131104 | tf_op jit(solution)/shard_map/ppermute | solution.py:260
  29.2 0.0 collective-permute-start.11
  29.2 0.0 collective-permute-done.7
  29.2 2.7 %collective-permute-start.8 = (f32[128,256]{1,0:T(8,128)S(1)}, f32[128,256]{1,0:T(8,128)S(1)}, u32[]{:S(2)}, u32[]{:S(2)}) collective-permute-start(f32[128,256]{1,0:T(8,128)S(1)} %collective-permute-done.7), channel_id=1, source_target_pairs={{0,14},{1,15},{2,0},{3,1},{4,2},{5,3},{6,4},{7,5},{8,6},{9,7},{10,... | collective-permute-start | bytes 393224 | tf_op jit(solution)/shard_map/ppermute | solution.py:260
  31.9 2.3 %collective-permute-done.11 = f32[128,256]{1,0:T(8,128)S(1)} collective-permute-done((f32[128,256]{1,0:T(8,128)S(1)}, f32[128,256]{1,0:T(8,128)S(1)}, u32[]{:S(2)}, u32[]{:S(2)}) %collective-permute-start.11) | collective-permute-done | bytes 131104 | tf_op jit(solution)/shard_map/ppermute | solution.py:260
  34.2 0.0 collective-permute-start.12
  34.2 0.0 collective-permute-done.8
  34.2 2.7 %collective-permute-start.9 = (f32[128,256]{1,0:T(8,128)S(1)}, f32[128,256]{1,0:T(8,128)S(1)}, u32[]{:S(2)}, u32[]{:S(2)}) collective-permute-start(f32[128,256]{1,0:T(8,128)S(1)} %collective-permute-done.8), channel_id=1, source_target_pairs={{0,14},{1,15},{2,0},{3,1},{4,2},{5,3},{6,4},{7,5},{8,6},{9,7},{10,... | collective-permute-start | bytes 393224 | tf_op jit(solution)/shard_map/ppermute | solution.py:260
  36.9 2.3 %collective-permute-done.12 = f32[128,256]{1,0:T(8,128)S(1)} collective-permute-done((f32[128,256]{1,0:T(8,128)S(1)}, f32[128,256]{1,0:T(8,128)S(1)}, u32[]{:S(2)}, u32[]{:S(2)}) %collective-permute-start.12) | collective-permute-done | bytes 131104 | tf_op jit(solution)/shard_map/ppermute | solution.py:260
  39.2 0.0 collective-permute-start.13
  39.3 0.0 collective-permute-done.9
  39.3 2.7 %collective-permute-start.14 = (f32[64,256]{1,0:T(8,128)S(1)}, f32[64,256]{1,0:T(8,128)S(1)}, u32[]{:S(2)}, u32[]{:S(2)}) collective-permute-start(f32[64,256]{1,0:T(8,128)S(1)} %slice.9), channel_id=1, source_target_pairs={{0,14},{1,15},{2,0},{3,1},{4,2},{5,3},{6,4},{7,5},{8,6},{9,7},{10,... | collective-permute-start | bytes 196616 | tf_op jit(solution)/shard_map/ppermute | solution.py:260
  42.0 2.1 %collective-permute-done.13 = f32[64,256]{1,0:T(8,128)S(1)} collective-permute-done((f32[64,256]{1,0:T(8,128)S(1)}, f32[64,256]{1,0:T(8,128)S(1)}, u32[]{:S(2)}, u32[]{:S(2)}) %collective-permute-start.13) | collective-permute-done | bytes 65568 | tf_op jit(solution)/shard_map/ppermute | solution.py:260
  44.1 0.0 collective-permute-done.14
  44.2 6.0 %collective-permute-start.15 = (f32[1024,256]{1,0:T(8,128)S(1)}, f32[1024,256]{1,0:T(8,128)S(1)}, u32[]{:S(2)}, u32[]{:S(2)}) collective-permute-start(f32[1024,256]{1,0:T(8,128)S(1)} %constant_dynamic-update-slice_fusion.own_ref), channel_id=1, source_target_pairs={{0,1},{1,0},{2,3},{3,2},{4,5},{5,4},{6,7},{7,6},{8,9},{9,8},{10,11... | collective-permute-start | bytes 3145736 | tf_op jit(solution)/shard_map/ppermute | solution.py:268
  50.2 0.1 pad_add_fusion.place
  50.2 2.2 %collective-permute-done.15.other_ref = f32[1024,256]{1,0:T(8,128)S(1)} collective-permute-done((f32[1024,256]{1,0:T(8,128)S(1)}, f32[1024,256]{1,0:T(8,128)S(1)}, u32[]{:S(2)}, u32[]{:S(2)}) %collective-permute-start.15) | collective-permute-done | bytes 1048608 | tf_op jit(solution)/shard_map/ppermute | solution.py:268
  52.5 9.5 %product.1 = (bf16[1024,512]{1,0:T(8,128)(2,1)}, bf16[1024,512]{1,0:T(8,128)(2,1)}, f32[16,296,128]{2,1,0:T(8,128)S(1)}) custom-call(s32[3]{0:T(128)S(1)} %pad_add_fusion.place, f32[1024,256]{1,0:T(8,128)S(1)} %constant_dynamic-update-slice_fusion.own_ref, f32[1024,256]{1,0:T(8,128)S(1)} %collective-permute-done.15.other_ref, f32[1024,4,256]{2,1,0:T(4,128)} %a_ref.1, ...), custom_call_target="tpu_custom_call" | custom-call | tf_op jit(solution)/shard_map/product/pallas_call | solution.py:300
  62.0 37.9 %all_to_all.15.terms_ref = f32[16,296,128]{2,1,0:T(8,128)S(1)} all-to-all(f32[16,296,128]{2,1,0:T(8,128)S(1)} %get-tuple-element.26), channel_id=1, replica_groups=mesh['row'=16,'col'=16] {'row'}, dimensions={0} | all-to-all | bytes 4849664 | tf_op jit(solution)/shard_map/all_to_all | solution.py:264
  99.9 2.1 %total.1 = (f32[16,40,128]{2,1,0:T(8,128)S(1)}, f32[16,256,128]{2,1,0:T(8,128)}) custom-call(s32[3]{0:T(128)S(1)} %pad_add_fusion.place, f32[16,296,128]{2,1,0:T(8,128)S(1)} %all_to_all.15.terms_ref), custom_call_target="tpu_custom_call" | custom-call | tf_op jit(solution)/shard_map/total/pallas_call | solution.py:312
  102.0 11.2 %all_to_all.16.own_ref = f32[16,40,128]{2,1,0:T(8,128)S(1)} all-to-all(f32[16,40,128]{2,1,0:T(8,128)S(1)} %get-tuple-element.27), channel_id=1, replica_groups=mesh['row'=16,'col'=16] {'row'}, dimensions={0} | all-to-all | bytes 655360 | tf_op jit(solution)/shard_map/all_to_all | solution.py:264
  113.2 3.7 %all-to-all-start.2 = ((f32[16,256,128]{2,1,0:T(8,128)}), f32[16,256,128]{2,1,0:T(8,128)S(1)}, u32[]{:S(2)}, u32[]{:S(2)}) async-start(f32[16,256,128]{2,1,0:T(8,128)} %get-tuple-element.33), calls=%async_computation.2 | async-start | bytes 4194304 | tf_op jit(solution)/shard_map/all_to_all | solution.py:264
  116.9 2.5 %collective-permute-start.16 = (f32[16,40,128]{2,1,0:T(8,128)S(1)}, f32[16,40,128]{2,1,0:T(8,128)S(1)}, u32[]{:S(2)}, u32[]{:S(2)}) collective-permute-start(f32[16,40,128]{2,1,0:T(8,128)S(1)} %all_to_all.16.own_ref), channel_id=1, source_target_pairs={{0,1},{1,0},{2,3},{3,2},{4,5},{5,4},{6,7},{7,6},{8,9},{9,8},{10,11... | collective-permute-start | bytes 983048 | tf_op jit(solution)/shard_map/ppermute | solution.py:268
  119.4 1.3 collective-permute-done.16.other_ref
  120.6 27.1 %factor.1 = (f32[512,512]{1,0:T(8,128)S(1)}, bf16[1024,512]{1,0:T(8,128)(2,1)}, bf16[1024,512]{1,0:T(8,128)(2,1)}) custom-call(s32[3]{0:T(128)S(1)} %pad_add_fusion.place, f32[16,40,128]{2,1,0:T(8,128)S(1)} %all_to_all.16.own_ref, f32[16,40,128]{2,1,0:T(8,128)S(1)} %collective-permute-done.16.other_ref, bf16[1024,512]{1,0:T(8,128)(2,1)} %get-tuple-element.28.high_ref, ...), custom_call_target="tpu_custom_call" | custom-call | tf_op jit(solution)/shard_map/factor/pallas_call | solution.py:321
  147.8 0.0 all-to-all-done.2.w_ref
  147.8 11.5 %remainder.1 = (f32[512,4,256]{2,1,0:T(4,128)}, f32[1024,4,256]{2,1,0:T(4,128)}) custom-call(s32[3]{0:T(128)S(1)} %pad_add_fusion.place, bf16[1024,512]{1,0:T(8,128)(2,1)} %get-tuple-element.30.qh_ref, bf16[1024,512]{1,0:T(8,128)(2,1)} %get-tuple-element.31.ql_ref, f32[1024,4,256]{2,1,0:T(4,128)} %a_ref.1, f32[512,512]{1,0:T(8,128)S(1)} %get-tuple-element.32.m_ref, ...), custom_call_target="tpu_custom_call" | custom-call | tf_op jit(solution)/shard_map/remainder/pallas_call | solution.py:330
  (11 shorter events, 0.1 us)
Async XLA Ops:
  2.3 15.1 %collective-permute-start = (f32[128,256]{1,0:T(8,128)}, f32[128,256]{1,0:T(8,128)S(1)}, u32[]{:S(2)}, u32[]{:S(2)}) collective-permute-start(f32[128,256]{1,0:T(8,128)} %get-tuple-element.19), channel_id=1, source_target_pairs={{0,2},{1,3},{16,18},{17,19},{32,34},{33,35},{48,50},{49,51},{64,66... | collective-permute-start | bytes 393224 | tf_op jit(solution)/shard_map/ppermute | solution.py:274
  6.7 12.0 %collective-permute-start.1 = (f32[128,256]{1,0:T(8,128)}, f32[128,256]{1,0:T(8,128)S(1)}, u32[]{:S(2)}, u32[]{:S(2)}) collective-permute-start(f32[128,256]{1,0:T(8,128)} %get-tuple-element.20), channel_id=1, source_target_pairs={{0,14},{1,15},{16,30},{17,31},{32,46},{33,47},{48,62},{49,63},{64,... | collective-permute-start | bytes 393224 | tf_op jit(solution)/shard_map/ppermute | solution.py:274
  13.5 6.6 %collective-permute-start.2 = (f32[128,256]{1,0:T(8,128)}, f32[128,256]{1,0:T(8,128)S(1)}, u32[]{:S(2)}, u32[]{:S(2)}) collective-permute-start(f32[128,256]{1,0:T(8,128)} %get-tuple-element.21), channel_id=1, source_target_pairs={{0,4},{1,5},{16,20},{17,21},{32,36},{33,37},{48,52},{49,53},{64,68... | collective-permute-start | bytes 393224 | tf_op jit(solution)/shard_map/ppermute | solution.py:274
  14.8 5.3 %collective-permute-start.3 = (f32[128,256]{1,0:T(8,128)}, f32[128,256]{1,0:T(8,128)S(1)}, u32[]{:S(2)}, u32[]{:S(2)}) collective-permute-start(f32[128,256]{1,0:T(8,128)} %get-tuple-element.22), channel_id=1, source_target_pairs={{0,12},{1,13},{16,28},{17,29},{32,44},{33,45},{48,60},{49,61},{64,... | collective-permute-start | bytes 393224 | tf_op jit(solution)/shard_map/ppermute | solution.py:274
  16.1 4.2 %collective-permute-start.4 = (f32[128,256]{1,0:T(8,128)}, f32[128,256]{1,0:T(8,128)S(1)}, u32[]{:S(2)}, u32[]{:S(2)}) collective-permute-start(f32[128,256]{1,0:T(8,128)} %get-tuple-element.23), channel_id=1, source_target_pairs={{0,8},{1,9},{16,24},{17,25},{32,40},{33,41},{48,56},{49,57},{64,72... | collective-permute-start | bytes 393224 | tf_op jit(solution)/shard_map/ppermute | solution.py:274
  17.4 5.7 %collective-permute-start.5 = (f32[128,256]{1,0:T(8,128)}, f32[128,256]{1,0:T(8,128)S(1)}, u32[]{:S(2)}, u32[]{:S(2)}) collective-permute-start(f32[128,256]{1,0:T(8,128)} %get-tuple-element.24), channel_id=1, source_target_pairs={{0,6},{1,7},{16,22},{17,23},{32,38},{33,39},{48,54},{49,55},{64,70... | collective-permute-start | bytes 393224 | tf_op jit(solution)/shard_map/ppermute | solution.py:274
  18.7 4.4 %collective-permute-start.6 = (f32[128,256]{1,0:T(8,128)}, f32[128,256]{1,0:T(8,128)S(1)}, u32[]{:S(2)}, u32[]{:S(2)}) collective-permute-start(f32[128,256]{1,0:T(8,128)} %get-tuple-element.25), channel_id=1, source_target_pairs={{0,10},{1,11},{16,26},{17,27},{32,42},{33,43},{48,58},{49,59},{64,... | collective-permute-start | bytes 393224 | tf_op jit(solution)/shard_map/ppermute | solution.py:274
  24.1 5.1 %collective-permute-start.10 = (f32[128,256]{1,0:T(8,128)S(1)}, f32[128,256]{1,0:T(8,128)S(1)}, u32[]{:S(2)}, u32[]{:S(2)}) collective-permute-start(f32[128,256]{1,0:T(8,128)S(1)} %add_add_fusion), channel_id=1, source_target_pairs={{0,2},{1,3},{2,4},{3,5},{4,6},{5,7},{6,8},{7,9},{8,10},{9,11},{10,... | collective-permute-start | bytes 393224 | tf_op jit(solution)/shard_map/ppermute | solution.py:260
  24.2 5.0 %collective-permute-start.7 = (f32[128,256]{1,0:T(8,128)S(1)}, f32[128,256]{1,0:T(8,128)S(1)}, u32[]{:S(2)}, u32[]{:S(2)}) collective-permute-start(f32[128,256]{1,0:T(8,128)S(1)} %add_add_fusion), channel_id=1, source_target_pairs={{0,14},{1,15},{2,0},{3,1},{4,2},{5,3},{6,4},{7,5},{8,6},{9,7},{10,... | collective-permute-start | bytes 393224 | tf_op jit(solution)/shard_map/ppermute | solution.py:260
  29.2 5.0 %collective-permute-start.11 = (f32[128,256]{1,0:T(8,128)S(1)}, f32[128,256]{1,0:T(8,128)S(1)}, u32[]{:S(2)}, u32[]{:S(2)}) collective-permute-start(f32[128,256]{1,0:T(8,128)S(1)} %collective-permute-done.10), channel_id=1, source_target_pairs={{0,2},{1,3},{2,4},{3,5},{4,6},{5,7},{6,8},{7,9},{8,10},{9,11},{10,... | collective-permute-start | bytes 393224 | tf_op jit(solution)/shard_map/ppermute | solution.py:260
  29.2 5.0 %collective-permute-start.8 = (f32[128,256]{1,0:T(8,128)S(1)}, f32[128,256]{1,0:T(8,128)S(1)}, u32[]{:S(2)}, u32[]{:S(2)}) collective-permute-start(f32[128,256]{1,0:T(8,128)S(1)} %collective-permute-done.7), channel_id=1, source_target_pairs={{0,14},{1,15},{2,0},{3,1},{4,2},{5,3},{6,4},{7,5},{8,6},{9,7},{10,... | collective-permute-start | bytes 393224 | tf_op jit(solution)/shard_map/ppermute | solution.py:260
  34.2 5.0 %collective-permute-start.12 = (f32[128,256]{1,0:T(8,128)S(1)}, f32[128,256]{1,0:T(8,128)S(1)}, u32[]{:S(2)}, u32[]{:S(2)}) collective-permute-start(f32[128,256]{1,0:T(8,128)S(1)} %collective-permute-done.11), channel_id=1, source_target_pairs={{0,2},{1,3},{2,4},{3,5},{4,6},{5,7},{6,8},{7,9},{8,10},{9,11},{10,... | collective-permute-start | bytes 393224 | tf_op jit(solution)/shard_map/ppermute | solution.py:260
  34.2 5.0 %collective-permute-start.9 = (f32[128,256]{1,0:T(8,128)S(1)}, f32[128,256]{1,0:T(8,128)S(1)}, u32[]{:S(2)}, u32[]{:S(2)}) collective-permute-start(f32[128,256]{1,0:T(8,128)S(1)} %collective-permute-done.8), channel_id=1, source_target_pairs={{0,14},{1,15},{2,0},{3,1},{4,2},{5,3},{6,4},{7,5},{8,6},{9,7},{10,... | collective-permute-start | bytes 393224 | tf_op jit(solution)/shard_map/ppermute | solution.py:260
  39.2 4.9 %collective-permute-start.13 = (f32[64,256]{1,0:T(8,128)S(1)}, f32[64,256]{1,0:T(8,128)S(1)}, u32[]{:S(2)}, u32[]{:S(2)}) collective-permute-start(f32[64,256]{1,0:T(8,128)S(1)} %slice.8), channel_id=1, source_target_pairs={{0,2},{1,3},{2,4},{3,5},{4,6},{5,7},{6,8},{7,9},{8,10},{9,11},{10,... | collective-permute-start | bytes 196616 | tf_op jit(solution)/shard_map/ppermute | solution.py:260
  39.3 4.9 %collective-permute-start.14 = (f32[64,256]{1,0:T(8,128)S(1)}, f32[64,256]{1,0:T(8,128)S(1)}, u32[]{:S(2)}, u32[]{:S(2)}) collective-permute-start(f32[64,256]{1,0:T(8,128)S(1)} %slice.9), channel_id=1, source_target_pairs={{0,14},{1,15},{2,0},{3,1},{4,2},{5,3},{6,4},{7,5},{8,6},{9,7},{10,... | collective-permute-start | bytes 196616 | tf_op jit(solution)/shard_map/ppermute | solution.py:260
  44.2 8.3 %collective-permute-start.15 = (f32[1024,256]{1,0:T(8,128)S(1)}, f32[1024,256]{1,0:T(8,128)S(1)}, u32[]{:S(2)}, u32[]{:S(2)}) collective-permute-start(f32[1024,256]{1,0:T(8,128)S(1)} %constant_dynamic-update-slice_fusion.own_ref), channel_id=1, source_target_pairs={{0,1},{1,0},{2,3},{3,2},{4,5},{5,4},{6,7},{7,6},{8,9},{9,8},{10,11... | collective-permute-start | bytes 3145736 | tf_op jit(solution)/shard_map/ppermute | solution.py:268
  113.2 34.6 %all-to-all-start.2 = ((f32[16,256,128]{2,1,0:T(8,128)}), f32[16,256,128]{2,1,0:T(8,128)S(1)}, u32[]{:S(2)}, u32[]{:S(2)}) async-start(f32[16,256,128]{2,1,0:T(8,128)} %get-tuple-element.33), calls=%async_computation.2 | async-start | bytes 4194304 | tf_op jit(solution)/shard_map/all_to_all | solution.py:264
  116.9 3.7 %collective-permute-start.16 = (f32[16,40,128]{2,1,0:T(8,128)S(1)}, f32[16,40,128]{2,1,0:T(8,128)S(1)}, u32[]{:S(2)}, u32[]{:S(2)}) collective-permute-start(f32[16,40,128]{2,1,0:T(8,128)S(1)} %all_to_all.16.own_ref), channel_id=1, source_target_pairs={{0,1},{1,0},{2,3},{3,2},{4,5},{5,4},{6,7},{7,6},{8,9},{9,8},{10,11... | collective-permute-start | bytes 983048 | tf_op jit(solution)/shard_map/ppermute | solution.py:268

commit v8 on v6

--- a/solution.py
+++ b/solution.py
@@ -229,6 +229,10 @@
     return pl.BlockSpec(shape, lambda g, place: (0,) * len(shape))
 
 
+def resident():
+    return pl.BlockSpec(memory_space=pltpu.VMEM)
+
+
 def f32(*shape):
     return jax.ShapeDtypeStruct(shape, jnp.float32)
 
@@ -303,7 +307,7 @@
     gram_rows = TILES * 8
     gram, sums = call(
         total_kernel, "total", 16, (1,),
-        [whole(PEERS, share_rows + gram_rows, TILE)],
+        [resident()],
         [whole(PEERS, gram_rows, TILE), whole(PEERS, share_rows, TILE)],
         [f32(PEERS, gram_rows, TILE), pltpu.HBM((PEERS, share_rows, TILE), jnp.float32)],
     )(place, exchange(terms))
@@ -312,7 +316,7 @@
 
     m, qh, ql = call(
         factor_kernel, "factor", 20, (1,),
-        [whole(PEERS, TILES * 8, TILE)] * 2 + [whole(rows, FULL)] * 2,
+        [resident()] * 2 + [whole(rows, FULL)] * 2,
         [whole(FULL, FULL), whole(rows, FULL), whole(rows, FULL)],
         [f32(FULL, FULL), bf16(rows, FULL), bf16(rows, FULL)],
         [pltpu.VMEM((NB, FULL, TILE), jnp.float32), pltpu.VMEM((NB, TILE, FULL), jnp.float32)],
@@ -321,7 +325,7 @@
     a_spec = pl.BlockSpec((step, blocks, width), lambda g, place: (g, 0, 0))
     return call(
         remainder_kernel, "remainder", 22, (steps,),
-        [panel_spec, panel_spec, a_spec, whole(FULL, FULL), whole(PEERS, share_rows, TILE)],
+        [panel_spec, panel_spec, a_spec, resident(), resident()],
         [pl.BlockSpec(memory_space=pl.ANY), a_spec],
         [f32(FULL, blocks, width), f32(rows, blocks, width)],
         [pltpu.VMEM((FULL, blocks * width), jnp.bfloat16)] * 2

time: 158 us -> 158 us (level)
  no operation moved by 1% of the time
where the time goes in v8:
time: 158 us
  Pallas kernels  52.6 us (33%)
  blocking collectives  49.1 us (31%)
  starting transfers between devices  38.5 us (24%)
  waiting for transfers between devices  15.6 us (10%)
    all_to_all x2, blocking collectives, exchange(): return lax.all_to_all(x, 'row', 0, 0)  49.1 us
    pallas_call x1, Pallas kernels, on_device(): call(factor_kernel, 'factor', 20, (1,), [resident()] * 2 + [whole(rows, F...  27.1 us
    ppermute x7, starting transfers between devices, share_panel(): own = own + lax.ppermute(mine[k], 'col', [(0, 2 * k), (1, 2 * k + 1)])  15.5 us
    pallas_call x1, Pallas kernels, on_device(): call(remainder_kernel, 'remainder', 22, (steps,), [panel_spec, panel_spec...  11.5 us
    ppermute x8, starting transfers between devices, shift(): return lax.ppermute(x, axis, [(i, (i + by) % PEERS) for i in range(PEERS)])  10.8 us
    pallas_call x1, Pallas kernels, on_device(): call(product_kernel, 'product', 20, (steps,), [own_spec, own_spec] + [pl....  9.52 us
    ppermute x8, waiting for transfers between devices, shift(): return lax.ppermute(x, axis, [(i, (i + by) % PEERS) for i in range(PEERS)])  9.11 us
    ppermute x2, starting transfers between devices, swap_cores(): return lax.ppermute(x, 'col', [(i, i ^ 1) for i in range(PEERS)])  8.45 us
  transfers between devices with their start and end apart: 18, of which 8 were waited for; matrix products, arithmetic and copies ran while one was open for 0% of the time, Pallas kernels for 17%

profile of v8, /device:TPU:1, one launch (start us, length us, event | category | flops | bytes accessed | tf_op | source)
XLA Modules:
  0.0 158.0 jit_solution(14226603692660983165)
XLA Ops:
  0.6 2.3 %panel.1 = (f32[128,256]{1,0:T(8,128)}, f32[128,256]{1,0:T(8,128)}, f32[128,256]{1,0:T(8,128)}, f32[128,256]{1,0:T(8,128)}, f32[128,256]{1,0:T(8,128)}, /*index=...) custom-call(f32[1024,4,256]{2,1,0:T(4,128)} %a_ref.1), custom_call_target="tpu_custom_call" | custom-call | tf_op jit(solution)/shard_map/panel/pallas_call | solution.py:280
  3.0 4.4 %collective-permute-start = (f32[128,256]{1,0:T(8,128)}, f32[128,256]{1,0:T(8,128)S(1)}, u32[]{:S(2)}, u32[]{:S(2)}) collective-permute-start(f32[128,256]{1,0:T(8,128)} %get-tuple-element.19), channel_id=1, source_target_pairs={{0,2},{1,3},{16,18},{17,19},{32,34},{33,35},{48,50},{49,51},{64,66... | collective-permute-start | bytes 393224 | tf_op jit(solution)/shard_map/ppermute | solution.py:263
  7.3 4.6 %collective-permute-start.1 = (f32[128,256]{1,0:T(8,128)}, f32[128,256]{1,0:T(8,128)S(1)}, u32[]{:S(2)}, u32[]{:S(2)}) collective-permute-start(f32[128,256]{1,0:T(8,128)} %get-tuple-element.20), channel_id=1, source_target_pairs={{0,14},{1,15},{16,30},{17,31},{32,46},{33,47},{48,62},{49,63},{64,... | collective-permute-start | bytes 393224 | tf_op jit(solution)/shard_map/ppermute | solution.py:263
  12.0 1.3 collective-permute-start.2
  13.3 1.3 collective-permute-start.3
  14.6 1.3 collective-permute-start.4
  15.9 0.0 collective-permute-done
  15.9 1.3 collective-permute-start.5
  17.2 0.0 collective-permute-done.1
  17.2 1.3 collective-permute-start.6
  18.5 0.0 collective-permute-done.2
  18.5 0.0 collective-permute-done.3
  18.5 0.2 collective-permute-done.4
  18.7 2.9 %collective-permute-done.5 = f32[128,256]{1,0:T(8,128)S(1)} collective-permute-done((f32[128,256]{1,0:T(8,128)}, f32[128,256]{1,0:T(8,128)S(1)}, u32[]{:S(2)}, u32[]{:S(2)}) %collective-permute-start.5) | collective-permute-done | bytes 131104 | tf_op jit(solution)/shard_map/ppermute | solution.py:263
  21.6 0.0 collective-permute-done.6
  21.6 1.0 add_add_fusion
  22.6 0.1 collective-permute-start.10
  22.7 2.7 %collective-permute-start.7 = (f32[128,256]{1,0:T(8,128)S(1)}, f32[128,256]{1,0:T(8,128)S(1)}, u32[]{:S(2)}, u32[]{:S(2)}) collective-permute-start(f32[128,256]{1,0:T(8,128)S(1)} %add_add_fusion), channel_id=1, source_target_pairs={{0,14},{1,15},{2,0},{3,1},{4,2},{5,3},{6,4},{7,5},{8,6},{9,7},{10,... | collective-permute-start | bytes 393224 | tf_op jit(solution)/shard_map/ppermute | solution.py:249
  25.3 2.4 %collective-permute-done.10 = f32[128,256]{1,0:T(8,128)S(1)} collective-permute-done((f32[128,256]{1,0:T(8,128)S(1)}, f32[128,256]{1,0:T(8,128)S(1)}, u32[]{:S(2)}, u32[]{:S(2)}) %collective-permute-start.10) | collective-permute-done | bytes 131104 | tf_op jit(solution)/shard_map/ppermute | solution.py:249
  27.7 0.0 collective-permute-start.11
  27.7 0.0 collective-permute-done.7
  27.7 2.7 %collective-permute-start.8 = (f32[128,256]{1,0:T(8,128)S(1)}, f32[128,256]{1,0:T(8,128)S(1)}, u32[]{:S(2)}, u32[]{:S(2)}) collective-permute-start(f32[128,256]{1,0:T(8,128)S(1)} %collective-permute-done.7), channel_id=1, source_target_pairs={{0,14},{1,15},{2,0},{3,1},{4,2},{5,3},{6,4},{7,5},{8,6},{9,7},{10,... | collective-permute-start | bytes 393224 | tf_op jit(solution)/shard_map/ppermute | solution.py:249
  30.4 2.3 %collective-permute-done.11 = f32[128,256]{1,0:T(8,128)S(1)} collective-permute-done((f32[128,256]{1,0:T(8,128)S(1)}, f32[128,256]{1,0:T(8,128)S(1)}, u32[]{:S(2)}, u32[]{:S(2)}) %collective-permute-start.11) | collective-permute-done | bytes 131104 | tf_op jit(solution)/shard_map/ppermute | solution.py:249
  32.7 0.0 collective-permute-start.12
  32.7 0.0 collective-permute-done.8
  32.7 2.7 %collective-permute-start.9 = (f32[128,256]{1,0:T(8,128)S(1)}, f32[128,256]{1,0:T(8,128)S(1)}, u32[]{:S(2)}, u32[]{:S(2)}) collective-permute-start(f32[128,256]{1,0:T(8,128)S(1)} %collective-permute-done.8), channel_id=1, source_target_pairs={{0,14},{1,15},{2,0},{3,1},{4,2},{5,3},{6,4},{7,5},{8,6},{9,7},{10,... | collective-permute-start | bytes 393224 | tf_op jit(solution)/shard_map/ppermute | solution.py:249
  35.4 2.3 %collective-permute-done.12 = f32[128,256]{1,0:T(8,128)S(1)} collective-permute-done((f32[128,256]{1,0:T(8,128)S(1)}, f32[128,256]{1,0:T(8,128)S(1)}, u32[]{:S(2)}, u32[]{:S(2)}) %collective-permute-start.12) | collective-permute-done | bytes 131104 | tf_op jit(solution)/shard_map/ppermute | solution.py:249
  37.7 0.0 collective-permute-start.13
  37.7 0.0 collective-permute-done.9
  37.8 2.7 %collective-permute-start.14 = (f32[64,256]{1,0:T(8,128)S(1)}, f32[64,256]{1,0:T(8,128)S(1)}, u32[]{:S(2)}, u32[]{:S(2)}) collective-permute-start(f32[64,256]{1,0:T(8,128)S(1)} %slice.9), channel_id=1, source_target_pairs={{0,14},{1,15},{2,0},{3,1},{4,2},{5,3},{6,4},{7,5},{8,6},{9,7},{10,... | collective-permute-start | bytes 196616 | tf_op jit(solution)/shard_map/ppermute | solution.py:249
  40.5 2.1 %collective-permute-done.13 = f32[64,256]{1,0:T(8,128)S(1)} collective-permute-done((f32[64,256]{1,0:T(8,128)S(1)}, f32[64,256]{1,0:T(8,128)S(1)}, u32[]{:S(2)}, u32[]{:S(2)}) %collective-permute-start.13) | collective-permute-done | bytes 65568 | tf_op jit(solution)/shard_map/ppermute | solution.py:249
  42.6 0.0 collective-permute-done.14
  42.7 6.0 %collective-permute-start.15 = (f32[1024,256]{1,0:T(8,128)S(1)}, f32[1024,256]{1,0:T(8,128)S(1)}, u32[]{:S(2)}, u32[]{:S(2)}) collective-permute-start(f32[1024,256]{1,0:T(8,128)S(1)} %constant_dynamic-update-slice_fusion.own_ref), channel_id=1, source_target_pairs={{0,1},{1,0},{2,3},{3,2},{4,5},{5,4},{6,7},{7,6},{8,9},{9,8},{10,11... | collective-permute-start | bytes 3145736 | tf_op jit(solution)/shard_map/ppermute | solution.py:257
  48.7 0.1 pad_add_fusion.place
  48.7 2.2 %collective-permute-done.15.other_ref = f32[1024,256]{1,0:T(8,128)S(1)} collective-permute-done((f32[1024,256]{1,0:T(8,128)S(1)}, f32[1024,256]{1,0:T(8,128)S(1)}, u32[]{:S(2)}, u32[]{:S(2)}) %collective-permute-start.15) | collective-permute-done | bytes 1048608 | tf_op jit(solution)/shard_map/ppermute | solution.py:257
  50.9 9.5 %product.1 = (bf16[1024,512]{1,0:T(8,128)(2,1)}, bf16[1024,512]{1,0:T(8,128)(2,1)}, f32[16,296,128]{2,1,0:T(8,128)S(1)}) custom-call(s32[3]{0:T(128)S(1)} %pad_add_fusion.place, f32[1024,256]{1,0:T(8,128)S(1)} %constant_dynamic-update-slice_fusion.own_ref, f32[1024,256]{1,0:T(8,128)S(1)} %collective-permute-done.15.other_ref, f32[1024,4,256]{2,1,0:T(4,128)} %a_ref.1, ...), custom_call_target="tpu_custom_call" | custom-call | tf_op jit(solution)/shard_map/product/pallas_call | solution.py:296
  60.5 37.9 %all_to_all.15.terms_ref = f32[16,296,128]{2,1,0:T(8,128)S(1)} all-to-all(f32[16,296,128]{2,1,0:T(8,128)S(1)} %get-tuple-element.26), channel_id=1, replica_groups=mesh['row'=16,'col'=16] {'row'}, dimensions={0} | all-to-all | bytes 4849664 | tf_op jit(solution)/shard_map/all_to_all | solution.py:253
  98.4 2.1 %total.1 = (f32[16,40,128]{2,1,0:T(8,128)S(1)}, f32[16,256,128]{2,1,0:T(8,128)}) custom-call(s32[3]{0:T(128)S(1)} %pad_add_fusion.place, f32[16,296,128]{2,1,0:T(8,128)S(1)} %all_to_all.15.terms_ref), custom_call_target="tpu_custom_call" | custom-call | tf_op jit(solution)/shard_map/total/pallas_call | solution.py:308
  100.4 11.2 %all_to_all.16.own_ref = f32[16,40,128]{2,1,0:T(8,128)S(1)} all-to-all(f32[16,40,128]{2,1,0:T(8,128)S(1)} %get-tuple-element.27), channel_id=1, replica_groups=mesh['row'=16,'col'=16] {'row'}, dimensions={0} | all-to-all | bytes 655360 | tf_op jit(solution)/shard_map/all_to_all | solution.py:253
  111.6 3.7 %all-to-all-start.2 = ((f32[16,256,128]{2,1,0:T(8,128)}), f32[16,256,128]{2,1,0:T(8,128)S(1)}, u32[]{:S(2)}, u32[]{:S(2)}) async-start(f32[16,256,128]{2,1,0:T(8,128)} %get-tuple-element.33), calls=%async_computation.2 | async-start | bytes 4194304 | tf_op jit(solution)/shard_map/all_to_all | solution.py:253
  115.4 2.5 %collective-permute-start.16 = (f32[16,40,128]{2,1,0:T(8,128)S(1)}, f32[16,40,128]{2,1,0:T(8,128)S(1)}, u32[]{:S(2)}, u32[]{:S(2)}) collective-permute-start(f32[16,40,128]{2,1,0:T(8,128)S(1)} %all_to_all.16.own_ref), channel_id=1, source_target_pairs={{0,1},{1,0},{2,3},{3,2},{4,5},{5,4},{6,7},{7,6},{8,9},{9,8},{10,11... | collective-permute-start | bytes 983048 | tf_op jit(solution)/shard_map/ppermute | solution.py:257
  117.9 1.3 collective-permute-done.16.other_ref
  119.1 27.1 %factor.1 = (f32[512,512]{1,0:T(8,128)S(1)}, bf16[1024,512]{1,0:T(8,128)(2,1)}, bf16[1024,512]{1,0:T(8,128)(2,1)}) custom-call(s32[3]{0:T(128)S(1)} %pad_add_fusion.place, f32[16,40,128]{2,1,0:T(8,128)S(1)} %all_to_all.16.own_ref, f32[16,40,128]{2,1,0:T(8,128)S(1)} %collective-permute-done.16.other_ref, bf16[1024,512]{1,0:T(8,128)(2,1)} %get-tuple-element.28.high_ref, ...), custom_call_target="tpu_custom_call" | custom-call | tf_op jit(solution)/shard_map/factor/pallas_call | solution.py:317
  146.3 0.0 all-to-all-done.2.w_ref
  146.3 11.5 %remainder.1 = (f32[512,4,256]{2,1,0:T(4,128)}, f32[1024,4,256]{2,1,0:T(4,128)}) custom-call(s32[3]{0:T(128)S(1)} %pad_add_fusion.place, bf16[1024,512]{1,0:T(8,128)(2,1)} %get-tuple-element.30.qh_ref, bf16[1024,512]{1,0:T(8,128)(2,1)} %get-tuple-element.31.ql_ref, f32[1024,4,256]{2,1,0:T(4,128)} %a_ref.1, f32[512,512]{1,0:T(8,128)S(1)} %get-tuple-element.32.m_ref, ...), custom_call_target="tpu_custom_call" | custom-call | tf_op jit(solution)/shard_map/remainder/pallas_call | solution.py:326
  (11 shorter events, 0.1 us)
Async XLA Ops:
  3.0 12.9 %collective-permute-start = (f32[128,256]{1,0:T(8,128)}, f32[128,256]{1,0:T(8,128)S(1)}, u32[]{:S(2)}, u32[]{:S(2)}) collective-permute-start(f32[128,256]{1,0:T(8,128)} %get-tuple-element.19), channel_id=1, source_target_pairs={{0,2},{1,3},{16,18},{17,19},{32,34},{33,35},{48,50},{49,51},{64,66... | collective-permute-start | bytes 393224 | tf_op jit(solution)/shard_map/ppermute | solution.py:263
  7.3 9.8 %collective-permute-start.1 = (f32[128,256]{1,0:T(8,128)}, f32[128,256]{1,0:T(8,128)S(1)}, u32[]{:S(2)}, u32[]{:S(2)}) collective-permute-start(f32[128,256]{1,0:T(8,128)} %get-tuple-element.20), channel_id=1, source_target_pairs={{0,14},{1,15},{16,30},{17,31},{32,46},{33,47},{48,62},{49,63},{64,... | collective-permute-start | bytes 393224 | tf_op jit(solution)/shard_map/ppermute | solution.py:263
  12.0 6.6 %collective-permute-start.2 = (f32[128,256]{1,0:T(8,128)}, f32[128,256]{1,0:T(8,128)S(1)}, u32[]{:S(2)}, u32[]{:S(2)}) collective-permute-start(f32[128,256]{1,0:T(8,128)} %get-tuple-element.21), channel_id=1, source_target_pairs={{0,4},{1,5},{16,20},{17,21},{32,36},{33,37},{48,52},{49,53},{64,68... | collective-permute-start | bytes 393224 | tf_op jit(solution)/shard_map/ppermute | solution.py:263
  13.3 5.3 %collective-permute-start.3 = (f32[128,256]{1,0:T(8,128)}, f32[128,256]{1,0:T(8,128)S(1)}, u32[]{:S(2)}, u32[]{:S(2)}) collective-permute-start(f32[128,256]{1,0:T(8,128)} %get-tuple-element.22), channel_id=1, source_target_pairs={{0,12},{1,13},{16,28},{17,29},{32,44},{33,45},{48,60},{49,61},{64,... | collective-permute-start | bytes 393224 | tf_op jit(solution)/shard_map/ppermute | solution.py:263
  14.6 4.2 %collective-permute-start.4 = (f32[128,256]{1,0:T(8,128)}, f32[128,256]{1,0:T(8,128)S(1)}, u32[]{:S(2)}, u32[]{:S(2)}) collective-permute-start(f32[128,256]{1,0:T(8,128)} %get-tuple-element.23), channel_id=1, source_target_pairs={{0,8},{1,9},{16,24},{17,25},{32,40},{33,41},{48,56},{49,57},{64,72... | collective-permute-start | bytes 393224 | tf_op jit(solution)/shard_map/ppermute | solution.py:263
  15.9 5.7 %collective-permute-start.5 = (f32[128,256]{1,0:T(8,128)}, f32[128,256]{1,0:T(8,128)S(1)}, u32[]{:S(2)}, u32[]{:S(2)}) collective-permute-start(f32[128,256]{1,0:T(8,128)} %get-tuple-element.24), channel_id=1, source_target_pairs={{0,6},{1,7},{16,22},{17,23},{32,38},{33,39},{48,54},{49,55},{64,70... | collective-permute-start | bytes 393224 | tf_op jit(solution)/shard_map/ppermute | solution.py:263
  17.2 4.4 %collective-permute-start.6 = (f32[128,256]{1,0:T(8,128)}, f32[128,256]{1,0:T(8,128)S(1)}, u32[]{:S(2)}, u32[]{:S(2)}) collective-permute-start(f32[128,256]{1,0:T(8,128)} %get-tuple-element.25), channel_id=1, source_target_pairs={{0,10},{1,11},{16,26},{17,27},{32,42},{33,43},{48,58},{49,59},{64,... | collective-permute-start | bytes 393224 | tf_op jit(solution)/shard_map/ppermute | solution.py:263
  22.6 5.1 %collective-permute-start.10 = (f32[128,256]{1,0:T(8,128)S(1)}, f32[128,256]{1,0:T(8,128)S(1)}, u32[]{:S(2)}, u32[]{:S(2)}) collective-permute-start(f32[128,256]{1,0:T(8,128)S(1)} %add_add_fusion), channel_id=1, source_target_pairs={{0,2},{1,3},{2,4},{3,5},{4,6},{5,7},{6,8},{7,9},{8,10},{9,11},{10,... | collective-permute-start | bytes 393224 | tf_op jit(solution)/shard_map/ppermute | solution.py:249
  22.7 5.0 %collective-permute-start.7 = (f32[128,256]{1,0:T(8,128)S(1)}, f32[128,256]{1,0:T(8,128)S(1)}, u32[]{:S(2)}, u32[]{:S(2)}) collective-permute-start(f32[128,256]{1,0:T(8,128)S(1)} %add_add_fusion), channel_id=1, source_target_pairs={{0,14},{1,15},{2,0},{3,1},{4,2},{5,3},{6,4},{7,5},{8,6},{9,7},{10,... | collective-permute-start | bytes 393224 | tf_op jit(solution)/shard_map/ppermute | solution.py:249
  27.7 5.0 %collective-permute-start.11 = (f32[128,256]{1,0:T(8,128)S(1)}, f32[128,256]{1,0:T(8,128)S(1)}, u32[]{:S(2)}, u32[]{:S(2)}) collective-permute-start(f32[128,256]{1,0:T(8,128)S(1)} %collective-permute-done.10), channel_id=1, source_target_pairs={{0,2},{1,3},{2,4},{3,5},{4,6},{5,7},{6,8},{7,9},{8,10},{9,11},{10,... | collective-permute-start | bytes 393224 | tf_op jit(solution)/shard_map/ppermute | solution.py:249
  27.7 5.0 %collective-permute-start.8 = (f32[128,256]{1,0:T(8,128)S(1)}, f32[128,256]{1,0:T(8,128)S(1)}, u32[]{:S(2)}, u32[]{:S(2)}) collective-permute-start(f32[128,256]{1,0:T(8,128)S(1)} %collective-permute-done.7), channel_id=1, source_target_pairs={{0,14},{1,15},{2,0},{3,1},{4,2},{5,3},{6,4},{7,5},{8,6},{9,7},{10,... | collective-permute-start | bytes 393224 | tf_op jit(solution)/shard_map/ppermute | solution.py:249
  32.7 5.0 %collective-permute-start.12 = (f32[128,256]{1,0:T(8,128)S(1)}, f32[128,256]{1,0:T(8,128)S(1)}, u32[]{:S(2)}, u32[]{:S(2)}) collective-permute-start(f32[128,256]{1,0:T(8,128)S(1)} %collective-permute-done.11), channel_id=1, source_target_pairs={{0,2},{1,3},{2,4},{3,5},{4,6},{5,7},{6,8},{7,9},{8,10},{9,11},{10,... | collective-permute-start | bytes 393224 | tf_op jit(solution)/shard_map/ppermute | solution.py:249
  32.7 5.0 %collective-permute-start.9 = (f32[128,256]{1,0:T(8,128)S(1)}, f32[128,256]{1,0:T(8,128)S(1)}, u32[]{:S(2)}, u32[]{:S(2)}) collective-permute-start(f32[128,256]{1,0:T(8,128)S(1)} %collective-permute-done.8), channel_id=1, source_target_pairs={{0,14},{1,15},{2,0},{3,1},{4,2},{5,3},{6,4},{7,5},{8,6},{9,7},{10,... | collective-permute-start | bytes 393224 | tf_op jit(solution)/shard_map/ppermute | solution.py:249
  37.7 4.9 %collective-permute-start.13 = (f32[64,256]{1,0:T(8,128)S(1)}, f32[64,256]{1,0:T(8,128)S(1)}, u32[]{:S(2)}, u32[]{:S(2)}) collective-permute-start(f32[64,256]{1,0:T(8,128)S(1)} %slice.8), channel_id=1, source_target_pairs={{0,2},{1,3},{2,4},{3,5},{4,6},{5,7},{6,8},{7,9},{8,10},{9,11},{10,... | collective-permute-start | bytes 196616 | tf_op jit(solution)/shard_map/ppermute | solution.py:249
  37.8 4.9 %collective-permute-start.14 = (f32[64,256]{1,0:T(8,128)S(1)}, f32[64,256]{1,0:T(8,128)S(1)}, u32[]{:S(2)}, u32[]{:S(2)}) collective-permute-start(f32[64,256]{1,0:T(8,128)S(1)} %slice.9), channel_id=1, source_target_pairs={{0,14},{1,15},{2,0},{3,1},{4,2},{5,3},{6,4},{7,5},{8,6},{9,7},{10,... | collective-permute-start | bytes 196616 | tf_op jit(solution)/shard_map/ppermute | solution.py:249
  42.7 8.3 %collective-permute-start.15 = (f32[1024,256]{1,0:T(8,128)S(1)}, f32[1024,256]{1,0:T(8,128)S(1)}, u32[]{:S(2)}, u32[]{:S(2)}) collective-permute-start(f32[1024,256]{1,0:T(8,128)S(1)} %constant_dynamic-update-slice_fusion.own_ref), channel_id=1, source_target_pairs={{0,1},{1,0},{2,3},{3,2},{4,5},{5,4},{6,7},{7,6},{8,9},{9,8},{10,11... | collective-permute-start | bytes 3145736 | tf_op jit(solution)/shard_map/ppermute | solution.py:257
  111.6 34.6 %all-to-all-start.2 = ((f32[16,256,128]{2,1,0:T(8,128)}), f32[16,256,128]{2,1,0:T(8,128)S(1)}, u32[]{:S(2)}, u32[]{:S(2)}) async-start(f32[16,256,128]{2,1,0:T(8,128)} %get-tuple-element.33), calls=%async_computation.2 | async-start | bytes 4194304 | tf_op jit(solution)/shard_map/all_to_all | solution.py:253
  115.4 3.7 %collective-permute-start.16 = (f32[16,40,128]{2,1,0:T(8,128)S(1)}, f32[16,40,128]{2,1,0:T(8,128)S(1)}, u32[]{:S(2)}, u32[]{:S(2)}) collective-permute-start(f32[16,40,128]{2,1,0:T(8,128)S(1)} %all_to_all.16.own_ref), channel_id=1, source_target_pairs={{0,1},{1,0},{2,3},{3,2},{4,5},{5,4},{6,7},{7,6},{8,9},{9,8},{10,11... | collective-permute-start | bytes 983048 | tf_op jit(solution)/shard_map/ppermute | solution.py:257
